TPU v7x, 256 devices: a whole 4x4x8 slice. The times are simulated.
256 devices in a mesh: dp: 4 (over x), state: 64 (over y, z, core).
Axes of the slice: x: 4, y: 4, z: 8, core: 2. Of those that a mesh axis runs over, the one named last changes fastest.
Arguments:
- alpha_init: bfloat16 [32, 1024, 1024], P('dp', 'state'), may hold values from 0.099609375 to 4
- tokens: int32 [32, 3], P('dp'), may hold values from 0 to 511
- trans_rows: bfloat16 [1024, 1024], replicated, may hold values from 5e-05 to 1.11, as said below
- trans_cols: bfloat16 [1024, 1024], replicated, may hold values from 5e-05 to 1.11, as said below
- emit_rows: bfloat16 [512, 1024], replicated, may hold values from 0.001 to 1, as said below
- emit_cols: bfloat16 [512, 1024], replicated, may hold values from 0.001 to 1, as said below
- backward: bfloat16 [3, 32, 1024, 1024], P(None, 'dp', None, 'state'), may hold values from 0.2 to 32, as said below
Outputs:
- alpha_final: bfloat16 [32, 1024, 1024], P('dp', 'state')
- counts_rows: float32 [1024, 1024], P(None, ('dp', 'state'))
- counts_cols: float32 [1024, 1024], P(None, ('dp', 'state'))
- loglik: float32 [32], P('dp')
Inputs may be any that keep to these rules, and one draw needn't show every extreme that they name: `trans_rows`: positive transition weights. `trans_cols`: positive transition weights. `emit_rows`: positive emission weights. `emit_cols`: positive emission weights. Positive backward weights.
All inputs are finite; a program needn't handle non-finite values.
Results may differ from a plain program's by a relative error of at most 0.0046.
Values may be sent and summed in bfloat16 or wider, within the bound.
No kernel may reach another device: no remote copies, remote signals or barrier semaphores. Data moves between devices by JAX's collectives and lax.ppermute only.
A program may use at most 128 MiB of HBM per device.

v0:
```python
import jax
import jax.numpy as jnp
from jax import lax
from jax.sharding import PartitionSpec as P

STEPS = 3


def on_device(alpha_init, tokens, trans_rows, trans_cols, emit_rows, emit_cols, backward):
    f32 = jnp.float32
    groups = lax.axis_size("state")
    seq_dev = alpha_init.shape[0]
    width_rows = trans_rows.shape[0]
    width_cols = trans_cols.shape[0]
    cols_dev = width_cols // groups
    offset = lax.axis_index("state") * cols_dev
    alpha = alpha_init
    sums_rows = jnp.zeros((width_rows, width_rows), f32)
    sums_cols = jnp.zeros((width_cols, width_cols), f32)
    loglik = jnp.zeros((seq_dev,), f32)
    for step in range(STEPS):
        tok = tokens[:, step]
        first = jnp.take(emit_rows, tok, axis=0).astype(f32)
        second_all = jnp.take(emit_cols, tok, axis=0)
        second = lax.dynamic_slice_in_dim(second_all, offset, cols_dev, 1).astype(f32)
        mixed = jnp.einsum("sij,jk->sik", alpha, trans_cols, preferred_element_type=f32).astype(
            jnp.bfloat16
        )
        mixed_cols = lax.all_to_all(mixed, "state", split_axis=2, concat_axis=1, tiled=True)
        moved = jnp.einsum("sik,il->slk", mixed_cols, trans_rows, preferred_element_type=f32)
        emission = first[:, :, None] * second[:, None, :]
        scaled = moved * emission
        total = lax.psum(jnp.sum(scaled, axis=(1, 2)), "state")
        norm = total / (width_rows * width_cols)
        weight = (emission * backward[step].astype(f32) / norm[:, None, None]).astype(jnp.bfloat16)
        pulled = jnp.einsum("il,slk->sik", trans_rows, weight, preferred_element_type=f32).astype(
            jnp.bfloat16
        )
        pulled_local = lax.all_to_all(pulled, "state", split_axis=1, concat_axis=2, tiled=True)
        sums_rows = sums_rows + jnp.einsum(
            "sik,slk->il", mixed_cols, weight, preferred_element_type=f32
        )
        sums_cols = sums_cols + jnp.einsum(
            "sij,sik->jk", alpha, pulled_local, preferred_element_type=f32
        )
        loglik = loglik + jnp.log(norm)
        fresh = (scaled / norm[:, None, None]).astype(jnp.bfloat16)
        alpha = lax.all_to_all(fresh, "state", split_axis=1, concat_axis=2, tiled=True)
    factor = 1.0 / (seq_dev * lax.axis_size("dp") * STEPS)
    terms_rows = trans_rows.astype(f32) * sums_rows * factor
    terms_cols = trans_cols.astype(f32) * sums_cols * factor
    counts_rows, counts_cols = (
        lax.psum_scatter(terms_rows, ("dp", "state"), scatter_dimension=1, tiled=True),
        lax.psum_scatter(terms_cols, ("dp", "state"), scatter_dimension=1, tiled=True),
    )
    return (alpha, counts_rows, counts_cols, loglik)


def solution(mesh):
    return jax.shard_map(
        on_device,
        mesh=mesh,
        in_specs=(
            P("dp", "state", None),
            P("dp", None),
            P(),
            P(),
            P(),
            P(),
            P(None, "dp", None, "state"),
        ),
        out_specs=(
            P("dp", "state", None),
            P(None, ("dp", "state")),
            P(None, ("dp", "state")),
            P("dp"),
        ),
        check_vma=False,
    )
```

profile of v0, /device:TPU:1, one launch (start us, length us, event | category | flops | bytes accessed | tf_op | source)
XLA Modules:
  0.0 961.5 jit_solution(3449522075632876979)
XLA Ops:
  14.0 13.2 %all-to-all-start = ((bf16[64,2,1024]{2,1,0:T(2,128)(2,1)}), bf16[64,2,1024]{2,1,0:T(2,128)(2,1)S(1)}, u32[]{:S(2)}, u32[]{:S(2)}) async-start(bf16[64,2,1024]{2,1,0:T(2,128)(2,1)} %reshape.105), calls=%async_computation | async-start | bytes 524288 | tf_op jit(solution)/shard_map/all_to_all | solution.py:29
  29.9 9.3 all-to-all-done
  49.4 123.8 %psum.21 = f32[8]{0:T(128)S(1)} all-reduce(f32[8]{0:T(128)S(1)} %get-tuple-element.19), channel_id=1, replica_groups=mesh['dp'=4,'state'=64] {'state'}, use_global_device_ids=true, to_apply=%region_1.3 | all-reduce | flops 8 | bytes 64 | tf_op jit(solution)/shard_map/psum | solution.py:33
  180.5 7.7 all-to-all-start.1
  191.4 8.5 all-to-all-done.1
  205.4 4.8 all_to_all.124
  217.6 6.1 all-to-all-start.2
  241.7 10.5 %all-to-all-start.6 = ((bf16[64,2,1024]{2,1,0:T(2,128)(2,1)}), bf16[64,2,1024]{2,1,0:T(2,128)(2,1)}, u32[]{:S(2)}, u32[]{:S(2)}) async-start(bf16[64,2,1024]{2,1,0:T(2,128)(2,1)} %reshape.117), calls=%async_computation.6 | async-start | bytes 524288 | tf_op jit(solution)/shard_map/all_to_all | solution.py:39
  265.8 124.1 %psum.22 = f32[8]{0:T(128)S(1)} all-reduce(f32[8]{0:T(128)S(1)} %get-tuple-element.21), channel_id=1, replica_groups=mesh['dp'=4,'state'=64] {'state'}, use_global_device_ids=true, to_apply=%region_3.5 | all-reduce | flops 8 | bytes 64 | tf_op jit(solution)/shard_map/psum | solution.py:33
  398.4 9.7 %all-to-all-start.3 = ((bf16[64,2,1024]{2,1,0:T(2,128)(2,1)}), bf16[64,2,1024]{2,1,0:T(2,128)(2,1)S(1)}, u32[]{:S(2)}, u32[]{:S(2)}) async-start(bf16[64,2,1024]{2,1,0:T(2,128)(2,1)} %reshape.111), calls=%async_computation.3 | async-start | bytes 524288 | tf_op jit(solution)/shard_map/all_to_all | solution.py:48
  419.8 5.3 all_to_all.144
  434.6 10.8 %all-to-all-start.7 = ((bf16[64,2,1024]{2,1,0:T(2,128)(2,1)}), bf16[64,2,1024]{2,1,0:T(2,128)(2,1)S(1)}, u32[]{:S(2)}, u32[]{:S(2)}) async-start(bf16[64,2,1024]{2,1,0:T(2,128)(2,1)} %reshape.119), calls=%async_computation.7 | async-start | bytes 524288 | tf_op jit(solution)/shard_map/all_to_all | solution.py:39
  465.5 10.9 %all-to-all-start.4 = ((bf16[64,2,1024]{2,1,0:T(2,128)(2,1)}), bf16[64,2,1024]{2,1,0:T(2,128)(2,1)S(1)}, u32[]{:S(2)}, u32[]{:S(2)}) async-start(bf16[64,2,1024]{2,1,0:T(2,128)(2,1)} %reshape.113), calls=%async_computation.4 | async-start | bytes 524288 | tf_op jit(solution)/shard_map/all_to_all | solution.py:29
  495.8 4.8 all_to_all.136
  501.9 124.1 %psum.23 = f32[8]{0:T(128)S(1)} all-reduce(f32[8]{0:T(128)S(1)} %get-tuple-element.23), channel_id=1, replica_groups=mesh['dp'=4,'state'=64] {'state'}, use_global_device_ids=true, to_apply=%region_5.7 | all-reduce | flops 8 | bytes 64 | tf_op jit(solution)/shard_map/psum | solution.py:33
  635.2 9.6 all-to-all-start.8
  644.9 6.5 fusion.4
  651.4 5.5 all-to-all-done.8
  660.9 4.8 all_to_all.152
  665.8 6.4 fusion.2
  678.0 6.4 all-to-all-start.5
  684.4 13.2 %all-to-all-done.5 = bf16[64,2,1024]{2,1,0:T(2,128)(2,1)S(1)} async-done(((bf16[64,2,1024]{2,1,0:T(2,128)(2,1)}), bf16[64,2,1024]{2,1,0:T(2,128)(2,1)S(1)}, u32[]{:S(2)}, u32[]{:S(2)}) %all-to-all-start.5) | async-done | bytes 262176 | tf_op jit(solution)/shard_map/all_to_all | solution.py:48
  701.7 5.4 all_to_all.140
  707.1 244.6 %all-reduce.5.cloned.1.call-done = (f32[1024,1024]{0,1:T(8,128)}, f32[1024,1024]{0,1:T(8,128)}) async-done(((f32[1024,1024]{0,1:T(8,128)}, f32[1024,1024]{0,1:T(8,128)}), (f32[1024,1024]{0,1:T(8,128)}, f32[1024,1024]{0,1:T(8,128)})) %all-reduce.5.cloned.1.call-update) | async-done | bytes 8388624
  (105 shorter events, 170.7 us)
Async XLA Ops:
  7.2 22.0 %copy-start = (bf16[512,1024]{1,0:T(8,128)(2,1)S(1)}, bf16[512,1024]{1,0:T(8,128)(2,1)}, u32[]{:S(2)}) copy-start(bf16[512,1024]{1,0:T(8,128)(2,1)} %param.13) | copy-start | bytes 3145732
  9.4 17.7 %copy-start.9 = (s32[8,3]{0,1:T(4,128)S(1)}, s32[8,3]{0,1:T(4,128)}, u32[]{:S(2)}) copy-start(s32[8,3]{0,1:T(4,128)} %param.10) | copy-start | bytes 292
  14.0 25.2 %all-to-all-start = ((bf16[64,2,1024]{2,1,0:T(2,128)(2,1)}), bf16[64,2,1024]{2,1,0:T(2,128)(2,1)S(1)}, u32[]{:S(2)}, u32[]{:S(2)}) async-start(bf16[64,2,1024]{2,1,0:T(2,128)(2,1)} %reshape.105), calls=%async_computation | async-start | bytes 524288 | tf_op jit(solution)/shard_map/all_to_all | solution.py:29
  43.3 4.9 copy-start.3
  180.5 19.4 %all-to-all-start.1 = ((bf16[64,2,1024]{2,1,0:T(2,128)(2,1)}), bf16[64,2,1024]{2,1,0:T(2,128)(2,1)}, u32[]{:S(2)}, u32[]{:S(2)}) async-start(bf16[64,2,1024]{2,1,0:T(2,128)(2,1)} %reshape.107), calls=%async_computation.1 | async-start | bytes 524288 | tf_op jit(solution)/shard_map/all_to_all | solution.py:48
  205.4 4.9 copy-start.2
  217.6 24.1 %all-to-all-start.2 = ((bf16[64,2,1024]{2,1,0:T(2,128)(2,1)}), bf16[64,2,1024]{2,1,0:T(2,128)(2,1)S(1)}, u32[]{:S(2)}, u32[]{:S(2)}) async-start(bf16[64,2,1024]{2,1,0:T(2,128)(2,1)} %reshape.109), calls=%async_computation.2 | async-start | bytes 524288 | tf_op jit(solution)/shard_map/all_to_all | solution.py:29
  241.7 156.7 %all-to-all-start.6 = ((bf16[64,2,1024]{2,1,0:T(2,128)(2,1)}), bf16[64,2,1024]{2,1,0:T(2,128)(2,1)}, u32[]{:S(2)}, u32[]{:S(2)}) async-start(bf16[64,2,1024]{2,1,0:T(2,128)(2,1)} %reshape.117), calls=%async_computation.6 | async-start | bytes 524288 | tf_op jit(solution)/shard_map/all_to_all | solution.py:39
  398.4 36.2 %all-to-all-start.3 = ((bf16[64,2,1024]{2,1,0:T(2,128)(2,1)}), bf16[64,2,1024]{2,1,0:T(2,128)(2,1)S(1)}, u32[]{:S(2)}, u32[]{:S(2)}) async-start(bf16[64,2,1024]{2,1,0:T(2,128)(2,1)} %reshape.111), calls=%async_computation.3 | async-start | bytes 524288 | tf_op jit(solution)/shard_map/all_to_all | solution.py:48
  427.7 17.7 %copy-start.8 = (bf16[8,16,1024]{2,1,0:T(8,128)(2,1)S(1)}, bf16[8,16,1024]{2,1,0:T(8,128)(2,1)}, u32[]{:S(2)}) copy-start(bf16[8,16,1024]{2,1,0:T(8,128)(2,1)} %param.9) | copy-start | bytes 786436
  434.6 30.9 %all-to-all-start.7 = ((bf16[64,2,1024]{2,1,0:T(2,128)(2,1)}), bf16[64,2,1024]{2,1,0:T(2,128)(2,1)S(1)}, u32[]{:S(2)}, u32[]{:S(2)}) async-start(bf16[64,2,1024]{2,1,0:T(2,128)(2,1)} %reshape.119), calls=%async_computation.7 | async-start | bytes 524288 | tf_op jit(solution)/shard_map/all_to_all | solution.py:39
  465.5 26.2 %all-to-all-start.4 = ((bf16[64,2,1024]{2,1,0:T(2,128)(2,1)}), bf16[64,2,1024]{2,1,0:T(2,128)(2,1)S(1)}, u32[]{:S(2)}, u32[]{:S(2)}) async-start(bf16[64,2,1024]{2,1,0:T(2,128)(2,1)} %reshape.113), calls=%async_computation.4 | async-start | bytes 524288 | tf_op jit(solution)/shard_map/all_to_all | solution.py:29
  495.8 4.9 copy-start.4
  628.3 16.5 %copy-start.5 = (bf16[1024,1024]{0,1:T(8,128)(2,1)S(1)}, bf16[1024,1024]{0,1:T(8,128)(2,1)}, u32[]{:S(2)}) copy-start(bf16[1024,1024]{0,1:T(8,128)(2,1)} %copy.51) | copy-start | bytes 6291460
  635.2 21.6 %all-to-all-start.8 = ((bf16[64,2,1024]{2,1,0:T(2,128)(2,1)}), bf16[64,2,1024]{2,1,0:T(2,128)(2,1)S(1)}, u32[]{:S(2)}, u32[]{:S(2)}) async-start(bf16[64,2,1024]{2,1,0:T(2,128)(2,1)} %reshape.121), calls=%async_computation.8 | async-start | bytes 524288 | tf_op jit(solution)/shard_map/all_to_all | solution.py:39
  644.8 306.9 %all-reduce.5.cloned.1.call-start = ((), (), s32[]{:S(2)}) async-start(), calls=%async_computation.9 | async-start | bytes 16777216
  660.9 4.9 copy-start.6
  672.2 1.0 copy-start.7
  678.0 19.6 %all-to-all-start.5 = ((bf16[64,2,1024]{2,1,0:T(2,128)(2,1)}), bf16[64,2,1024]{2,1,0:T(2,128)(2,1)S(1)}, u32[]{:S(2)}, u32[]{:S(2)}) async-start(bf16[64,2,1024]{2,1,0:T(2,128)(2,1)} %reshape.115), calls=%async_computation.5 | async-start | bytes 524288 | tf_op jit(solution)/shard_map/all_to_all | solution.py:48
  699.0 255.4 %copy-start.1 = (bf16[512,1024]{1,0:T(8,128)(2,1)S(1)}, bf16[512,1024]{1,0:T(8,128)(2,1)}, u32[]{:S(2)}) copy-start(bf16[512,1024]{1,0:T(8,128)(2,1)} %param.13) | copy-start | bytes 3145732
Sparse Core Ops, SparseCore 0:
  672.4 279.2 all-reduce.4
where the time goes:
time: 971 us; the launch traced here: 961 us
  blocking collectives  372 us (38%)
  waiting for transfers between devices  281 us (29%)
  local copies, waits for them, and re-layouts  164 us (17%)
  starting transfers between devices  84.9 us (9%)
  matrix products  41.4 us (4%)
  between operations  14.7 us (2%)
    psum x3, blocking collectives, on_device(): total = lax.psum(jnp.sum(scaled, axis=(1, 2)), 'state')  372 us
    unnamed x2, waiting for transfers between devices  245 us
    unnamed x42, local copies, waits for them, and re-layouts  62.4 us
    all_to_all x3, starting transfers between devices, on_device(): lax.all_to_all(pulled, 'state', split_axis=1, concat_axis=2, tiled=True)  30.9 us
    all_to_all x3, starting transfers between devices, on_device(): lax.all_to_all(mixed, 'state', split_axis=2, concat_axis=1, tiled=True)  30.2 us
    all_to_all x6, local copies, waits for them, and re-layouts, on_device(): lax.all_to_all(pulled, 'state', split_axis=1, concat_axis=2, tiled=True)  24.6 us
    all_to_all x6, local copies, waits for them, and re-layouts, on_device(): lax.all_to_all(fresh, 'state', split_axis=1, concat_axis=2, tiled=True)  24.6 us
    all_to_all x6, local copies, waits for them, and re-layouts, on_device(): lax.all_to_all(mixed, 'state', split_axis=2, concat_axis=1, tiled=True)  24.1 us
  transfers between devices with their start and end apart: 10, of which 5 were waited for; matrix products, arithmetic and copies ran while one was open for 11% of the time, Pallas kernels for 0%

commit v1 on v0

v1 whole, which is shorter than its diff:
```python
import jax
import jax.numpy as jnp
from jax import lax
from jax.experimental import pallas as pl
from jax.experimental.pallas import tpu as pltpu
from jax.sharding import PartitionSpec as P

STEPS = 3
F32 = jnp.float32
BF16 = jnp.bfloat16
SEQ_DEV = 8
PART = 16
ROWS = SEQ_DEV * PART
WIDTH = 1024
PEERS = WIDTH // PART
VMEM = 48 * 2**20


def iota(shape, dim):
    return lax.broadcasted_iota(jnp.int32, shape, dim)


def dot(a, b):
    return lax.dot_general(a, b, (((1,), (0,)), ((), ())), preferred_element_type=F32)


def dot_nt(a, b):
    return lax.dot_general(a, b, (((1,), (1,)), ((), ())), preferred_element_type=F32)


def dot_tn(a, b):
    return lax.dot_general(a, b, (((0,), (0,)), ((), ())), preferred_element_type=F32)


def pick(tok_ref, emit_ref):
    hot = [
        (tok_ref[:, t : t + 1] == iota((SEQ_DEV, emit_ref.shape[0]), 1)).astype(F32)
        for t in range(STEPS)
    ]
    return dot(jnp.concatenate(hot, axis=0).astype(BF16), emit_ref[...])


def step_of(v, t):
    return v[t * SEQ_DEV : (t + 1) * SEQ_DEV]


def spread(v):
    n = v.shape[-1]
    return jnp.broadcast_to(v[:, None, :], (SEQ_DEV, PART, n)).reshape(ROWS, n)


def column_of(v, offset):
    at = offset + (iota((ROWS, WIDTH), 0) & (PART - 1))
    return jnp.sum(jnp.where(iota((ROWS, WIDTH), 1) == at, spread(v), 0.0), axis=1, keepdims=True)


def swap(tiles):
    group = iota((PART, 128), 1) >> 4
    for bit in (1, 2, 4):
        low = (group & bit) == 0
        out = list(tiles)
        for s in range(SEQ_DEV):
            if s & bit == 0:
                a, b = tiles[s], tiles[s + bit]
                out[s] = jnp.where(low, a, pltpu.roll(b, PART * bit, 1))
                out[s + bit] = jnp.where(low, pltpu.roll(a, 128 - PART * bit, 1), b)
        tiles = out
    return tiles


def to_wire(src_ref, dst_ref, row):
    @pl.loop(0, PEERS // SEQ_DEV)
    def _(g):
        lanes = pl.ds(pl.multiple_of(g * 128, 128), 128)
        tiles = swap([src_ref[s * PART : (s + 1) * PART, lanes] for s in range(SEQ_DEV)])
        for s in range(SEQ_DEV):
            dst_ref[g * SEQ_DEV + s, row : row + PART, :] = tiles[s].astype(BF16)


def from_wire(src_ref, row, store):
    @pl.loop(0, PEERS // SEQ_DEV)
    def _(g):
        tiles = swap(
            [src_ref[g * SEQ_DEV + s, row : row + PART, :].astype(F32) for s in range(SEQ_DEV)]
        )
        lanes = pl.ds(pl.multiple_of(g * 128, 128), 128)
        for s in range(SEQ_DEV):
            store(s, lanes, tiles[s])


def inverse_norm(total_ref, t):
    at = STEPS * (iota((ROWS, 128), 0) >> 4) + t
    total = jnp.sum(
        jnp.where(iota((ROWS, 128), 1) == at, total_ref[...], 0.0), axis=1, keepdims=True
    )
    return float(WIDTH * WIDTH) / total


def rows_kernel(alpha_ref, tok_ref, cols_ref, emit_cols_ref, wire_ref, y_ref, sums_ref, x_ref):
    second = pick(tok_ref, emit_cols_ref)
    y = alpha_ref[...]
    sums = jnp.zeros((ROWS, 128), F32)
    for t in range(STEPS):
        x = dot(y, cols_ref[...])
        x_ref[...] = x
        y32 = x * spread(step_of(second, t))
        total = jnp.sum(y32, axis=1, keepdims=True)
        sums = jnp.where(iota((ROWS, 128), 1) == t, total, sums)
        to_wire(x_ref, wire_ref, t * PART)
        if t < STEPS - 1:
            y = y32.astype(BF16)
            y_ref[t] = y
    sums_ref[...] = sums


def weights_kernel(
    tok_ref, rows_ref, cols_ref, emit_rows_ref, emit_cols_ref, back_ref, sums_ref,
    wire_ref, weight_ref, norm_ref, take_rows_ref, take_cols_ref, first_ref, local_ref,
    wt_ref, g_ref,
):
    me = lax.axis_index("state")
    offset = me * PART
    first = pick(tok_ref, emit_rows_ref)
    first_ref[...] = first
    second = pick(tok_ref, emit_cols_ref)
    local = jnp.zeros((ROWS, 128), F32)
    for t in range(STEPS):
        column = column_of(step_of(second, t), offset)
        local = jnp.where(iota((ROWS, 128), 1) == t, column, local)
        w = spread(step_of(first, t)) * column * back_ref[t].astype(F32)
        wt_ref[t * ROWS : (t + 1) * ROWS, :] = w.astype(BF16)
        weight_ref[:, t * ROWS : (t + 1) * ROWS] = w.T.astype(BF16)
    local_ref[...] = local

    pair = (iota((SEQ_DEV, ROWS), 1) >> 4 == iota((SEQ_DEV, ROWS), 0)).astype(BF16)
    factor = [dot_tn(step_of(first, t).astype(BF16), pair) for t in range(STEPS - 1)]
    v = dot_nt(rows_ref[...], wt_ref[...])

    def put(t, value):
        wire_ref[:, t * PART : (t + 1) * PART, :] = value.astype(BF16).reshape(PEERS, PART, ROWS)

    put(0, v[:, :ROWS])
    g_ref[:, :ROWS] = (factor[0] * v[:, ROWS : 2 * ROWS]).astype(BF16)
    g_ref[:, ROWS:] = (factor[1] * v[:, 2 * ROWS :]).astype(BF16)
    v = dot(rows_ref[...], g_ref[...])
    put(1, v[:, :ROWS])
    g_ref[:, :ROWS] = (factor[0] * v[:, ROWS:]).astype(BF16)
    put(2, dot(rows_ref[...], g_ref[:, :ROWS]))

    p = dot_nt(first.astype(BF16), rows_ref[...])
    back = [step_of(p, 0)]
    p = dot_nt((p[SEQ_DEV:] * first[: 2 * SEQ_DEV]).astype(BF16), rows_ref[...])
    back.append(step_of(p, 0))
    p = dot_nt((p[SEQ_DEV:] * first[:SEQ_DEV]).astype(BF16), rows_ref[...])
    back.append(p)
    norm = jnp.zeros((1, 128), F32)
    for t in range(STEPS):
        part = sums_ref[:, t : t + 1] * column_of(back[t], offset)
        at = STEPS * (iota((ROWS, 128), 0) >> 4) + t
        norm = norm + jnp.sum(jnp.where(iota((ROWS, 128), 1) == at, part, 0.0), axis=0, keepdims=True)
    norm_ref[...] = norm

    chip = (lax.axis_index("dp") * PEERS + me) * 4
    hot = (iota((8, WIDTH), 1) == chip + iota((8, WIDTH), 0)) & (iota((8, WIDTH), 0) < 4)
    hot = hot.astype(F32).astype(BF16)
    take_rows_ref[...] = dot_nt(hot, rows_ref[...])
    take_cols_ref[...] = dot_nt(hot, cols_ref[...])


def columns_kernel(
    wire_ref, weight_ref, rows_ref, first_ref, local_ref, total_ref, out_ref, sums_ref, m_ref
):
    first = first_ref[...]

    def x_of(t):
        x = wire_ref[:, t * PART : (t + 1) * PART, :].reshape(WIDTH, ROWS)
        return x.astype(F32).T

    inv = [inverse_norm(total_ref, t) for t in range(STEPS)]
    f0, f1, f2 = (spread(step_of(first, t)) for t in range(STEPS))
    m_ref[:ROWS] = (x_of(0) * inv[0]).astype(BF16)
    x12 = jnp.concatenate([x_of(1).astype(BF16), x_of(2).astype(BF16)], axis=0)
    h = dot(x12, rows_ref[...])
    m_ref[ROWS : 2 * ROWS] = (h[:ROWS] * f0 * inv[1]).astype(BF16)
    h = dot((h[ROWS:] * f0).astype(BF16), rows_ref[...]) * f1
    m_ref[2 * ROWS :] = (h * inv[2]).astype(BF16)
    a = dot(h.astype(BF16), rows_ref[...]) * f2 * (local_ref[:, 2:3] * inv[2])
    out_ref[...] = a.T.astype(BF16).reshape(PEERS, PART, ROWS)

    @pl.loop(0, WIDTH // 256)
    def _(b):
        at = pl.ds(pl.multiple_of(b * 256, 256), 256)
        sums_ref[at, :] = dot(weight_ref[at, :], m_ref[...]).astype(BF16)


def pulled_kernel(wire_ref, alpha_ref, y_ref, total_ref, sums_ref, v_ref, vt_ref, ys_ref):
    for t in range(STEPS):

        def store(s, lanes, tile):
            v_ref[s * PART : (s + 1) * PART, lanes] = tile

        from_wire(wire_ref, t * PART, store)
        vt_ref[:, t * ROWS : (t + 1) * ROWS] = v_ref[...].T.astype(BF16)
        y = alpha_ref[...] if t == 0 else y_ref[t - 1]
        ys_ref[t * ROWS : (t + 1) * ROWS] = (y.astype(F32) * inverse_norm(total_ref, t)).astype(BF16)

    @pl.loop(0, WIDTH // 256)
    def _(b):
        at = pl.ds(pl.multiple_of(b * 256, 256), 256)
        sums_ref[at, :] = dot(vt_ref[at, :], ys_ref[...]).astype(BF16)


def final_kernel(wire_ref, out_ref):
    def store(s, lanes, tile):
        out_ref[s * PART : (s + 1) * PART, lanes] = tile.astype(BF16)

    from_wire(wire_ref, 0, store)


def call(kernel, name, outs, scratch=(), flops=10**9, moved=8 * 10**6):
    return pl.pallas_call(
        kernel,
        name=name,
        out_shape=[jax.ShapeDtypeStruct(s, d) for s, d in outs],
        scratch_shapes=[pltpu.VMEM(s, d) for s, d in scratch],
        compiler_params=pltpu.CompilerParams(vmem_limit_bytes=VMEM),
        cost_estimate=pl.CostEstimate(flops=flops, bytes_accessed=moved, transcendentals=0),
    )


def exchange(x, groups=None, axis="state"):
    return lax.all_to_all(x, axis, 0, 0, axis_index_groups=groups, tiled=True)


def on_device(alpha_init, tokens, trans_rows, trans_cols, emit_rows, emit_cols, backward):
    alpha = alpha_init.reshape(ROWS, WIDTH)
    back = jnp.swapaxes(backward, 2, 3).reshape(STEPS, ROWS, WIDTH)
    wire = (PEERS, STEPS * PART, ROWS)

    x_wire, y, sums = call(
        rows_kernel, "rows",
        [(wire, BF16), ((STEPS - 1, ROWS, WIDTH), BF16), ((ROWS, 128), F32)],
        [((ROWS, WIDTH), F32)],
    )(alpha, tokens, trans_cols, emit_cols)
    x_got = exchange(x_wire)

    v_wire, weight, norm, take_rows, take_cols, first, local = call(
        weights_kernel, "weights",
        [
            (wire, BF16), ((WIDTH, STEPS * ROWS), BF16), ((1, 128), F32), ((8, WIDTH), F32),
            ((8, WIDTH), F32), ((STEPS * SEQ_DEV, WIDTH), F32), ((ROWS, 128), F32),
        ],
        [((STEPS * ROWS, WIDTH), BF16), ((WIDTH, 2 * ROWS), BF16)],
    )(tokens, trans_rows, trans_cols, emit_rows, emit_cols, back, sums)
    norms = exchange(jnp.broadcast_to(norm[None], (PEERS, 1, 128)))
    v_got = exchange(v_wire)
    total = jnp.sum(norms, axis=0)

    a_wire, sums_rows = call(
        columns_kernel, "columns",
        [((PEERS, PART, ROWS), BF16), ((WIDTH, WIDTH), BF16)],
        [((STEPS * ROWS, WIDTH), BF16)],
    )(x_got, weight, trans_rows, first, local, total)
    a_got = exchange(a_wire)

    (sums_cols,) = call(
        pulled_kernel, "pulled", [((WIDTH, WIDTH), BF16)],
        [((ROWS, WIDTH), F32), ((WIDTH, STEPS * ROWS), BF16), ((STEPS * ROWS, WIDTH), BF16)],
    )(v_got, alpha, y, total)

    ny, nz = 4, 8
    core = lax.axis_index("state") & 1
    pairs = [(i, i ^ 1) for i in range(PEERS)]
    group_y = [[(b * nz + z) * 2 + c for b in range(ny)] for z in range(nz) for c in range(2)]
    group_z = [[(b * nz + z) * 2 + c for z in range(nz)] for b in range(ny) for c in range(2)]
    keep = jnp.where(core == 0, sums_rows, sums_cols)
    give = jnp.where(core == 0, sums_cols, sums_rows)
    part = keep.astype(F32) + lax.ppermute(give, "state", pairs).astype(F32)
    part = exchange(part.astype(BF16).reshape(4, 256, WIDTH), axis="dp")
    part = jnp.sum(part.astype(F32), axis=0)
    part = exchange(part.astype(BF16).reshape(ny, 64, WIDTH), group_y)
    part = jnp.sum(part.astype(F32), axis=0)
    part = exchange(part.astype(BF16).reshape(nz, 8, WIDTH), group_z)
    part = jnp.sum(part.astype(F32), axis=0)
    mine = jnp.where(core == 0, part[:4], part[4:])
    other = lax.ppermute(jnp.where(core == 0, part[4:], part[:4]), "state", pairs)
    scale = 1.0 / (SEQ_DEV * 4 * STEPS)
    counts_rows = jnp.where(core == 0, mine, other) * take_rows[:4] * scale
    counts_cols = jnp.where(core == 0, other, mine) * take_cols[:4] * scale

    (alpha_final,) = call(final_kernel, "final", [((ROWS, WIDTH), BF16)])(a_got)
    loglik = jnp.log(total[0, 2 : 3 * SEQ_DEV : 3] / (WIDTH * WIDTH))
    return (
        alpha_final.reshape(SEQ_DEV, PART, WIDTH),
        counts_rows.T,
        counts_cols.T,
        loglik,
    )


def solution(mesh):
    return jax.shard_map(
        on_device,
        mesh=mesh,
        in_specs=(
            P("dp", "state", None),
            P("dp", None),
            P(),
            P(),
            P(),
            P(),
            P(None, "dp", None, "state"),
        ),
        out_specs=(
            P("dp", "state", None),
            P(None, ("dp", "state")),
            P(None, ("dp", "state")),
            P("dp"),
        ),
        check_vma=False,
    )
```

time: 971 us -> 191 us (0.20)
  blocking collectives: 372 us -> 91.6 us
  waiting for transfers between devices: 281 us -> 33.9 us
  local copies, waits for them, and re-layouts: 164 us -> 9.61 us
  starting transfers between devices: 84.9 us -> 18.4 us
  matrix products: 41.4 us -> 0 us
  Pallas kernels: 0 us -> 31.5 us
  between operations: 14.7 us -> 0.76 us
    psum x3 -> x0, blocking collectives: 372 us -> none  [on_device(): total = lax.psum(jnp.sum(scaled, axis=(1, 2)), 'state')]
    unnamed x2 -> x0, waiting for transfers between devices: 245 us -> none
    all_to_all x0 -> x4, blocking collectives: none -> 91.6 us  [exchange(): return lax.all_to_all(x, axis, 0, 0, axis_index_groups=groups, tiled=True)]
    all_to_all x18 -> x0, local copies, waits for them, and re-layouts: 73.3 us -> none  [the longest x6 24.6 us: on_device(): lax.all_to_all(pulled, 'state', split_axis=1, concat_axis=2, tiled=True)]
    all_to_all x9 -> x3, starting transfers between devices: 84.9 us -> 17.2 us  [exchange(): return lax.all_to_all(x, axis, 0, 0, axis_index_groups=groups, tiled=True)]
    unnamed x42 -> x31, local copies, waits for them, and re-layouts: 62.4 us -> 9.5 us
    dot_general x15 -> x0, matrix products: 41.4 us -> none  [the longest x3 14 us: on_device(): jnp.einsum('sik,slk->il', mixed_cols, weight, preferred_element_type=f32)]
    pallas_call x0 -> x5, Pallas kernels: none -> 31.5 us  [the longest x1 9.39 us: on_device(): call(weights_kernel, 'weights', [(wire, BF16), ((WIDTH, STEPS * ROWS), BF...]
  transfers between devices with their start and end apart: 10 -> 5, of which waited for: 5 -> 4; matrix products, arithmetic and copies ran while one was open for 11% -> 0% of each run, Pallas kernels for 0% -> 5%
where the time goes in v1:
time: 191 us; the launch traced here: 190 us
  blocking collectives  91.6 us (48%)
  waiting for transfers between devices  33.9 us (18%)
  Pallas kernels  31.5 us (16%)
  starting transfers between devices  18.4 us (10%)
  local copies, waits for them, and re-layouts  9.61 us (5%)
  other arithmetic  4.14 us (2%)
    all_to_all x4, blocking collectives, exchange(): return lax.all_to_all(x, axis, 0, 0, axis_index_groups=groups, tiled=True)  91.6 us
    all_to_all x3, waiting for transfers between devices, exchange(): return lax.all_to_all(x, axis, 0, 0, axis_index_groups=groups, tiled=True)  30.1 us
    all_to_all x3, starting transfers between devices, exchange(): return lax.all_to_all(x, axis, 0, 0, axis_index_groups=groups, tiled=True)  17.2 us
    unnamed x31, local copies, waits for them, and re-layouts  9.5 us
    pallas_call x1, Pallas kernels, on_device(): call(weights_kernel, 'weights', [(wire, BF16), ((WIDTH, STEPS * ROWS), BF...  9.39 us
    pallas_call x1, Pallas kernels, on_device(): call(rows_kernel, 'rows', [(wire, BF16), ((STEPS - 1, ROWS, WIDTH), BF16)...  8.21 us
    pallas_call x1, Pallas kernels, on_device(): call(pulled_kernel, 'pulled', [((WIDTH, WIDTH), BF16)], [((ROWS, WIDTH),...  7.8 us
  transfers between devices with their start and end apart: 5, of which 4 were waited for; matrix products, arithmetic and copies ran while one was open for 0% of the time, Pallas kernels for 5%

profile of v1, /device:TPU:1, one launch (start us, length us, event | category | flops | bytes accessed | tf_op | source)
XLA Modules:
  0.0 189.9 jit_solution(7330338921647141711)
XLA Ops:
  1.4 1.6 copy-done.3
  3.0 1.2 copy-done.4
  4.2 0.9 copy-done.11
  5.2 8.2 %rows.1 = (bf16[64,48,128]{2,1,0:T(8,128)(2,1)}, bf16[2,128,1024]{2,1,0:T(8,128)(2,1)S(1)}, f32[128,128]{1,0:T(8,128)S(1)}) custom-call(bf16[128,1024]{1,0:T(8,128)(2,1)S(1)} %bitcast.22, s32[8,3]{1,0:T(8,128)S(1)} %copy.15.tok_ref, bf16[1024,1024]{1,0:T(8,128)(2,1)S(1)} %copy-done.3, bf16[512,1024]{1,0:T(8,128)(2,1)S(1)} %copy-done.4), custom_call_target="tpu_custom_call" | custom-call | flops 1000000000 | bytes 8000000 | tf_op jit(solution)/shard_map/rows/pallas_call | solution.py:240
  13.4 9.4 %weights.1 = (bf16[64,48,128]{2,1,0:T(8,128)(2,1)S(1)}, bf16[1024,384]{1,0:T(8,128)(2,1)S(1)}, f32[1,128]{1,0:T(1,128)S(1)}, f32[8,1024]{1,0:T(8,128)S(1)}, f32[...) custom-call(s32[8,3]{1,0:T(8,128)S(1)} %copy.15.tok_ref, bf16[1024,1024]{1,0:T(8,128)(2,1)} %rows_ref.3, ...), custom_call_target="tpu_custom_call" | custom-call | flops 1000000000 | bytes 8000000 | tf_op jit(solution)/shard_map/weights/pallas_call | solution.py:247
  22.8 22.4 %all_to_all.35 = f32[64,1,128]{2,1,0:T(1,128)S(1)} all-to-all(f32[64,1,128]{2,1,0:T(1,128)S(1)} %broadcast_in_dim.9), channel_id=1, replica_groups=mesh['dp'=4,'state'=64] {'state'}, dimensions={0} | all-to-all | bytes 65536 | tf_op jit(solution)/shard_map/all_to_all | solution.py:232
  45.2 27.7 %all_to_all.36.wire_ref = bf16[64,48,128]{2,1,0:T(8,128)(2,1)} all-to-all(bf16[64,48,128]{2,1,0:T(8,128)(2,1)S(1)} %get-tuple-element.24), channel_id=1, replica_groups=mesh['dp'=4,'state'=64] {'state'}, dimensions={0} | all-to-all | bytes 1572864 | tf_op jit(solution)/shard_map/all_to_all | solution.py:232
  72.9 6.2 %all-to-all-start = ((bf16[64,48,128]{2,1,0:T(8,128)(2,1)}), bf16[64,48,128]{2,1,0:T(8,128)(2,1)S(1)}, u32[]{:S(2)}, u32[]{:S(2)}) async-start(bf16[64,48,128]{2,1,0:T(8,128)(2,1)} %get-tuple-element.16), calls=%async_computation | async-start | bytes 1572864 | tf_op jit(solution)/shard_map/all_to_all | solution.py:232
  79.2 1.3 copy-done.8
  80.4 1.0 copy-done.14
  81.5 7.8 %pulled.1 = bf16[1024,1024]{1,0:T(8,128)(2,1)S(1)} custom-call(bf16[64,48,128]{2,1,0:T(8,128)(2,1)S(1)} %copy-done.8, bf16[128,1024]{1,0:T(8,128)(2,1)S(1)} %bitcast.23, bf16[2,128,1024]{2,1,0:T(8,128)(2,1)S(1)} %copy-done.14, f32[1,128]{1,0:T(1,128)S(1)} %bitcast.18), custom_call_target="tpu_custom_call" | custom-call | flops 1000000000 | bytes 8000000 | tf_op jit(solution)/shard_map/pulled/pallas_call | solution.py:266
  89.3 1.3 copy-done.1
  90.6 11.5 %all-to-all-done.wire_ref = bf16[64,48,128]{2,1,0:T(8,128)(2,1)S(1)} async-done(((bf16[64,48,128]{2,1,0:T(8,128)(2,1)}), bf16[64,48,128]{2,1,0:T(8,128)(2,1)S(1)}, u32[]{:S(2)}, u32[]{:S(2)}) %all-to-all-start) | async-done | bytes 786464 | tf_op jit(solution)/shard_map/all_to_all | solution.py:232
  102.1 1.3 copy-done.10
  103.4 3.6 %columns.1 = (bf16[64,16,128]{2,1,0:T(8,128)(2,1)}, bf16[1024,1024]{1,0:T(8,128)(2,1)S(1)}) custom-call(bf16[64,48,128]{2,1,0:T(8,128)(2,1)S(1)} %all-to-all-done.wire_ref, bf16[1024,384]{1,0:T(8,128)(2,1)S(1)} %copy-done.10, bf16[1024,1024]{1,0:T(8,128)(2,1)S(1)} %copy-done, f32[24,1024]{1,0:T(8,128)S(1)} %get-tuple-element.19.first_ref, ...), custom_call_target="tpu_custom_call" | custom-call | flops 1000000000 | bytes 8000000 | tf_op jit(solution)/shard_map/columns/pallas_call | solution.py:259
  107.7 3.8 %collective-permute-done = bf16[1024,1024]{1,0:T(8,128)(2,1)S(1)} collective-permute-done((bf16[1024,1024]{1,0:T(8,128)(2,1)S(1)}, bf16[1024,1024]{1,0:T(8,128)(2,1)S(1)}, u32[]{:S(2)}, u32[]{:S(2)}) %collective-permute-start) | collective-permute-done | bytes 2097184 | tf_op jit(solution)/shard_map/ppermute | solution.py:278
  111.5 1.5 add_convert_fusion
  113.0 29.3 %all_to_all.37 = bf16[4,256,1024]{2,1,0:T(8,128)(2,1)S(1)} all-to-all(bf16[4,256,1024]{2,1,0:T(8,128)(2,1)S(1)} %bitcast.24), channel_id=1, replica_groups=mesh['dp'=4,'state'=64] {'dp'}, dimensions={0} | all-to-all | bytes 4194304 | tf_op jit(solution)/shard_map/all_to_all | solution.py:232
  142.7 12.3 %all_to_all.38 = bf16[4,64,1024]{2,1,0:T(8,128)(2,1)S(1)} all-to-all(bf16[4,64,1024]{2,1,0:T(8,128)(2,1)S(1)} %bitcast.25), channel_id=1, replica_groups={{0,16,32,48},{1,17,33,49},{2,18,34,50},{3,19,35,51},{4,20,36,52},{5,21,..., dimensions={0} | all-to-all | bytes 1048576 | tf_op jit(solution)/shard_map/all_to_all | solution.py:232
  155.7 3.4 %all-to-all-start.6 = ((bf16[8,8,1024]{2,1,0:T(8,128)(2,1)}), bf16[8,8,1024]{2,1,0:T(8,128)(2,1)S(1)}, u32[]{:S(2)}, u32[]{:S(2)}) async-start(bf16[8,8,1024]{2,1,0:T(8,128)(2,1)} %bitcast.9), calls=%async_computation.6 | async-start | bytes 262144 | tf_op jit(solution)/shard_map/all_to_all | solution.py:232
  159.2 7.8 %all-to-all-done.6 = bf16[8,8,1024]{2,1,0:T(8,128)(2,1)S(1)} async-done(((bf16[8,8,1024]{2,1,0:T(8,128)(2,1)}), bf16[8,8,1024]{2,1,0:T(8,128)(2,1)S(1)}, u32[]{:S(2)}, u32[]{:S(2)}) %all-to-all-start.6) | async-done | bytes 131104 | tf_op jit(solution)/shard_map/all_to_all | solution.py:232
  167.0 7.7 %all-to-all-start.2 = ((bf16[64,16,128]{2,1,0:T(8,128)(2,1)}), bf16[64,16,128]{2,1,0:T(8,128)(2,1)S(1)}, u32[]{:S(2)}, u32[]{:S(2)}) async-start(bf16[64,16,128]{2,1,0:T(8,128)(2,1)} %get-tuple-element.22), calls=%async_computation.2 | async-start | bytes 524288 | tf_op jit(solution)/shard_map/all_to_all | solution.py:232
  175.9 10.8 %all-to-all-done.2.wire_ref = bf16[64,16,128]{2,1,0:T(8,128)(2,1)S(1)} async-done(((bf16[64,16,128]{2,1,0:T(8,128)(2,1)}), bf16[64,16,128]{2,1,0:T(8,128)(2,1)S(1)}, u32[]{:S(2)}, u32[]{:S(2)}) %all-to-all-start.2) | async-done | bytes 262176 | tf_op jit(solution)/shard_map/all_to_all | solution.py:232
  186.7 2.5 %final.1 = bf16[128,1024]{1,0:T(8,128)(2,1)} custom-call(bf16[64,16,128]{2,1,0:T(8,128)(2,1)S(1)} %all-to-all-done.2.wire_ref), custom_call_target="tpu_custom_call" | custom-call | flops 1000000000 | bytes 8000000 | tf_op jit(solution)/shard_map/final/pallas_call | solution.py:291
  (37 shorter events, 4.7 us)
Async XLA Ops:
  1.4 1.6 copy-start.3
  3.0 1.2 copy-start.4
  4.2 0.9 copy-start.11
  5.2 8.2 %copy-start.5 = (bf16[512,1024]{1,0:T(8,128)(2,1)S(1)}, bf16[512,1024]{1,0:T(8,128)(2,1)}, u32[]{:S(2)}) copy-start(bf16[512,1024]{1,0:T(8,128)(2,1)} %emit_cols_ref.3) | copy-start | bytes 3145732
  5.2 8.2 %copy-start.6 = (bf16[512,1024]{1,0:T(8,128)(2,1)S(1)}, bf16[512,1024]{1,0:T(8,128)(2,1)}, u32[]{:S(2)}) copy-start(bf16[512,1024]{1,0:T(8,128)(2,1)} %emit_rows_ref.1) | copy-start | bytes 3145732
  5.2 8.2 %copy-start.7 = (bf16[3,8,1024,16]{2,3,1,0:T(8,128)(2,1)S(1)}, bf16[3,8,1024,16]{2,3,1,0:T(8,128)(2,1)}, u32[]{:S(2)}) copy-start(bf16[3,8,1024,16]{2,3,1,0:T(8,128)(2,1)} %param.13) | copy-start | bytes 2359300
  13.4 9.4 %copy-start.13 = (bf16[2,128,1024]{2,1,0:T(8,128)(2,1)}, bf16[2,128,1024]{2,1,0:T(8,128)(2,1)S(1)}, u32[]{:S(2)}) copy-start(bf16[2,128,1024]{2,1,0:T(8,128)(2,1)S(1)} %get-tuple-element.25.y_ref) | copy-start | bytes 1572868
  22.8 50.1 %copy-start.9 = (bf16[1024,384]{1,0:T(8,128)(2,1)}, bf16[1024,384]{1,0:T(8,128)(2,1)S(1)}, u32[]{:S(2)}) copy-start(bf16[1024,384]{1,0:T(8,128)(2,1)S(1)} %get-tuple-element.18.weight_ref) | copy-start | bytes 2359300
  22.8 56.4 %copy-start.12 = (bf16[8,16,1024]{2,1,0:T(8,128)(2,1)S(1)}, bf16[8,16,1024]{2,1,0:T(8,128)(2,1)}, u32[]{:S(2)}) copy-start(bf16[8,16,1024]{2,1,0:T(8,128)(2,1)} %param.7) | copy-start | bytes 786436
  72.9 29.2 %all-to-all-start = ((bf16[64,48,128]{2,1,0:T(8,128)(2,1)}), bf16[64,48,128]{2,1,0:T(8,128)(2,1)S(1)}, u32[]{:S(2)}, u32[]{:S(2)}) async-start(bf16[64,48,128]{2,1,0:T(8,128)(2,1)} %get-tuple-element.16), calls=%async_computation | async-start | bytes 1572864 | tf_op jit(solution)/shard_map/all_to_all | solution.py:232
  79.1 23.0 %copy-start = (bf16[1024,1024]{1,0:T(8,128)(2,1)S(1)}, bf16[1024,1024]{1,0:T(8,128)(2,1)}, u32[]{:S(2)}) copy-start(bf16[1024,1024]{1,0:T(8,128)(2,1)} %rows_ref.3) | copy-start | bytes 6291460
  79.1 1.3 copy-start.8
  80.4 1.0 copy-start.14
  89.3 1.3 copy-start.1
  102.1 4.9 %copy-start.2 = (bf16[1024,1024]{1,0:T(8,128)(2,1)S(1)}, bf16[1024,1024]{1,0:T(8,128)(2,1)}, u32[]{:S(2)}) copy-start(bf16[1024,1024]{1,0:T(8,128)(2,1)} %copy-done.1) | copy-start | bytes 6291460
  102.1 1.3 copy-start.10
  107.2 4.3 %collective-permute-start = (bf16[1024,1024]{1,0:T(8,128)(2,1)S(1)}, bf16[1024,1024]{1,0:T(8,128)(2,1)S(1)}, u32[]{:S(2)}, u32[]{:S(2)}) collective-permute-start(bf16[1024,1024]{1,0:T(8,128)(2,1)S(1)} %broadcast_select_fusion), channel_id=1, source_target_pairs={{0,1},{1,0},{2,3},{3,2},{4,5},{5,4},{6,7},{7,6},{8,9},{9,8},{10,11... | collective-permute-start | bytes 6291464 | tf_op jit(solution)/shard_map/ppermute | solution.py:278
  155.7 11.3 %all-to-all-start.6 = ((bf16[8,8,1024]{2,1,0:T(8,128)(2,1)}), bf16[8,8,1024]{2,1,0:T(8,128)(2,1)S(1)}, u32[]{:S(2)}, u32[]{:S(2)}) async-start(bf16[8,8,1024]{2,1,0:T(8,128)(2,1)} %bitcast.9), calls=%async_computation.6 | async-start | bytes 262144 | tf_op jit(solution)/shard_map/all_to_all | solution.py:232
  167.0 19.7 %all-to-all-start.2 = ((bf16[64,16,128]{2,1,0:T(8,128)(2,1)}), bf16[64,16,128]{2,1,0:T(8,128)(2,1)S(1)}, u32[]{:S(2)}, u32[]{:S(2)}) async-start(bf16[64,16,128]{2,1,0:T(8,128)(2,1)} %get-tuple-element.22), calls=%async_computation.2 | async-start | bytes 524288 | tf_op jit(solution)/shard_map/all_to_all | solution.py:232
  175.3 14.0 %collective-permute-start.1 = (f32[4,1024]{1,0:T(4,128)S(1)}, f32[4,1024]{1,0:T(4,128)S(1)}, u32[]{:S(2)}, u32[]{:S(2)}) collective-permute-start(f32[4,1024]{1,0:T(4,128)S(1)} %slice_select_fusion), channel_id=1, source_target_pairs={{0,1},{1,0},{2,3},{3,2},{4,5},{5,4},{6,7},{7,6},{8,9},{9,8},{10,11... | collective-permute-start | bytes 49160 | tf_op jit(solution)/shard_map/ppermute | solution.py:286

commit v2 on v1

v2 whole, which is shorter than its diff:
```python
import jax
import jax.numpy as jnp
from jax import lax
from jax.experimental import pallas as pl
from jax.experimental.pallas import tpu as pltpu
from jax.sharding import PartitionSpec as P

STEPS = 3
F32 = jnp.float32
BF16 = jnp.bfloat16
SEQ_DEV = 8
PART = 16
ROWS = SEQ_DEV * PART
WIDTH = 1024
PEERS = WIDTH // PART
VMEM = 24 * 2**20
ALONE = 60 * 2**20
NORM = 2 * STEPS * PART
WIRE = NORM + 8


def iota(shape, dim):
    return lax.broadcasted_iota(jnp.int32, shape, dim)


def dot(a, b):
    return lax.dot_general(a, b, (((1,), (0,)), ((), ())), preferred_element_type=F32)


def dot_nt(a, b):
    return lax.dot_general(a, b, (((1,), (1,)), ((), ())), preferred_element_type=F32)


def dot_tn(a, b):
    return lax.dot_general(a, b, (((0,), (0,)), ((), ())), preferred_element_type=F32)


def pick(tok_ref, emit_ref):
    rows = emit_ref.shape[0]
    hot = [
        (tok_ref[t : t + 1, :] == iota((rows, SEQ_DEV), 0)).astype(F32) for t in range(STEPS)
    ]
    return dot_tn(jnp.concatenate(hot, axis=1).astype(BF16), emit_ref[...])


def step_of(v, t):
    return v[t * SEQ_DEV : (t + 1) * SEQ_DEV]


def spread(v):
    n = v.shape[-1]
    return jnp.broadcast_to(v[:, None, :], (SEQ_DEV, PART, n)).reshape(ROWS, n)


def column_of(v, offset):
    at = offset + (iota((ROWS, WIDTH), 0) & (PART - 1))
    return jnp.sum(jnp.where(iota((ROWS, WIDTH), 1) == at, spread(v), 0.0), axis=1, keepdims=True)


def swap(tiles):
    group = iota((PART, 128), 1) >> 4
    for bit in (1, 2, 4):
        low = (group & bit) == 0
        out = list(tiles)
        for s in range(SEQ_DEV):
            if s & bit == 0:
                a, b = tiles[s], tiles[s + bit]
                out[s] = jnp.where(low, a, pltpu.roll(b, PART * bit, 1))
                out[s + bit] = jnp.where(low, pltpu.roll(a, 128 - PART * bit, 1), b)
        tiles = out
    return tiles


def to_wire(src_ref, dst_ref, row):
    for g in range(PEERS // SEQ_DEV):
        lanes = slice(g * 128, (g + 1) * 128)
        tiles = swap([src_ref[s * PART : (s + 1) * PART, lanes] for s in range(SEQ_DEV)])
        for s in range(SEQ_DEV):
            dst_ref[g * SEQ_DEV + s, row : row + PART, :] = tiles[s].astype(BF16)


def from_wire(src_ref, row, store):
    for g in range(PEERS // SEQ_DEV):
        tiles = swap(
            [src_ref[g * SEQ_DEV + s, row : row + PART, :].astype(F32) for s in range(SEQ_DEV)]
        )
        lanes = slice(g * 128, (g + 1) * 128)
        for s in range(SEQ_DEV):
            store(s, lanes, tiles[s])


def state_index():
    return (lax.axis_index("y") * 8 + lax.axis_index("z")) * 2 + lax.axis_index("core")


def total_of(wire_ref):
    return jnp.sum(jnp.sum(wire_ref[:, NORM:WIRE, :].astype(F32), axis=0), axis=0, keepdims=True)


def inverse_norm(totals, t):
    at = STEPS * (iota((ROWS, 128), 0) >> 4) + t
    total = jnp.sum(jnp.where(iota((ROWS, 128), 1) == at, totals, 0.0), axis=1, keepdims=True)
    return float(WIDTH * WIDTH) / total


def send_kernel(
    tok_ref, alpha_hbm, rows_hbm, cols_hbm, emit_rows_hbm, emit_cols_hbm, back_hbm,
    wire_hbm, y_hbm, alpha_ref, rows_ref, cols_ref, emit_rows_ref, emit_cols_ref, back_ref,
    wire_ref, y_ref, x_ref, wt_ref, g_ref, in_sem, out_sem,
):
    pairs = [
        (emit_cols_hbm, emit_cols_ref), (alpha_hbm, alpha_ref), (cols_hbm, cols_ref),
        (emit_rows_hbm, emit_rows_ref), (back_hbm, back_ref), (rows_hbm, rows_ref),
    ]
    loads = [pltpu.make_async_copy(a, b, in_sem.at[n]) for n, (a, b) in enumerate(pairs)]
    for load in loads:
        load.start()
    stores = []

    def keep(src, dst):
        store = pltpu.make_async_copy(src, dst, out_sem.at[len(stores)])
        store.start()
        stores.append(store)

    def send(n, value):
        x_ref[...] = value
        at = slice(n * PART, (n + 1) * PART)
        to_wire(x_ref, wire_ref, n * PART)
        keep(wire_ref.at[:, at, :], wire_hbm.at[:, at, :])

    offset = state_index() * PART
    loads[0].wait()
    second = pick(tok_ref, emit_cols_ref)
    loads[1].wait()
    loads[2].wait()
    y = alpha_ref[...]
    sums = []
    for t in range(STEPS):
        x = dot(y, cols_ref[...])
        y32 = x * spread(step_of(second, t))
        sums.append(jnp.sum(y32, axis=1, keepdims=True))
        if t < STEPS - 1:
            y = y32.astype(BF16)
            y_ref[t] = y
        send(t, x)
    keep(y_ref, y_hbm)

    loads[3].wait()
    first = pick(tok_ref, emit_rows_ref)
    f0, f1 = (spread(step_of(first, t)) for t in range(2))
    loads[4].wait()
    for t in range(STEPS):
        column = column_of(step_of(second, t), offset)
        w = spread(step_of(first, t)) * column * back_ref[t].astype(F32)
        wt_ref[t * ROWS : (t + 1) * ROWS, :] = w.astype(BF16)
    wt_ref[STEPS * ROWS :, :] = first.astype(BF16)
    loads[5].wait()
    v = dot_nt(wt_ref[...], rows_ref[...])
    ends = [v[3 * ROWS : 3 * ROWS + 8]]
    g_ref[:ROWS] = (v[ROWS : 2 * ROWS] * f0).astype(BF16)
    g_ref[ROWS : 2 * ROWS] = (v[2 * ROWS : 3 * ROWS] * f1).astype(BF16)
    g_ref[2 * ROWS :] = (v[3 * ROWS + 8 :] * first[:16]).astype(BF16)
    send(STEPS, v[:ROWS])
    v = dot_nt(g_ref[...], rows_ref[...])
    ends.append(v[2 * ROWS : 2 * ROWS + 8])
    g_ref[:ROWS] = (v[ROWS : 2 * ROWS] * f0).astype(BF16)
    tail = (v[2 * ROWS + 8 :] * first[:8]).astype(BF16)
    g_ref[ROWS : ROWS + 16] = jnp.concatenate([tail, tail], axis=0)
    send(STEPS + 1, v[:ROWS])
    v = dot_nt(g_ref[: ROWS + 16], rows_ref[...])
    ends.append(v[ROWS : ROWS + 8])
    send(STEPS + 2, v[:ROWS])

    norm = jnp.zeros((1, 128), F32)
    for t in range(STEPS):
        part = sums[t] * column_of(ends[t], offset)
        at = STEPS * (iota((ROWS, 128), 0) >> 4) + t
        norm = norm + jnp.sum(jnp.where(iota((ROWS, 128), 1) == at, part, 0.0), axis=0, keepdims=True)
    high = norm.astype(BF16).astype(F32)
    middle = (norm - high).astype(BF16).astype(F32)
    low = norm - high - middle
    row = iota((8, 128), 0)
    parts = jnp.where(row == 0, high, jnp.where(row == 1, middle, jnp.where(row == 2, low, 0.0)))
    wire_ref[:, NORM:WIRE, :] = jnp.broadcast_to(parts.astype(BF16)[None], (PEERS, 8, 128))
    keep(wire_ref.at[:, NORM:WIRE, :], wire_hbm.at[:, NORM:WIRE, :])
    for store in stores:
        store.wait()


def to_row(column):
    return jnp.sum(
        jnp.where(iota((128, 128), 0) == iota((128, 128), 1), column, 0.0), axis=0, keepdims=True
    )


def local_kernel(
    tok_ref, rows_ref, cols_ref, emit_rows_ref, emit_cols_ref, back_ref,
    weight_ref, turned_ref, factor_ref, local_ref, take_rows_ref, take_cols_ref,
):
    me = state_index()
    first = pick(tok_ref, emit_rows_ref)
    second = pick(tok_ref, emit_cols_ref)
    pair = (iota((SEQ_DEV, ROWS), 1) >> 4 == iota((SEQ_DEV, ROWS), 0)).astype(F32).astype(BF16)
    for t in range(STEPS):
        column = column_of(step_of(second, t), me * PART)
        w = spread(step_of(first, t)) * column * back_ref[t].astype(F32)
        weight_ref[:, t * ROWS : (t + 1) * ROWS] = w.T.astype(BF16)
        factor_ref[t] = dot_tn(step_of(first, t).astype(BF16), pair).astype(BF16)
        if t == STEPS - 1:
            local_ref[...] = to_row(column)

    @pl.loop(0, WIDTH // 128)
    def _(b):
        at = pl.ds(pl.multiple_of(b * 128, 128), 128)
        turned_ref[at, :] = rows_ref[:, at].astype(F32).T.astype(BF16)

    mine = (lax.axis_index("dp") * PEERS + me) * 4
    hot = (iota((8, WIDTH), 1) == mine + iota((8, WIDTH), 0)) & (iota((8, WIDTH), 0) < 4)
    hot = hot.astype(F32).astype(BF16)
    take_rows_ref[...] = dot_nt(hot, rows_ref[...])
    take_cols_ref[...] = dot_nt(hot, cols_ref[...])


def counts_kernel(
    wire_hbm, y_hbm, alpha_hbm, turned_hbm, factor_hbm, weight_hbm, local_ref,
    out_hbm, keep_hbm, give_hbm, total_ref,
    wire_ref, y_ref, alpha_ref, turned_ref, factor_ref, weight_ref, out_ref,
    rows_ref, cols_ref, ys_ref, m_ref, in_sem, out_sem,
):
    pairs = [
        (wire_hbm, wire_ref), (y_hbm, y_ref), (alpha_hbm, alpha_ref), (turned_hbm, turned_ref),
        (factor_hbm, factor_ref), (weight_hbm, weight_ref),
    ]
    loads = [pltpu.make_async_copy(a, b, in_sem.at[n]) for n, (a, b) in enumerate(pairs)]
    for load in loads:
        load.start()
    for load in loads[:3]:
        load.wait()
    core = lax.axis_index("core")
    keep_rows = pltpu.make_async_copy(rows_ref, keep_hbm, out_sem.at[1])
    give_rows = pltpu.make_async_copy(rows_ref, give_hbm, out_sem.at[1])
    keep_cols = pltpu.make_async_copy(cols_ref, keep_hbm, out_sem.at[2])
    give_cols = pltpu.make_async_copy(cols_ref, give_hbm, out_sem.at[2])

    totals = total_of(wire_ref)
    total_ref[...] = totals
    inverse = [inverse_norm(totals, t) for t in range(STEPS)]
    inv = [to_row(i) for i in inverse]
    for t in range(STEPS):
        y = alpha_ref[...] if t == 0 else y_ref[t - 1]
        ys_ref[t * ROWS : (t + 1) * ROWS] = (y.astype(F32) * inverse[t]).astype(BF16)
    for b in range(4):
        peers = slice(b * 16, (b + 1) * 16)
        v = jnp.concatenate(
            [
                wire_ref[peers, (STEPS + t) * PART : (STEPS + t + 1) * PART, :].reshape(256, ROWS)
                for t in range(STEPS)
            ],
            axis=1,
        )
        cols_ref[b * 256 : (b + 1) * 256, :] = dot(v, ys_ref[...]).astype(BF16)

    @pl.when(core == 0)
    def _():
        give_cols.start()

    @pl.when(core == 1)
    def _():
        keep_cols.start()

    def x_of(t):
        return wire_ref[:, t * PART : (t + 1) * PART, :].reshape(WIDTH, ROWS)

    m_ref[:, :ROWS] = (x_of(0).astype(F32) * inv[0]).astype(BF16)
    loads[3].wait()
    loads[4].wait()
    f0, f1, f2 = (factor_ref[t].astype(F32) for t in range(STEPS))
    h = dot(turned_ref[...], jnp.concatenate([x_of(1), x_of(2)], axis=1))
    m_ref[:, ROWS : 2 * ROWS] = (h[:, :ROWS] * f0 * inv[1]).astype(BF16)
    h = dot(turned_ref[...], (h[:, ROWS:] * f0).astype(BF16)) * f1
    m_ref[:, 2 * ROWS :] = (h * inv[2]).astype(BF16)
    a = dot(turned_ref[...], h.astype(BF16)) * f2 * (local_ref[...] * inv[2])
    out_ref[...] = a.astype(BF16).reshape(PEERS, PART, ROWS)
    send = pltpu.make_async_copy(out_ref, out_hbm, out_sem.at[0])
    send.start()
    loads[5].wait()
    for b in range(WIDTH // 256):
        at = slice(b * 256, (b + 1) * 256)
        rows_ref[:, at] = dot_nt(weight_ref[...], m_ref[at, :]).astype(BF16)

    @pl.when(core == 0)
    def _():
        keep_rows.start()
        keep_rows.wait()
        give_cols.wait()

    @pl.when(core == 1)
    def _():
        give_rows.start()
        give_rows.wait()
        keep_cols.wait()

    send.wait()


def pair_kernel(keep_ref, got_ref, *outs):
    half = WIDTH // 2
    x, y = lax.axis_index("dp"), lax.axis_index("y")

    def piece(at, lanes):
        return (keep_ref[at, lanes].astype(F32) + got_ref[at, lanes].astype(F32)).astype(BF16)

    for d in range(4):
        at = pl.ds(pl.multiple_of(((x + d) & 3) * 256, 256), 256)
        outs[d][...] = piece(at, slice(0, half))
        for b in range(4):
            at = pl.ds(pl.multiple_of(b * 256 + ((y + d) & 3) * 64, 64), 64)
            outs[4 + d][b * 64 : (b + 1) * 64, :] = piece(at, slice(half, WIDTH))


def plane_kernel(*refs):
    ins, outs, (sum_ref,) = refs[:8], refs[8:16], refs[16:]
    for side in range(2):
        at = lax.axis_index("y" if side == 0 else "dp")
        group = ins[4 * side : 4 * side + 4]
        sum_ref[...] = sum(r[...].astype(F32) for r in group)
        for d in range(4):
            rows = pl.ds(pl.multiple_of(((at + d) & 3) * 64, 64), 64)
            outs[4 * side + d][...] = sum_ref[rows, :].astype(BF16)


def line_kernel(*refs):
    ins, out_ref = refs[:8], refs[8]
    half = WIDTH // 2
    for side in range(2):
        group = ins[4 * side : 4 * side + 4]
        total = sum(r[...].astype(F32) for r in group).astype(BF16)
        out_ref[:, side * half : (side + 1) * half] = total


def final_kernel(wire_ref, out_ref):
    def store(s, lanes, tile):
        out_ref[s * PART : (s + 1) * PART, lanes] = tile.astype(BF16)

    from_wire(wire_ref, 0, store)


def call(kernel, name, outs, scratch=(), flops=10**9, moved=8 * 10**6, limit=VMEM, specs=None):
    return pl.pallas_call(
        kernel,
        name=name,
        out_shape=[jax.ShapeDtypeStruct(s, d) for s, d in outs],
        scratch_shapes=[s if hasattr(s, "dtype") else pltpu.VMEM(*s) for s in scratch],
        compiler_params=pltpu.CompilerParams(vmem_limit_bytes=limit),
        cost_estimate=pl.CostEstimate(flops=flops, bytes_accessed=moved, transcendentals=0),
        **(specs or {}),
    )


def ring(x, axis, d, n=4):
    return lax.ppermute(x, axis, [(i, (i + d) % n) for i in range(n)])


def spread_out(pieces, axis):
    far, right, left = (ring(pieces[d], axis, d) for d in (2, 1, 3))
    return [pieces[0], right, far, left]


def on_device(alpha_init, tokens, trans_rows, trans_cols, emit_rows, emit_cols, backward):
    alpha = alpha_init.reshape(ROWS, WIDTH)
    back = jnp.swapaxes(backward, 2, 3).reshape(STEPS, ROWS, WIDTH)
    tok = tokens.T
    half = WIDTH // 2
    state = ("y", "z", "core")

    hbm = pl.BlockSpec(memory_space=pltpu.HBM)
    wire_shape, y_shape = (PEERS, WIRE, ROWS), (STEPS - 1, ROWS, WIDTH)
    square, emit_shape = (WIDTH, WIDTH), emit_rows.shape
    wire, y = call(
        send_kernel, "send", [(wire_shape, BF16), (y_shape, BF16)],
        [
            ((ROWS, WIDTH), BF16), (square, BF16), (square, BF16), (emit_shape, BF16),
            (emit_shape, BF16), ((STEPS, ROWS, WIDTH), BF16), (wire_shape, BF16),
            (y_shape, BF16), ((ROWS, WIDTH), F32), ((STEPS * (ROWS + 8), WIDTH), BF16),
            ((2 * (ROWS + 8), WIDTH), BF16), pltpu.SemaphoreType.DMA((6,)),
            pltpu.SemaphoreType.DMA((8,)),
        ],
        limit=ALONE,
        specs=dict(
            in_specs=[pl.BlockSpec(memory_space=pltpu.VMEM)] + [hbm] * 6, out_specs=[hbm] * 2
        ),
    )(tok, alpha, trans_rows, trans_cols, emit_rows, emit_cols, back)
    got = lax.all_to_all(wire, state, 0, 0, tiled=True)

    weight, turned, factor, local, take_rows, take_cols = call(
        local_kernel, "local",
        [
            ((WIDTH, STEPS * ROWS), BF16), (square, BF16), ((STEPS, WIDTH, ROWS), BF16),
            ((1, ROWS), F32), ((8, WIDTH), F32), ((8, WIDTH), F32),
        ],
        limit=ALONE,
    )(tok, trans_rows, trans_cols, emit_rows, emit_cols, back)

    a_shape = (PEERS, PART, ROWS)
    a_wire, keep, give, total = call(
        counts_kernel, "counts",
        [(a_shape, BF16), (square, BF16), (square, BF16), ((1, 128), F32)],
        [
            (wire_shape, BF16), (y_shape, BF16), ((ROWS, WIDTH), BF16), (square, BF16),
            ((STEPS, WIDTH, ROWS), BF16), ((WIDTH, STEPS * ROWS), BF16), (a_shape, BF16),
            (square, BF16), (square, BF16), ((STEPS * ROWS, WIDTH), BF16),
            ((WIDTH, STEPS * ROWS), BF16), pltpu.SemaphoreType.DMA((6,)),
            pltpu.SemaphoreType.DMA((3,)),
        ],
        limit=ALONE,
        specs=dict(
            in_specs=[hbm] * 6 + [pl.BlockSpec(memory_space=pltpu.VMEM)],
            out_specs=[hbm] * 3 + [pl.BlockSpec(memory_space=pltpu.VMEM)],
        ),
    )(got, y, alpha, turned, factor, weight, local)

    core = lax.axis_index("core")
    swap_cores = [(0, 1), (1, 0)]
    pieces = call(pair_kernel, "pair", [((256, half), BF16)] * 8)(
        keep, lax.ppermute(give, "core", swap_cores)
    )
    a_wire, *pieces = lax.optimization_barrier((a_wire, *pieces))
    parts = spread_out(pieces[:4], "dp") + spread_out(pieces[4:], "y")
    a_got = lax.all_to_all(a_wire, state, 0, 0, tiled=True)
    pieces = call(plane_kernel, "plane", [((64, half), BF16)] * 8, [((256, half), F32)])(*parts)
    a_got, *pieces = lax.optimization_barrier((a_got, *pieces))
    parts = spread_out(pieces[:4], "y") + spread_out(pieces[4:], "dp")
    (part,) = call(line_kernel, "line", [((64, WIDTH), BF16)])(*parts)
    (alpha_final,) = call(final_kernel, "final", [((ROWS, WIDTH), BF16)])(a_got)
    part, alpha_final = lax.optimization_barrier((part, alpha_final))
    part = lax.all_to_all(part.reshape(8, 8, WIDTH), "z", 0, 0, tiled=True)
    part = jnp.sum(part.astype(F32), axis=0)
    mine = jnp.where(core == 0, part[:4], part[4:])
    other = lax.ppermute(jnp.where(core == 0, part[4:], part[:4]), "core", swap_cores)
    scale = 1.0 / (SEQ_DEV * 4 * STEPS)
    counts_rows = jnp.where(core == 0, mine, other) * take_rows[:4] * scale
    counts_cols = jnp.where(core == 0, other, mine) * take_cols[:4] * scale

    loglik = jnp.log(total[0, 2 : 3 * SEQ_DEV : 3] / (WIDTH * WIDTH))
    return (
        alpha_final.reshape(SEQ_DEV, PART, WIDTH),
        counts_rows.T,
        counts_cols.T,
        loglik,
    )


def solution(mesh):
    mesh = jax.sharding.Mesh(mesh.devices.reshape(4, 4, 8, 2), ("dp", "y", "z", "core"))
    state = ("y", "z", "core")
    return jax.shard_map(
        on_device,
        mesh=mesh,
        in_specs=(
            P("dp", state, None),
            P("dp", None),
            P(),
            P(),
            P(),
            P(),
            P(None, "dp", None, state),
        ),
        out_specs=(
            P("dp", state, None),
            P(None, ("dp", *state)),
            P(None, ("dp", *state)),
            P("dp"),
        ),
        check_vma=False,
    )
```

time: 191 us -> 143 us (0.75)
  blocking collectives: 91.6 us -> 0 us
  starting transfers between devices: 18.4 us -> 46.8 us
  waiting for transfers between devices: 33.9 us -> 61.2 us
  local copies, waits for them, and re-layouts: 9.61 us -> 2.89 us
  other arithmetic: 4.14 us -> 1.18 us
    all_to_all x4 -> x0, blocking collectives: 91.6 us -> none  [exchange(): return lax.all_to_all(x, axis, 0, 0, axis_index_groups=groups, tiled=True)]
    ppermute x2 -> x14, starting transfers between devices: 1.14 us -> 21.1 us  [the longest x12 16.8 us: ring(): return lax.ppermute(x, axis, [(i, (i + d) % n) for i in range(n)])]
    ppermute x2 -> x14, waiting for transfers between devices: 3.79 us -> 18 us  [the longest x12 13.3 us: ring(): return lax.ppermute(x, axis, [(i, (i + d) % n) for i in range(n)])]
    all_to_all x3, waiting for transfers between devices: 30.1 us -> 43.2 us  [the longest x1 35.4 us: on_device(): got = lax.all_to_all(wire, state, 0, 0, tiled=True)]
    all_to_all x3, starting transfers between devices: 17.2 us -> 25.7 us  [the longest x1 13.2 us: on_device(): got = lax.all_to_all(wire, state, 0, 0, tiled=True)]
    unnamed x31 -> x10, local copies, waits for them, and re-layouts: 9.5 us -> 2.79 us
    pallas_call x4 -> x6, Pallas kernels: 29 us -> 28.6 us  [the longest x1 10.8 us: on_device(): call(counts_kernel, 'counts', [(a_shape, BF16), (square, BF16), (square,...]
  transfers between devices with their start and end apart: 5 -> 17, of which waited for: 4 -> 10; matrix products, arithmetic and copies ran while one was open for 0% -> 0% of each run, Pallas kernels for 5% -> 6%
where the time goes in v2:
time: 143 us
  waiting for transfers between devices  61.2 us (43%)
  starting transfers between devices  46.8 us (33%)
  Pallas kernels  29.9 us (21%)
  local copies, waits for them, and re-layouts  2.89 us (2%)
    all_to_all x1, waiting for transfers between devices, on_device(): got = lax.all_to_all(wire, state, 0, 0, tiled=True)  35.4 us
    ppermute x12, starting transfers between devices, ring(): return lax.ppermute(x, axis, [(i, (i + d) % n) for i in range(n)])  16.8 us
    ppermute x12, waiting for transfers between devices, ring(): return lax.ppermute(x, axis, [(i, (i + d) % n) for i in range(n)])  13.3 us
    all_to_all x1, starting transfers between devices, on_device(): got = lax.all_to_all(wire, state, 0, 0, tiled=True)  13.2 us
    pallas_call x1, Pallas kernels, on_device(): call(counts_kernel, 'counts', [(a_shape, BF16), (square, BF16), (square,...  10.8 us
    pallas_call x1, Pallas kernels, on_device(): call(send_kernel, 'send', [(wire_shape, BF16), (y_shape, BF16)], [((ROWS,...  8.92 us
    all_to_all x1, waiting for transfers between devices, on_device(): part = lax.all_to_all(part.reshape(8, 8, WIDTH), 'z', 0, 0, tiled=True)  7.88 us
    pallas_call x1, Pallas kernels, on_device(): call(local_kernel, 'local', [((WIDTH, STEPS * ROWS), BF16), (square, BF16...  7.24 us
  transfers between devices with their start and end apart: 17, of which 10 were waited for; matrix products, arithmetic and copies ran while one was open for 0% of the time, Pallas kernels for 6%

profile of v2, /device:TPU:1, one launch (start us, length us, event | category | flops | bytes accessed | tf_op | source)
XLA Modules:
  0.0 142.7 jit_solution(18371584240699556167)
XLA Ops:
  0.6 8.9 %send.1 = (bf16[64,104,128]{2,1,0:T(8,128)(2,1)}, bf16[2,128,1024]{2,1,0:T(8,128)(2,1)}) custom-call(s32[3,8]{1,0:T(4,128)} %bitcast.17, bf16[128,1024]{1,0:T(8,128)(2,1)} %bitcast.15, bf16[1024,1024]{1,0:T(8,128)(2,1)} %rows_ref.1, bf16[1024,1024]{1,0:T(8,128)(2,1)} %cols_ref.1, bf16[512,1024]{1,0:T(8,128)(2,1)} %emit_rows_ref.1, ...), custom_call_target="tpu_custom_call" | custom-call | flops 1000000000 | bytes 8000000 | tf_op jit(solution)/shard_map/send/pallas_call | solution.py:379
  9.6 13.2 %all-to-all-start = ((bf16[64,104,128]{2,1,0:T(8,128)(2,1)}), bf16[64,104,128]{2,1,0:T(8,128)(2,1)S(1)}, u32[]{:S(2)}, u32[]{:S(2)}) async-start(bf16[64,104,128]{2,1,0:T(8,128)(2,1)} %get-tuple-element.52), calls=%async_computation | async-start | bytes 3407872 | tf_op jit(solution)/shard_map/all_to_all | solution.py:393
  22.8 7.2 %local.1 = (bf16[1024,384]{1,0:T(8,128)(2,1)}, bf16[1024,1024]{1,0:T(8,128)(2,1)}, bf16[3,1024,128]{2,1,0:T(8,128)(2,1)}, f32[1,128]{1,0:T(1,128)}, f32[8,1024]{1,0:T(8,128)}, /*index=5*/f32[8,1024]{1,0:T(8,128)}) custom-call(s32[3,8]{1,0:T(4,128)} %bitcast.18, bf16[1024,1024]{1,0:T(8,128)(2,1)} %rows_ref.1, bf16[1024,1024]{1,0:T(8,128)(2,1)} %cols_ref.1, ...), custom_call_target="tpu_custom_call" | custom-call | flops 1000000000 | bytes 8000000 | tf_op jit(solution)/shard_map/local/pallas_call | solution.py:395
  30.0 35.4 %all-to-all-done.wire_hbm = bf16[64,104,128]{2,1,0:T(8,128)(2,1)S(1)} async-done(((bf16[64,104,128]{2,1,0:T(8,128)(2,1)}), bf16[64,104,128]{2,1,0:T(8,128)(2,1)S(1)}, u32[]{:S(2)}, u32[]{:S(2)}) %all-to-all-start) | async-done | bytes 1703968 | tf_op jit(solution)/shard_map/all_to_all | solution.py:393
  65.3 1.2 copy-done.1
  66.5 10.8 %counts.1 = (bf16[64,16,128]{2,1,0:T(8,128)(2,1)}, bf16[1024,1024]{1,0:T(8,128)(2,1)}, bf16[1024,1024]{1,0:T(8,128)(2,1)}, f32[1,128]{1,0:T(1,128)}) custom-call(bf16[64,104,128]{2,1,0:T(8,128)(2,1)} %copy-done.1, bf16[2,128,1024]{2,1,0:T(8,128)(2,1)} %get-tuple-element.53.y_hbm, bf16[128,1024]{1,0:T(8,128)(2,1)} %bitcast.16, ...), custom_call_target="tpu_custom_call" | custom-call | flops 1000000000 | bytes 8000000 | tf_op jit(solution)/shard_map/counts/pallas_call | solution.py:405
  77.5 4.3 %collective-permute-done.got_ref = bf16[1024,1024]{1,0:T(8,128)(2,1)S(1)} collective-permute-done((bf16[1024,1024]{1,0:T(8,128)(2,1)}, bf16[1024,1024]{1,0:T(8,128)(2,1)S(1)}, u32[]{:S(2)}, u32[]{:S(2)}) %collective-permute-start) | collective-permute-done | bytes 2097184 | tf_op jit(solution)/shard_map/ppermute | solution.py:425
  81.8 1.6 %copy-done = bf16[1024,1024]{1,0:T(8,128)(2,1)S(1)} copy-done((bf16[1024,1024]{1,0:T(8,128)(2,1)S(1)}, bf16[1024,1024]{1,0:T(8,128)(2,1)}, u32[]{:S(2)}) %copy-start) | copy-done | bytes 2097176
  83.9 1.3 collective-permute-start.1
  85.1 6.3 %all-to-all-start.1 = ((bf16[64,16,128]{2,1,0:T(8,128)(2,1)}), bf16[64,16,128]{2,1,0:T(8,128)(2,1)S(1)}, u32[]{:S(2)}, u32[]{:S(2)}) async-start(bf16[64,16,128]{2,1,0:T(8,128)(2,1)} %get-tuple-element.69), calls=%async_computation.1 | async-start | bytes 524288 | tf_op jit(solution)/shard_map/all_to_all | solution.py:429
  91.5 2.5 %collective-permute-start.2 = (bf16[256,512]{1,0:T(8,128)(2,1)S(1)}, bf16[256,512]{1,0:T(8,128)(2,1)S(1)}, u32[]{:S(2)}, u32[]{:S(2)}) collective-permute-start(bf16[256,512]{1,0:T(8,128)(2,1)S(1)} %get-tuple-element.72), channel_id=1, source_target_pairs={{0,128},{64,192},{128,0},{192,64},{1,129},{65,193},{129,1},{193,65... | collective-permute-start | bytes 786440 | tf_op jit(solution)/shard_map/ppermute | solution.py:361
  94.0 1.1 collective-permute-start.3
  95.2 1.4 collective-permute-start.4
  96.6 2.6 %collective-permute-start.5 = (bf16[256,512]{1,0:T(8,128)(2,1)S(1)}, bf16[256,512]{1,0:T(8,128)(2,1)S(1)}, u32[]{:S(2)}, u32[]{:S(2)}) collective-permute-start(bf16[256,512]{1,0:T(8,128)(2,1)S(1)} %get-tuple-element.76), channel_id=1, source_target_pairs={{0,32},{16,48},{32,0},{48,16},{1,33},{17,49},{33,1},{49,17},{2,34}... | collective-permute-start | bytes 786440 | tf_op jit(solution)/shard_map/ppermute | solution.py:361
  99.2 1.1 collective-permute-start.6
  100.5 4.7 %collective-permute-done.3.refs_3_ = bf16[256,512]{1,0:T(8,128)(2,1)S(1)} collective-permute-done((bf16[256,512]{1,0:T(8,128)(2,1)S(1)}, bf16[256,512]{1,0:T(8,128)(2,1)S(1)}, u32[]{:S(2)}, u32[]{:S(2)}) %collective-permute-start.3) | collective-permute-done | bytes 262176 | tf_op jit(solution)/shard_map/ppermute | solution.py:361
  106.2 6.2 %collective-permute-done.5.refs_6_ = bf16[256,512]{1,0:T(8,128)(2,1)S(1)} collective-permute-done((bf16[256,512]{1,0:T(8,128)(2,1)S(1)}, bf16[256,512]{1,0:T(8,128)(2,1)S(1)}, u32[]{:S(2)}, u32[]{:S(2)}) %collective-permute-start.5) | collective-permute-done | bytes 262176 | tf_op jit(solution)/shard_map/ppermute | solution.py:361
  113.6 1.1 collective-permute-start.11
  114.7 1.4 collective-permute-start.12
  116.7 2.3 %collective-permute-start.8 = (bf16[64,512]{1,0:T(8,128)(2,1)S(1)}, bf16[64,512]{1,0:T(8,128)(2,1)S(1)}, u32[]{:S(2)}, u32[]{:S(2)}) collective-permute-start(bf16[64,512]{1,0:T(8,128)(2,1)S(1)} %get-tuple-element.88), channel_id=1, source_target_pairs={{0,32},{16,48},{32,0},{48,16},{1,33},{17,49},{33,1},{49,17},{2,34}... | collective-permute-start | bytes 196616 | tf_op jit(solution)/shard_map/ppermute | solution.py:361
  119.6 1.3 final.1
  122.8 6.1 %all-to-all-start.2 = ((bf16[8,8,1024]{2,1,0:T(8,128)(2,1)}), bf16[8,8,1024]{2,1,0:T(8,128)(2,1)S(1)}, u32[]{:S(2)}, u32[]{:S(2)}) async-start(bf16[8,8,1024]{2,1,0:T(8,128)(2,1)} %bitcast.6), calls=%async_computation.2 | async-start | bytes 262144 | tf_op jit(solution)/shard_map/all_to_all | solution.py:436
  129.1 7.9 %all-to-all-done.2 = bf16[8,8,1024]{2,1,0:T(8,128)(2,1)S(1)} async-done(((bf16[8,8,1024]{2,1,0:T(8,128)(2,1)}), bf16[8,8,1024]{2,1,0:T(8,128)(2,1)S(1)}, u32[]{:S(2)}, u32[]{:S(2)}) %all-to-all-start.2) | async-done | bytes 131104 | tf_op jit(solution)/shard_map/all_to_all | solution.py:436
  137.0 4.2 %collective-permute-start.13 = (f32[4,1024]{1,0:T(4,128)S(1)}, f32[4,1024]{1,0:T(4,128)S(1)}, u32[]{:S(2)}, u32[]{:S(2)}) collective-permute-start(f32[4,1024]{1,0:T(4,128)S(1)} %slice_select_fusion), channel_id=1, source_target_pairs={{0,1},{1,0},{2,3},{3,2},{4,5},{5,4},{6,7},{7,6},{8,9},{9,8},{10,11... | collective-permute-start | bytes 49160 | tf_op jit(solution)/shard_map/ppermute | solution.py:439
  (32 shorter events, 7.7 us)
Async XLA Ops:
  9.6 55.8 %all-to-all-start = ((bf16[64,104,128]{2,1,0:T(8,128)(2,1)}), bf16[64,104,128]{2,1,0:T(8,128)(2,1)S(1)}, u32[]{:S(2)}, u32[]{:S(2)}) async-start(bf16[64,104,128]{2,1,0:T(8,128)(2,1)} %get-tuple-element.52), calls=%async_computation | async-start | bytes 3407872 | tf_op jit(solution)/shard_map/all_to_all | solution.py:393
  65.3 1.2 copy-start.1
  77.3 4.5 %collective-permute-start = (bf16[1024,1024]{1,0:T(8,128)(2,1)}, bf16[1024,1024]{1,0:T(8,128)(2,1)S(1)}, u32[]{:S(2)}, u32[]{:S(2)}) collective-permute-start(bf16[1024,1024]{1,0:T(8,128)(2,1)} %get-tuple-element.60), channel_id=1, source_target_pairs={{0,1},{1,0},{2,3},{3,2},{4,5},{5,4},{6,7},{7,6},{8,9},{9,8},{10,11... | collective-permute-start | bytes 6291464 | tf_op jit(solution)/shard_map/ppermute | solution.py:425
  81.8 1.6 %copy-start = (bf16[1024,1024]{1,0:T(8,128)(2,1)S(1)}, bf16[1024,1024]{1,0:T(8,128)(2,1)}, u32[]{:S(2)}) copy-start(bf16[1024,1024]{1,0:T(8,128)(2,1)} %get-tuple-element.59.keep_ref) | copy-start | bytes 6291460
  83.9 15.3 %collective-permute-start.1 = (bf16[256,512]{1,0:T(8,128)(2,1)S(1)}, bf16[256,512]{1,0:T(8,128)(2,1)S(1)}, u32[]{:S(2)}, u32[]{:S(2)}) collective-permute-start(bf16[256,512]{1,0:T(8,128)(2,1)S(1)} %get-tuple-element.71), channel_id=1, source_target_pairs={{0,64},{64,128},{128,192},{192,0},{1,65},{65,129},{129,193},{193,1... | collective-permute-start | bytes 786440 | tf_op jit(solution)/shard_map/ppermute | solution.py:361
  85.1 27.7 %all-to-all-start.1 = ((bf16[64,16,128]{2,1,0:T(8,128)(2,1)}), bf16[64,16,128]{2,1,0:T(8,128)(2,1)S(1)}, u32[]{:S(2)}, u32[]{:S(2)}) async-start(bf16[64,16,128]{2,1,0:T(8,128)(2,1)} %get-tuple-element.69), calls=%async_computation.1 | async-start | bytes 524288 | tf_op jit(solution)/shard_map/all_to_all | solution.py:429
  91.5 9.0 %collective-permute-start.2 = (bf16[256,512]{1,0:T(8,128)(2,1)S(1)}, bf16[256,512]{1,0:T(8,128)(2,1)S(1)}, u32[]{:S(2)}, u32[]{:S(2)}) collective-permute-start(bf16[256,512]{1,0:T(8,128)(2,1)S(1)} %get-tuple-element.72), channel_id=1, source_target_pairs={{0,128},{64,192},{128,0},{192,64},{1,129},{65,193},{129,1},{193,65... | collective-permute-start | bytes 786440 | tf_op jit(solution)/shard_map/ppermute | solution.py:361
  94.0 11.2 %collective-permute-start.3 = (bf16[256,512]{1,0:T(8,128)(2,1)S(1)}, bf16[256,512]{1,0:T(8,128)(2,1)S(1)}, u32[]{:S(2)}, u32[]{:S(2)}) collective-permute-start(bf16[256,512]{1,0:T(8,128)(2,1)S(1)} %get-tuple-element.73), channel_id=1, source_target_pairs={{0,192},{64,0},{128,64},{192,128},{1,193},{65,1},{129,65},{193,129... | collective-permute-start | bytes 786440 | tf_op jit(solution)/shard_map/ppermute | solution.py:361
  95.2 11.0 %collective-permute-start.4 = (bf16[256,512]{1,0:T(8,128)(2,1)S(1)}, bf16[256,512]{1,0:T(8,128)(2,1)S(1)}, u32[]{:S(2)}, u32[]{:S(2)}) collective-permute-start(bf16[256,512]{1,0:T(8,128)(2,1)S(1)} %get-tuple-element.75), channel_id=1, source_target_pairs={{0,16},{16,32},{32,48},{48,0},{1,17},{17,33},{33,49},{49,1},{2,18}... | collective-permute-start | bytes 786440 | tf_op jit(solution)/shard_map/ppermute | solution.py:361
  96.6 15.8 %collective-permute-start.5 = (bf16[256,512]{1,0:T(8,128)(2,1)S(1)}, bf16[256,512]{1,0:T(8,128)(2,1)S(1)}, u32[]{:S(2)}, u32[]{:S(2)}) collective-permute-start(bf16[256,512]{1,0:T(8,128)(2,1)S(1)} %get-tuple-element.76), channel_id=1, source_target_pairs={{0,32},{16,48},{32,0},{48,16},{1,33},{17,49},{33,1},{49,17},{2,34}... | collective-permute-start | bytes 786440 | tf_op jit(solution)/shard_map/ppermute | solution.py:361
  99.2 13.2 %collective-permute-start.6 = (bf16[256,512]{1,0:T(8,128)(2,1)S(1)}, bf16[256,512]{1,0:T(8,128)(2,1)S(1)}, u32[]{:S(2)}, u32[]{:S(2)}) collective-permute-start(bf16[256,512]{1,0:T(8,128)(2,1)S(1)} %get-tuple-element.77), channel_id=1, source_target_pairs={{0,48},{16,0},{32,16},{48,32},{1,49},{17,1},{33,17},{49,33},{2,50}... | collective-permute-start | bytes 786440 | tf_op jit(solution)/shard_map/ppermute | solution.py:361
  112.8 6.2 %collective-permute-start.10 = (bf16[64,512]{1,0:T(8,128)(2,1)S(1)}, bf16[64,512]{1,0:T(8,128)(2,1)S(1)}, u32[]{:S(2)}, u32[]{:S(2)}) collective-permute-start(bf16[64,512]{1,0:T(8,128)(2,1)S(1)} %get-tuple-element.91), channel_id=1, source_target_pairs={{0,64},{64,128},{128,192},{192,0},{1,65},{65,129},{129,193},{193,1... | collective-permute-start | bytes 196616 | tf_op jit(solution)/shard_map/ppermute | solution.py:361
  113.6 7.3 %collective-permute-start.11 = (bf16[64,512]{1,0:T(8,128)(2,1)S(1)}, bf16[64,512]{1,0:T(8,128)(2,1)S(1)}, u32[]{:S(2)}, u32[]{:S(2)}) collective-permute-start(bf16[64,512]{1,0:T(8,128)(2,1)S(1)} %get-tuple-element.92), channel_id=1, source_target_pairs={{0,128},{64,192},{128,0},{192,64},{1,129},{65,193},{129,1},{193,65... | collective-permute-start | bytes 196616 | tf_op jit(solution)/shard_map/ppermute | solution.py:361
  114.7 6.2 %collective-permute-start.12 = (bf16[64,512]{1,0:T(8,128)(2,1)S(1)}, bf16[64,512]{1,0:T(8,128)(2,1)S(1)}, u32[]{:S(2)}, u32[]{:S(2)}) collective-permute-start(bf16[64,512]{1,0:T(8,128)(2,1)S(1)} %get-tuple-element.93), channel_id=1, source_target_pairs={{0,192},{64,0},{128,64},{192,128},{1,193},{65,1},{129,65},{193,129... | collective-permute-start | bytes 196616 | tf_op jit(solution)/shard_map/ppermute | solution.py:361
  116.1 4.8 %collective-permute-start.7 = (bf16[64,512]{1,0:T(8,128)(2,1)S(1)}, bf16[64,512]{1,0:T(8,128)(2,1)S(1)}, u32[]{:S(2)}, u32[]{:S(2)}) collective-permute-start(bf16[64,512]{1,0:T(8,128)(2,1)S(1)} %get-tuple-element.87), channel_id=1, source_target_pairs={{0,16},{16,32},{32,48},{48,0},{1,17},{17,33},{33,49},{49,1},{2,18}... | collective-permute-start | bytes 196616 | tf_op jit(solution)/shard_map/ppermute | solution.py:361
  116.7 4.7 %collective-permute-start.8 = (bf16[64,512]{1,0:T(8,128)(2,1)S(1)}, bf16[64,512]{1,0:T(8,128)(2,1)S(1)}, u32[]{:S(2)}, u32[]{:S(2)}) collective-permute-start(bf16[64,512]{1,0:T(8,128)(2,1)S(1)} %get-tuple-element.88), channel_id=1, source_target_pairs={{0,32},{16,48},{32,0},{48,16},{1,33},{17,49},{33,1},{49,17},{2,34}... | collective-permute-start | bytes 196616 | tf_op jit(solution)/shard_map/ppermute | solution.py:361
  119.0 3.1 %collective-permute-start.9 = (bf16[64,512]{1,0:T(8,128)(2,1)S(1)}, bf16[64,512]{1,0:T(8,128)(2,1)S(1)}, u32[]{:S(2)}, u32[]{:S(2)}) collective-permute-start(bf16[64,512]{1,0:T(8,128)(2,1)S(1)} %get-tuple-element.89), channel_id=1, source_target_pairs={{0,48},{16,0},{32,16},{48,32},{1,49},{17,1},{33,17},{49,33},{2,50}... | collective-permute-start | bytes 196616 | tf_op jit(solution)/shard_map/ppermute | solution.py:361
  120.9 8.1 %copy-start.4 = (f32[1,128]{1,0:T(1,128)S(1)}, f32[1,128]{1,0:T(1,128)}, u32[]{:S(2)}) copy-start(f32[1,128]{1,0:T(1,128)} %get-tuple-element.99) | copy-start | bytes 1540
  120.9 21.1 %copy-start.2 = (f32[8,1024]{1,0:T(8,128)S(1)}, f32[8,1024]{1,0:T(8,128)}, u32[]{:S(2)}) copy-start(f32[8,1024]{1,0:T(8,128)} %get-tuple-element.97) | copy-start | bytes 98308
  120.9 21.1 %copy-start.3 = (f32[8,1024]{1,0:T(8,128)S(1)}, f32[8,1024]{1,0:T(8,128)}, u32[]{:S(2)}) copy-start(f32[8,1024]{1,0:T(8,128)} %get-tuple-element.98) | copy-start | bytes 98308
  122.8 14.1 %all-to-all-start.2 = ((bf16[8,8,1024]{2,1,0:T(8,128)(2,1)}), bf16[8,8,1024]{2,1,0:T(8,128)(2,1)S(1)}, u32[]{:S(2)}, u32[]{:S(2)}) async-start(bf16[8,8,1024]{2,1,0:T(8,128)(2,1)} %bitcast.6), calls=%async_computation.2 | async-start | bytes 262144 | tf_op jit(solution)/shard_map/all_to_all | solution.py:436
  137.0 5.0 %collective-permute-start.13 = (f32[4,1024]{1,0:T(4,128)S(1)}, f32[4,1024]{1,0:T(4,128)S(1)}, u32[]{:S(2)}, u32[]{:S(2)}) collective-permute-start(f32[4,1024]{1,0:T(4,128)S(1)} %slice_select_fusion), channel_id=1, source_target_pairs={{0,1},{1,0},{2,3},{3,2},{4,5},{5,4},{6,7},{7,6},{8,9},{9,8},{10,11... | collective-permute-start | bytes 49160 | tf_op jit(solution)/shard_map/ppermute | solution.py:439

commit v3 on v2

--- a/solution.py
+++ b/solution.py
@@ -1,3 +1,5 @@
+import functools
+
 import jax
 import jax.numpy as jnp
 from jax import lax
@@ -222,30 +224,45 @@
 
 
 def counts_kernel(
-    wire_hbm, y_hbm, alpha_hbm, turned_hbm, factor_hbm, weight_hbm, local_ref,
-    out_hbm, keep_hbm, give_hbm, total_ref,
-    wire_ref, y_ref, alpha_ref, turned_ref, factor_ref, weight_ref, out_ref,
-    rows_ref, cols_ref, ys_ref, m_ref, in_sem, out_sem,
+    wire_ref, local_ref, y_hbm, alpha_hbm, turned_hbm, factor_hbm, weight_hbm,
+    out_hbm, keep_left, keep_right, give_left, give_right, total_ref,
+    y_ref, alpha_ref, turned_ref, factor_ref, weight_ref, out_ref, ys_ref, m_ref,
+    in_sem, out_sem,
 ):
     pairs = [
-        (wire_hbm, wire_ref), (y_hbm, y_ref), (alpha_hbm, alpha_ref), (turned_hbm, turned_ref),
+        (y_hbm, y_ref), (alpha_hbm, alpha_ref), (turned_hbm, turned_ref),
         (factor_hbm, factor_ref), (weight_hbm, weight_ref),
     ]
     loads = [pltpu.make_async_copy(a, b, in_sem.at[n]) for n, (a, b) in enumerate(pairs)]
     for load in loads:
         load.start()
-    for load in loads[:3]:
-        load.wait()
     core = lax.axis_index("core")
-    keep_rows = pltpu.make_async_copy(rows_ref, keep_hbm, out_sem.at[1])
-    give_rows = pltpu.make_async_copy(rows_ref, give_hbm, out_sem.at[1])
-    keep_cols = pltpu.make_async_copy(cols_ref, keep_hbm, out_sem.at[2])
-    give_cols = pltpu.make_async_copy(cols_ref, give_hbm, out_sem.at[2])
+    half = WIDTH // 2
+
+    def put(own, left, right, at, value):
+        value = value.astype(BF16)
+        rows, lanes = at
+        targets = ((keep_left, keep_right), (give_left, give_right))
+        for choice in range(2):
+
+            @pl.when((core == own) if choice == 0 else (core != own))
+            def _():
+                if left:
+                    targets[choice][0][rows, lanes] = value[:, :half] if right else value
+                if right:
+                    targets[choice][1][rows, lanes] = value[:, half:] if left else value
 
     totals = total_of(wire_ref)
     total_ref[...] = totals
     inverse = [inverse_norm(totals, t) for t in range(STEPS)]
     inv = [to_row(i) for i in inverse]
+
+    def x_of(t):
+        return wire_ref[:, t * PART : (t + 1) * PART, :].reshape(WIDTH, ROWS)
+
+    m_ref[:, :ROWS] = (x_of(0).astype(F32) * inv[0]).astype(BF16)
+    loads[0].wait()
+    loads[1].wait()
     for t in range(STEPS):
         y = alpha_ref[...] if t == 0 else y_ref[t - 1]
         ys_ref[t * ROWS : (t + 1) * ROWS] = (y.astype(F32) * inverse[t]).astype(BF16)
@@ -258,22 +275,11 @@
             ],
             axis=1,
         )
-        cols_ref[b * 256 : (b + 1) * 256, :] = dot(v, ys_ref[...]).astype(BF16)
-
-    @pl.when(core == 0)
-    def _():
-        give_cols.start()
-
-    @pl.when(core == 1)
-    def _():
-        keep_cols.start()
-
-    def x_of(t):
-        return wire_ref[:, t * PART : (t + 1) * PART, :].reshape(WIDTH, ROWS)
-
-    m_ref[:, :ROWS] = (x_of(0).astype(F32) * inv[0]).astype(BF16)
+        at = (slice(b * 256, (b + 1) * 256), slice(0, half))
+        put(1, True, True, at, dot(v, ys_ref[...]))
+
+    loads[2].wait()
     loads[3].wait()
-    loads[4].wait()
     f0, f1, f2 = (factor_ref[t].astype(F32) for t in range(STEPS))
     h = dot(turned_ref[...], jnp.concatenate([x_of(1), x_of(2)], axis=1))
     m_ref[:, ROWS : 2 * ROWS] = (h[:, :ROWS] * f0 * inv[1]).astype(BF16)
@@ -281,41 +287,25 @@
     m_ref[:, 2 * ROWS :] = (h * inv[2]).astype(BF16)
     a = dot(turned_ref[...], h.astype(BF16)) * f2 * (local_ref[...] * inv[2])
     out_ref[...] = a.astype(BF16).reshape(PEERS, PART, ROWS)
-    send = pltpu.make_async_copy(out_ref, out_hbm, out_sem.at[0])
+    send = pltpu.make_async_copy(out_ref, out_hbm, out_sem)
     send.start()
-    loads[5].wait()
-    for b in range(WIDTH // 256):
-        at = slice(b * 256, (b + 1) * 256)
-        rows_ref[:, at] = dot_nt(weight_ref[...], m_ref[at, :]).astype(BF16)
-
-    @pl.when(core == 0)
-    def _():
-        keep_rows.start()
-        keep_rows.wait()
-        give_cols.wait()
-
-    @pl.when(core == 1)
-    def _():
-        give_rows.start()
-        give_rows.wait()
-        keep_cols.wait()
-
+    loads[4].wait()
+    for b in range(4):
+        value = dot_nt(weight_ref[...], m_ref[b * 256 : (b + 1) * 256, :])
+        at = (slice(0, WIDTH), slice((b & 1) * 256, (b & 1) * 256 + 256))
+        put(0, b < 2, b >= 2, at, value)
     send.wait()
 
 
-def pair_kernel(keep_ref, got_ref, *outs):
-    half = WIDTH // 2
-    x, y = lax.axis_index("dp"), lax.axis_index("y")
-
-    def piece(at, lanes):
-        return (keep_ref[at, lanes].astype(F32) + got_ref[at, lanes].astype(F32)).astype(BF16)
-
+def pair_kernel(axis, keep_ref, got_ref, *outs):
+    me = lax.axis_index(axis)
     for d in range(4):
-        at = pl.ds(pl.multiple_of(((x + d) & 3) * 256, 256), 256)
-        outs[d][...] = piece(at, slice(0, half))
+        to = (me + d) & 3
         for b in range(4):
-            at = pl.ds(pl.multiple_of(b * 256 + ((y + d) & 3) * 64, 64), 64)
-            outs[4 + d][b * 64 : (b + 1) * 64, :] = piece(at, slice(half, WIDTH))
+            row = to * 256 + b * 64 if axis == "dp" else b * 256 + to * 64
+            at = pl.ds(pl.multiple_of(row, 64), 64)
+            total = keep_ref[at, :].astype(F32) + got_ref[at, :].astype(F32)
+            outs[d][b * 64 : (b + 1) * 64, :] = total.astype(BF16)
 
 
 def plane_kernel(*refs):
@@ -364,6 +354,10 @@
 def spread_out(pieces, axis):
     far, right, left = (ring(pieces[d], axis, d) for d in (2, 1, 3))
     return [pieces[0], right, far, left]
+
+
+def in_hbm(*arrays):
+    return [pltpu.with_memory_space_constraint(v, pltpu.HBM) for v in arrays]
 
 
 def on_device(alpha_init, tokens, trans_rows, trans_cols, emit_rows, emit_cols, backward):
@@ -402,38 +396,39 @@
     )(tok, trans_rows, trans_cols, emit_rows, emit_cols, back)
 
     a_shape = (PEERS, PART, ROWS)
-    a_wire, keep, give, total = call(
+    vmem = pl.BlockSpec(memory_space=pltpu.VMEM)
+    a_wire, *ends, total = call(
         counts_kernel, "counts",
-        [(a_shape, BF16), (square, BF16), (square, BF16), ((1, 128), F32)],
+        [(a_shape, BF16), *[((WIDTH, half), BF16)] * 4, ((1, 128), F32)],
         [
-            (wire_shape, BF16), (y_shape, BF16), ((ROWS, WIDTH), BF16), (square, BF16),
+            (y_shape, BF16), ((ROWS, WIDTH), BF16), (square, BF16),
             ((STEPS, WIDTH, ROWS), BF16), ((WIDTH, STEPS * ROWS), BF16), (a_shape, BF16),
-            (square, BF16), (square, BF16), ((STEPS * ROWS, WIDTH), BF16),
-            ((WIDTH, STEPS * ROWS), BF16), pltpu.SemaphoreType.DMA((6,)),
-            pltpu.SemaphoreType.DMA((3,)),
+            ((STEPS * ROWS, WIDTH), BF16), ((WIDTH, STEPS * ROWS), BF16),
+            pltpu.SemaphoreType.DMA((5,)), pltpu.SemaphoreType.DMA(()),
         ],
-        limit=ALONE,
-        specs=dict(
-            in_specs=[hbm] * 6 + [pl.BlockSpec(memory_space=pltpu.VMEM)],
-            out_specs=[hbm] * 3 + [pl.BlockSpec(memory_space=pltpu.VMEM)],
-        ),
-    )(got, y, alpha, turned, factor, weight, local)
+        limit=40 * 2**20,
+        specs=dict(in_specs=[vmem] * 2 + [hbm] * 5, out_specs=[hbm] + [vmem] * 5),
+    )(got, local, *in_hbm(y, alpha, turned, factor, weight))
+    keep, give = ends[:2], ends[2:]
 
     core = lax.axis_index("core")
     swap_cores = [(0, 1), (1, 0)]
-    pieces = call(pair_kernel, "pair", [((256, half), BF16)] * 8)(
-        keep, lax.ppermute(give, "core", swap_cores)
-    )
-    a_wire, *pieces = lax.optimization_barrier((a_wire, *pieces))
-    parts = spread_out(pieces[:4], "dp") + spread_out(pieces[4:], "y")
+    parts = []
+    for n, axis in enumerate(("dp", "y")):
+        got_half = lax.ppermute(give[n], "core", swap_cores)
+        pieces = call(functools.partial(pair_kernel, axis), "pair_" + axis, [((256, half), BF16)] * 4)(
+            keep[n], got_half
+        )
+        parts += spread_out(pieces, axis)
+    a_wire, parts[1] = lax.optimization_barrier((a_wire, parts[1]))
     a_got = lax.all_to_all(a_wire, state, 0, 0, tiled=True)
     pieces = call(plane_kernel, "plane", [((64, half), BF16)] * 8, [((256, half), F32)])(*parts)
-    a_got, *pieces = lax.optimization_barrier((a_got, *pieces))
     parts = spread_out(pieces[:4], "y") + spread_out(pieces[4:], "dp")
     (part,) = call(line_kernel, "line", [((64, WIDTH), BF16)])(*parts)
     (alpha_final,) = call(final_kernel, "final", [((ROWS, WIDTH), BF16)])(a_got)
-    part, alpha_final = lax.optimization_barrier((part, alpha_final))
     part = lax.all_to_all(part.reshape(8, 8, WIDTH), "z", 0, 0, tiled=True)
+    loglik = jnp.log(total[0, 2 : 3 * SEQ_DEV : 3] / (WIDTH * WIDTH))
+    part, alpha_final, loglik = lax.optimization_barrier((part, alpha_final, loglik))
     part = jnp.sum(part.astype(F32), axis=0)
     mine = jnp.where(core == 0, part[:4], part[4:])
     other = lax.ppermute(jnp.where(core == 0, part[4:], part[:4]), "core", swap_cores)
@@ -441,7 +436,6 @@
     counts_rows = jnp.where(core == 0, mine, other) * take_rows[:4] * scale
     counts_cols = jnp.where(core == 0, other, mine) * take_cols[:4] * scale
 
-    loglik = jnp.log(total[0, 2 : 3 * SEQ_DEV : 3] / (WIDTH * WIDTH))
     return (
         alpha_final.reshape(SEQ_DEV, PART, WIDTH),
         counts_rows.T,

time: 143 us -> 131 us (0.916)
  waiting for transfers between devices: 61.2 us -> 52.1 us
  starting transfers between devices: 46.8 us -> 45.3 us
    ppermute x12, waiting for transfers between devices: 13.3 us -> 7.79 us  [ring(): return lax.ppermute(x, axis, [(i, (i + d) % n) for i in range(n)])]
    all_to_all x1, starting transfers between devices: 6.14 us -> 3.5 us  [on_device(): part = lax.all_to_all(part.reshape(8, 8, WIDTH), 'z', 0, 0, tiled=True)]
    ppermute x1 -> x2, waiting for transfers between devices: 4.32 us -> 2.15 us  [on_device(): got_half = lax.ppermute(give[n], 'core', swap_cores)]
    all_to_all x1, waiting for transfers between devices: 7.88 us -> 5.99 us  [on_device(): part = lax.all_to_all(part.reshape(8, 8, WIDTH), 'z', 0, 0, tiled=True)]
    pallas_call x2 -> x3, Pallas kernels: 11.3 us -> 10.1 us  [the longest x1 9.64 us: on_device(): call(counts_kernel, 'counts', [(a_shape, BF16), *[((WIDTH, half), BF16)]...]
  transfers between devices with their start and end apart: 17 -> 18, of which waited for: 10 -> 9; matrix products, arithmetic and copies ran while one was open for 0% -> 0% of each run, Pallas kernels for 6% -> 8%
where the time goes in v3:
time: 131 us
  waiting for transfers between devices  52.1 us (40%)
  starting transfers between devices  45.3 us (35%)
  Pallas kernels  28.8 us (22%)
  local copies, waits for them, and re-layouts  2.4 us (2%)
    all_to_all x1, waiting for transfers between devices, on_device(): got = lax.all_to_all(wire, state, 0, 0, tiled=True)  35.4 us
    ppermute x12, starting transfers between devices, ring(): return lax.ppermute(x, axis, [(i, (i + d) % n) for i in range(n)])  16.7 us
    all_to_all x1, starting transfers between devices, on_device(): got = lax.all_to_all(wire, state, 0, 0, tiled=True)  13.2 us
    pallas_call x1, Pallas kernels, on_device(): call(counts_kernel, 'counts', [(a_shape, BF16), *[((WIDTH, half), BF16)]...  9.64 us
    pallas_call x1, Pallas kernels, on_device(): call(send_kernel, 'send', [(wire_shape, BF16), (y_shape, BF16)], [((ROWS,...  8.93 us
    ppermute x12, waiting for transfers between devices, ring(): return lax.ppermute(x, axis, [(i, (i + d) % n) for i in range(n)])  7.79 us
    all_to_all x1, starting transfers between devices, on_device(): a_got = lax.all_to_all(a_wire, state, 0, 0, tiled=True)  7.31 us
    pallas_call x1, Pallas kernels, on_device(): call(local_kernel, 'local', [((WIDTH, STEPS * ROWS), BF16), (square, BF16...  7.25 us
  transfers between devices with their start and end apart: 18, of which 9 were waited for; matrix products, arithmetic and copies ran while one was open for 0% of the time, Pallas kernels for 8%

profile of v3, /device:TPU:1, one launch (start us, length us, event | category | flops | bytes accessed | tf_op | source)
XLA Modules:
  0.0 130.5 jit_solution(6739651979393620837)
XLA Ops:
  0.6 8.9 %send.1 = (bf16[64,104,128]{2,1,0:T(8,128)(2,1)}, bf16[2,128,1024]{2,1,0:T(8,128)(2,1)}) custom-call(s32[3,8]{1,0:T(4,128)} %bitcast.17, bf16[128,1024]{1,0:T(8,128)(2,1)} %bitcast.15, bf16[1024,1024]{1,0:T(8,128)(2,1)} %rows_ref.1, bf16[1024,1024]{1,0:T(8,128)(2,1)} %cols_ref.1, bf16[512,1024]{1,0:T(8,128)(2,1)} %emit_rows_ref.1, ...), custom_call_target="tpu_custom_call" | custom-call | flops 1000000000 | bytes 8000000 | tf_op jit(solution)/shard_map/send/pallas_call | solution.py:373
  9.6 13.2 %all-to-all-start = ((bf16[64,104,128]{2,1,0:T(8,128)(2,1)}), bf16[64,104,128]{2,1,0:T(8,128)(2,1)S(1)}, u32[]{:S(2)}, u32[]{:S(2)}) async-start(bf16[64,104,128]{2,1,0:T(8,128)(2,1)} %get-tuple-element.39), calls=%async_computation | async-start | bytes 3407872 | tf_op jit(solution)/shard_map/all_to_all | solution.py:387
  22.7 7.3 %local.1 = (bf16[1024,384]{1,0:T(8,128)(2,1)}, bf16[1024,1024]{1,0:T(8,128)(2,1)}, bf16[3,1024,128]{2,1,0:T(8,128)(2,1)}, f32[1,128]{1,0:T(1,128)}, f32[8,1024]{1,0:T(8,128)}, /*index=5*/f32[8,1024]{1,0:T(8,128)}) custom-call(s32[3,8]{1,0:T(4,128)} %bitcast.18, bf16[1024,1024]{1,0:T(8,128)(2,1)} %rows_ref.1, bf16[1024,1024]{1,0:T(8,128)(2,1)} %cols_ref.1, ...), custom_call_target="tpu_custom_call" | custom-call | flops 1000000000 | bytes 8000000 | tf_op jit(solution)/shard_map/local/pallas_call | solution.py:389
  30.0 35.4 %all-to-all-done.wire_ref = bf16[64,104,128]{2,1,0:T(8,128)(2,1)S(1)} async-done(((bf16[64,104,128]{2,1,0:T(8,128)(2,1)}), bf16[64,104,128]{2,1,0:T(8,128)(2,1)S(1)}, u32[]{:S(2)}, u32[]{:S(2)}) %all-to-all-start) | async-done | bytes 1703968 | tf_op jit(solution)/shard_map/all_to_all | solution.py:387
  66.0 9.6 %counts.1 = (bf16[64,16,128]{2,1,0:T(8,128)(2,1)}, bf16[1024,512]{1,0:T(8,128)(2,1)S(1)}, bf16[1024,512]{1,0:T(8,128)(2,1)S(1)}, bf16[1024,512]{1,0:T(8,128)(2,1...) custom-call(bf16[64,104,128]{2,1,0:T(8,128)(2,1)S(1)} %all-to-all-done.wire_ref, f32[1,128]{1,0:T(1,128)S(1)} %copy-done, ...), custom_call_target="tpu_custom_call" | custom-call | flops 1000000000 | bytes 8000000 | tf_op jit(solution)/shard_map/counts/pallas_call | solution.py:400
  76.2 2.1 %collective-permute-done.got_ref = bf16[1024,512]{1,0:T(8,128)(2,1)S(1)} collective-permute-done((bf16[1024,512]{1,0:T(8,128)(2,1)S(1)}, bf16[1024,512]{1,0:T(8,128)(2,1)S(1)}, u32[]{:S(2)}, u32[]{:S(2)}) %collective-permute-start) | collective-permute-done | bytes 1048608 | tf_op jit(solution)/shard_map/ppermute | solution.py:418
  78.6 1.3 collective-permute-start.1
  80.9 1.2 collective-permute-start.5
  82.1 2.6 %collective-permute-start.6 = (bf16[256,512]{1,0:T(8,128)(2,1)S(1)}, bf16[256,512]{1,0:T(8,128)(2,1)S(1)}, u32[]{:S(2)}, u32[]{:S(2)}) collective-permute-start(bf16[256,512]{1,0:T(8,128)(2,1)S(1)} %get-tuple-element.57), channel_id=1, source_target_pairs={{0,32},{16,48},{32,0},{48,16},{1,33},{17,49},{33,1},{49,17},{2,34}... | collective-permute-start | bytes 786440 | tf_op jit(solution)/shard_map/ppermute | solution.py:351
  84.7 1.1 collective-permute-start.7
  85.8 2.7 %collective-permute-start.2 = (bf16[256,512]{1,0:T(8,128)(2,1)S(1)}, bf16[256,512]{1,0:T(8,128)(2,1)S(1)}, u32[]{:S(2)}, u32[]{:S(2)}) collective-permute-start(bf16[256,512]{1,0:T(8,128)(2,1)S(1)} %get-tuple-element.51), channel_id=1, source_target_pairs={{0,128},{64,192},{128,0},{192,64},{1,129},{65,193},{129,1},{193,65... | collective-permute-start | bytes 786440 | tf_op jit(solution)/shard_map/ppermute | solution.py:351
  88.5 0.9 collective-permute-start.3
  89.4 7.3 %all-to-all-start.2 = ((bf16[64,16,128]{2,1,0:T(8,128)(2,1)}), bf16[64,16,128]{2,1,0:T(8,128)(2,1)S(1)}, u32[]{:S(2)}, u32[]{:S(2)}) async-start(bf16[64,16,128]{2,1,0:T(8,128)(2,1)} %get-tuple-element.67), calls=%async_computation.2 | async-start | bytes 524288 | tf_op jit(solution)/shard_map/all_to_all | solution.py:424
  96.8 3.4 %collective-permute-done.3.refs_3_ = bf16[256,512]{1,0:T(8,128)(2,1)S(1)} collective-permute-done((bf16[256,512]{1,0:T(8,128)(2,1)S(1)}, bf16[256,512]{1,0:T(8,128)(2,1)S(1)}, u32[]{:S(2)}, u32[]{:S(2)}) %collective-permute-start.3) | collective-permute-done | bytes 262176 | tf_op jit(solution)/shard_map/ppermute | solution.py:351
  100.2 0.9 copy-done.2
  101.7 2.3 %collective-permute-start.11 = (bf16[64,512]{1,0:T(8,128)(2,1)S(1)}, bf16[64,512]{1,0:T(8,128)(2,1)S(1)}, u32[]{:S(2)}, u32[]{:S(2)}) collective-permute-start(bf16[64,512]{1,0:T(8,128)(2,1)S(1)} %get-tuple-element.64), channel_id=1, source_target_pairs={{0,64},{64,128},{128,192},{192,0},{1,65},{65,129},{129,193},{193,1... | collective-permute-start | bytes 196616 | tf_op jit(solution)/shard_map/ppermute | solution.py:351
  103.9 2.4 %collective-permute-start.12 = (bf16[64,512]{1,0:T(8,128)(2,1)S(1)}, bf16[64,512]{1,0:T(8,128)(2,1)S(1)}, u32[]{:S(2)}, u32[]{:S(2)}) collective-permute-start(bf16[64,512]{1,0:T(8,128)(2,1)S(1)} %get-tuple-element.65), channel_id=1, source_target_pairs={{0,128},{64,192},{128,0},{192,64},{1,129},{65,193},{129,1},{193,65... | collective-permute-start | bytes 196616 | tf_op jit(solution)/shard_map/ppermute | solution.py:351
  106.4 1.3 %collective-permute-start.8 = (bf16[64,512]{1,0:T(8,128)(2,1)S(1)}, bf16[64,512]{1,0:T(8,128)(2,1)S(1)}, u32[]{:S(2)}, u32[]{:S(2)}) collective-permute-start(bf16[64,512]{1,0:T(8,128)(2,1)S(1)} %get-tuple-element.60), channel_id=1, source_target_pairs={{0,16},{16,32},{32,48},{48,0},{1,17},{17,33},{33,49},{49,1},{2,18}... | collective-permute-start | bytes 196616 | tf_op jit(solution)/shard_map/ppermute | solution.py:351
  108.9 1.2 collective-permute-done.13.refs_7_
  110.7 2.2 %collective-permute-done.9.refs_2_ = bf16[64,512]{1,0:T(8,128)(2,1)S(1)} collective-permute-done((bf16[64,512]{1,0:T(8,128)(2,1)S(1)}, bf16[64,512]{1,0:T(8,128)(2,1)S(1)}, u32[]{:S(2)}, u32[]{:S(2)}) %collective-permute-start.9) | collective-permute-done | bytes 65568 | tf_op jit(solution)/shard_map/ppermute | solution.py:351
  113.7 3.5 %all-to-all-start.1 = ((bf16[8,8,1024]{2,1,0:T(8,128)(2,1)}), bf16[8,8,1024]{2,1,0:T(8,128)(2,1)S(1)}, u32[]{:S(2)}, u32[]{:S(2)}) async-start(bf16[8,8,1024]{2,1,0:T(8,128)(2,1)} %bitcast.5), calls=%async_computation.1 | async-start | bytes 262144 | tf_op jit(solution)/shard_map/all_to_all | solution.py:429
  117.7 1.3 %final.1 = bf16[128,1024]{1,0:T(8,128)(2,1)} custom-call(bf16[64,16,128]{2,1,0:T(8,128)(2,1)S(1)} %all-to-all-done.2.wire_ref), custom_call_target="tpu_custom_call" | custom-call | flops 1000000000 | bytes 8000000 | tf_op jit(solution)/shard_map/final/pallas_call | solution.py:428
  119.1 6.0 %all-to-all-done.1 = bf16[8,8,1024]{2,1,0:T(8,128)(2,1)S(1)} async-done(((bf16[8,8,1024]{2,1,0:T(8,128)(2,1)}), bf16[8,8,1024]{2,1,0:T(8,128)(2,1)S(1)}, u32[]{:S(2)}, u32[]{:S(2)}) %all-to-all-start.1) | async-done | bytes 131104 | tf_op jit(solution)/shard_map/all_to_all | solution.py:429
  125.1 3.9 %collective-permute-start.14 = (f32[4,1024]{1,0:T(4,128)S(1)}, f32[4,1024]{1,0:T(4,128)S(1)}, u32[]{:S(2)}, u32[]{:S(2)}) collective-permute-start(f32[4,1024]{1,0:T(4,128)S(1)} %slice_select_fusion), channel_id=1, source_target_pairs={{0,1},{1,0},{2,3},{3,2},{4,5},{5,4},{6,7},{7,6},{8,9},{9,8},{10,11... | collective-permute-start | bytes 49160 | tf_op jit(solution)/shard_map/ppermute | solution.py:434
  (35 shorter events, 7.7 us)
Async XLA Ops:
  9.6 55.8 %all-to-all-start = ((bf16[64,104,128]{2,1,0:T(8,128)(2,1)}), bf16[64,104,128]{2,1,0:T(8,128)(2,1)S(1)}, u32[]{:S(2)}, u32[]{:S(2)}) async-start(bf16[64,104,128]{2,1,0:T(8,128)(2,1)} %get-tuple-element.39), calls=%async_computation | async-start | bytes 3407872 | tf_op jit(solution)/shard_map/all_to_all | solution.py:387
  65.4 0.7 copy-start
  75.7 2.7 %collective-permute-start = (bf16[1024,512]{1,0:T(8,128)(2,1)S(1)}, bf16[1024,512]{1,0:T(8,128)(2,1)S(1)}, u32[]{:S(2)}, u32[]{:S(2)}) collective-permute-start(bf16[1024,512]{1,0:T(8,128)(2,1)S(1)} %get-tuple-element.46), channel_id=1, source_target_pairs={{0,1},{1,0},{2,3},{3,2},{4,5},{5,4},{6,7},{7,6},{8,9},{9,8},{10,11... | collective-permute-start | bytes 3145736 | tf_op jit(solution)/shard_map/ppermute | solution.py:418
  75.8 4.1 %collective-permute-start.4 = (bf16[1024,512]{1,0:T(8,128)(2,1)S(1)}, bf16[1024,512]{1,0:T(8,128)(2,1)S(1)}, u32[]{:S(2)}, u32[]{:S(2)}) collective-permute-start(bf16[1024,512]{1,0:T(8,128)(2,1)S(1)} %get-tuple-element.54), channel_id=1, source_target_pairs={{0,1},{1,0},{2,3},{3,2},{4,5},{5,4},{6,7},{7,6},{8,9},{9,8},{10,11... | collective-permute-start | bytes 3145736 | tf_op jit(solution)/shard_map/ppermute | solution.py:418
  78.6 9.9 %collective-permute-start.1 = (bf16[256,512]{1,0:T(8,128)(2,1)S(1)}, bf16[256,512]{1,0:T(8,128)(2,1)S(1)}, u32[]{:S(2)}, u32[]{:S(2)}) collective-permute-start(bf16[256,512]{1,0:T(8,128)(2,1)S(1)} %get-tuple-element.49), channel_id=1, source_target_pairs={{0,64},{64,128},{128,192},{192,0},{1,65},{65,129},{129,193},{193,1... | collective-permute-start | bytes 786440 | tf_op jit(solution)/shard_map/ppermute | solution.py:351
  80.2 0.7 copy-start.1
  80.9 15.8 %collective-permute-start.5 = (bf16[256,512]{1,0:T(8,128)(2,1)S(1)}, bf16[256,512]{1,0:T(8,128)(2,1)S(1)}, u32[]{:S(2)}, u32[]{:S(2)}) collective-permute-start(bf16[256,512]{1,0:T(8,128)(2,1)S(1)} %get-tuple-element.56), channel_id=1, source_target_pairs={{0,16},{16,32},{32,48},{48,0},{1,17},{17,33},{33,49},{49,1},{2,18}... | collective-permute-start | bytes 786440 | tf_op jit(solution)/shard_map/ppermute | solution.py:351
  82.1 14.6 %collective-permute-start.6 = (bf16[256,512]{1,0:T(8,128)(2,1)S(1)}, bf16[256,512]{1,0:T(8,128)(2,1)S(1)}, u32[]{:S(2)}, u32[]{:S(2)}) collective-permute-start(bf16[256,512]{1,0:T(8,128)(2,1)S(1)} %get-tuple-element.57), channel_id=1, source_target_pairs={{0,32},{16,48},{32,0},{48,16},{1,33},{17,49},{33,1},{49,17},{2,34}... | collective-permute-start | bytes 786440 | tf_op jit(solution)/shard_map/ppermute | solution.py:351
  84.7 12.0 %collective-permute-start.7 = (bf16[256,512]{1,0:T(8,128)(2,1)S(1)}, bf16[256,512]{1,0:T(8,128)(2,1)S(1)}, u32[]{:S(2)}, u32[]{:S(2)}) collective-permute-start(bf16[256,512]{1,0:T(8,128)(2,1)S(1)} %get-tuple-element.58), channel_id=1, source_target_pairs={{0,48},{16,0},{32,16},{48,32},{1,49},{17,1},{33,17},{49,33},{2,50}... | collective-permute-start | bytes 786440 | tf_op jit(solution)/shard_map/ppermute | solution.py:351
  85.8 11.0 %collective-permute-start.2 = (bf16[256,512]{1,0:T(8,128)(2,1)S(1)}, bf16[256,512]{1,0:T(8,128)(2,1)S(1)}, u32[]{:S(2)}, u32[]{:S(2)}) collective-permute-start(bf16[256,512]{1,0:T(8,128)(2,1)S(1)} %get-tuple-element.51), channel_id=1, source_target_pairs={{0,128},{64,192},{128,0},{192,64},{1,129},{65,193},{129,1},{193,65... | collective-permute-start | bytes 786440 | tf_op jit(solution)/shard_map/ppermute | solution.py:351
  88.5 11.7 %collective-permute-start.3 = (bf16[256,512]{1,0:T(8,128)(2,1)S(1)}, bf16[256,512]{1,0:T(8,128)(2,1)S(1)}, u32[]{:S(2)}, u32[]{:S(2)}) collective-permute-start(bf16[256,512]{1,0:T(8,128)(2,1)S(1)} %get-tuple-element.52), channel_id=1, source_target_pairs={{0,192},{64,0},{128,64},{192,128},{1,193},{65,1},{129,65},{193,129... | collective-permute-start | bytes 786440 | tf_op jit(solution)/shard_map/ppermute | solution.py:351
  89.4 24.3 %all-to-all-start.2 = ((bf16[64,16,128]{2,1,0:T(8,128)(2,1)}), bf16[64,16,128]{2,1,0:T(8,128)(2,1)S(1)}, u32[]{:S(2)}, u32[]{:S(2)}) async-start(bf16[64,16,128]{2,1,0:T(8,128)(2,1)} %get-tuple-element.67), calls=%async_computation.2 | async-start | bytes 524288 | tf_op jit(solution)/shard_map/all_to_all | solution.py:424
  100.2 0.9 copy-start.2
  101.6 6.1 %collective-permute-start.10 = (bf16[64,512]{1,0:T(8,128)(2,1)S(1)}, bf16[64,512]{1,0:T(8,128)(2,1)S(1)}, u32[]{:S(2)}, u32[]{:S(2)}) collective-permute-start(bf16[64,512]{1,0:T(8,128)(2,1)S(1)} %get-tuple-element.62), channel_id=1, source_target_pairs={{0,48},{16,0},{32,16},{48,32},{1,49},{17,1},{33,17},{49,33},{2,50}... | collective-permute-start | bytes 196616 | tf_op jit(solution)/shard_map/ppermute | solution.py:351
  101.7 7.0 %collective-permute-start.11 = (bf16[64,512]{1,0:T(8,128)(2,1)S(1)}, bf16[64,512]{1,0:T(8,128)(2,1)S(1)}, u32[]{:S(2)}, u32[]{:S(2)}) collective-permute-start(bf16[64,512]{1,0:T(8,128)(2,1)S(1)} %get-tuple-element.64), channel_id=1, source_target_pairs={{0,64},{64,128},{128,192},{192,0},{1,65},{65,129},{129,193},{193,1... | collective-permute-start | bytes 196616 | tf_op jit(solution)/shard_map/ppermute | solution.py:351
  103.9 5.0 %collective-permute-start.12 = (bf16[64,512]{1,0:T(8,128)(2,1)S(1)}, bf16[64,512]{1,0:T(8,128)(2,1)S(1)}, u32[]{:S(2)}, u32[]{:S(2)}) collective-permute-start(bf16[64,512]{1,0:T(8,128)(2,1)S(1)} %get-tuple-element.65), channel_id=1, source_target_pairs={{0,128},{64,192},{128,0},{192,64},{1,129},{65,193},{129,1},{193,65... | collective-permute-start | bytes 196616 | tf_op jit(solution)/shard_map/ppermute | solution.py:351
  106.3 3.8 %collective-permute-start.13 = (bf16[64,512]{1,0:T(8,128)(2,1)S(1)}, bf16[64,512]{1,0:T(8,128)(2,1)S(1)}, u32[]{:S(2)}, u32[]{:S(2)}) collective-permute-start(bf16[64,512]{1,0:T(8,128)(2,1)S(1)} %get-tuple-element.66), channel_id=1, source_target_pairs={{0,192},{64,0},{128,64},{192,128},{1,193},{65,1},{129,65},{193,129... | collective-permute-start | bytes 196616 | tf_op jit(solution)/shard_map/ppermute | solution.py:351
  106.4 4.3 %collective-permute-start.8 = (bf16[64,512]{1,0:T(8,128)(2,1)S(1)}, bf16[64,512]{1,0:T(8,128)(2,1)S(1)}, u32[]{:S(2)}, u32[]{:S(2)}) collective-permute-start(bf16[64,512]{1,0:T(8,128)(2,1)S(1)} %get-tuple-element.60), channel_id=1, source_target_pairs={{0,16},{16,32},{32,48},{48,0},{1,17},{17,33},{33,49},{49,1},{2,18}... | collective-permute-start | bytes 196616 | tf_op jit(solution)/shard_map/ppermute | solution.py:351
  107.7 5.3 %collective-permute-start.9 = (bf16[64,512]{1,0:T(8,128)(2,1)S(1)}, bf16[64,512]{1,0:T(8,128)(2,1)S(1)}, u32[]{:S(2)}, u32[]{:S(2)}) collective-permute-start(bf16[64,512]{1,0:T(8,128)(2,1)S(1)} %get-tuple-element.61), channel_id=1, source_target_pairs={{0,32},{16,48},{32,0},{48,16},{1,33},{17,49},{33,1},{49,17},{2,34}... | collective-permute-start | bytes 196616 | tf_op jit(solution)/shard_map/ppermute | solution.py:351
  113.7 16.2 %copy-start.3 = (f32[8,1024]{1,0:T(8,128)S(1)}, f32[8,1024]{1,0:T(8,128)}, u32[]{:S(2)}) copy-start(f32[8,1024]{1,0:T(8,128)} %get-tuple-element.71) | copy-start | bytes 98308
  113.7 16.2 %copy-start.4 = (f32[8,1024]{1,0:T(8,128)S(1)}, f32[8,1024]{1,0:T(8,128)}, u32[]{:S(2)}) copy-start(f32[8,1024]{1,0:T(8,128)} %get-tuple-element.72) | copy-start | bytes 98308
  113.7 11.3 %all-to-all-start.1 = ((bf16[8,8,1024]{2,1,0:T(8,128)(2,1)}), bf16[8,8,1024]{2,1,0:T(8,128)(2,1)S(1)}, u32[]{:S(2)}, u32[]{:S(2)}) async-start(bf16[8,8,1024]{2,1,0:T(8,128)(2,1)} %bitcast.5), calls=%async_computation.1 | async-start | bytes 262144 | tf_op jit(solution)/shard_map/all_to_all | solution.py:429
  125.1 4.8 %collective-permute-start.14 = (f32[4,1024]{1,0:T(4,128)S(1)}, f32[4,1024]{1,0:T(4,128)S(1)}, u32[]{:S(2)}, u32[]{:S(2)}) collective-permute-start(f32[4,1024]{1,0:T(4,128)S(1)} %slice_select_fusion), channel_id=1, source_target_pairs={{0,1},{1,0},{2,3},{3,2},{4,5},{5,4},{6,7},{7,6},{8,9},{9,8},{10,11... | collective-permute-start | bytes 49160 | tf_op jit(solution)/shard_map/ppermute | solution.py:434

commit v4 on v3

--- a/solution.py
+++ b/solution.py
@@ -1,5 +1,3 @@
-import functools
-
 import jax
 import jax.numpy as jnp
 from jax import lax
@@ -224,14 +222,14 @@
 
 
 def counts_kernel(
-    wire_ref, local_ref, y_hbm, alpha_hbm, turned_hbm, factor_hbm, weight_hbm,
-    out_hbm, keep_left, keep_right, give_left, give_right, total_ref,
-    y_ref, alpha_ref, turned_ref, factor_ref, weight_ref, out_ref, ys_ref, m_ref,
+    wire_ref, y_hbm, alpha_hbm, turned_hbm, factor_hbm, local_hbm, weight_hbm,
+    out_hbm, keep_ref, give_ref, total_ref,
+    y_ref, alpha_ref, turned_ref, factor_ref, local_ref, weight_ref, out_ref, ys_ref, m_ref,
     in_sem, out_sem,
 ):
     pairs = [
         (y_hbm, y_ref), (alpha_hbm, alpha_ref), (turned_hbm, turned_ref),
-        (factor_hbm, factor_ref), (weight_hbm, weight_ref),
+        (factor_hbm, factor_ref), (local_hbm, local_ref), (weight_hbm, weight_ref),
     ]
     loads = [pltpu.make_async_copy(a, b, in_sem.at[n]) for n, (a, b) in enumerate(pairs)]
     for load in loads:
@@ -239,18 +237,14 @@
     core = lax.axis_index("core")
     half = WIDTH // 2
 
-    def put(own, left, right, at, value):
-        value = value.astype(BF16)
-        rows, lanes = at
-        targets = ((keep_left, keep_right), (give_left, give_right))
-        for choice in range(2):
-
-            @pl.when((core == own) if choice == 0 else (core != own))
-            def _():
-                if left:
-                    targets[choice][0][rows, lanes] = value[:, :half] if right else value
-                if right:
-                    targets[choice][1][rows, lanes] = value[:, half:] if left else value
+    def put(term, side, rows, lanes, value):
+        @pl.when(core == side)
+        def _():
+            keep_ref[term, rows, lanes] = value.astype(BF16)
+
+        @pl.when(core != side)
+        def _():
+            give_ref[term, rows, lanes] = value.astype(BF16)
 
     totals = total_of(wire_ref)
     total_ref[...] = totals
@@ -275,11 +269,14 @@
             ],
             axis=1,
         )
-        at = (slice(b * 256, (b + 1) * 256), slice(0, half))
-        put(1, True, True, at, dot(v, ys_ref[...]))
+        value = dot(v, ys_ref[...])
+        for side in range(2):
+            part = value[:, side * half : (side + 1) * half]
+            put(1, side, slice(b * 256, (b + 1) * 256), slice(0, half), part)
 
     loads[2].wait()
     loads[3].wait()
+    loads[4].wait()
     f0, f1, f2 = (factor_ref[t].astype(F32) for t in range(STEPS))
     h = dot(turned_ref[...], jnp.concatenate([x_of(1), x_of(2)], axis=1))
     m_ref[:, ROWS : 2 * ROWS] = (h[:, :ROWS] * f0 * inv[1]).astype(BF16)
@@ -289,43 +286,54 @@
     out_ref[...] = a.astype(BF16).reshape(PEERS, PART, ROWS)
     send = pltpu.make_async_copy(out_ref, out_hbm, out_sem)
     send.start()
-    loads[4].wait()
+    loads[5].wait()
     for b in range(4):
         value = dot_nt(weight_ref[...], m_ref[b * 256 : (b + 1) * 256, :])
-        at = (slice(0, WIDTH), slice((b & 1) * 256, (b & 1) * 256 + 256))
-        put(0, b < 2, b >= 2, at, value)
+        put(0, b // 2, slice(0, WIDTH), slice((b & 1) * 256, (b & 1) * 256 + 256), value)
     send.wait()
 
 
-def pair_kernel(axis, keep_ref, got_ref, *outs):
-    me = lax.axis_index(axis)
-    for d in range(4):
+def place(turn):
+    x, y = lax.axis_index("dp"), lax.axis_index("y")
+    return jnp.where((lax.axis_index("core") == 0) != turn, x, y)
+
+
+def pair_kernel(keep_ref, got_ref, own_hbm, *refs):
+    outs, own_ref, sem = [refs[3], *refs[:3]], refs[3], refs[4]
+    along_dp = lax.axis_index("core") == 0
+    me = place(False)
+    for d in (2, 1, 3, 0):
         to = (me + d) & 3
         for b in range(4):
-            row = to * 256 + b * 64 if axis == "dp" else b * 256 + to * 64
+            row = jnp.where(along_dp, to * 256 + b * 64, b * 256 + to * 64)
             at = pl.ds(pl.multiple_of(row, 64), 64)
-            total = keep_ref[at, :].astype(F32) + got_ref[at, :].astype(F32)
-            outs[d][b * 64 : (b + 1) * 64, :] = total.astype(BF16)
-
-
-def plane_kernel(*refs):
-    ins, outs, (sum_ref,) = refs[:8], refs[8:16], refs[16:]
-    for side in range(2):
-        at = lax.axis_index("y" if side == 0 else "dp")
-        group = ins[4 * side : 4 * side + 4]
-        sum_ref[...] = sum(r[...].astype(F32) for r in group)
-        for d in range(4):
-            rows = pl.ds(pl.multiple_of(((at + d) & 3) * 64, 64), 64)
-            outs[4 * side + d][...] = sum_ref[rows, :].astype(BF16)
+            for term in range(2):
+                total = keep_ref[term, at, :].astype(F32) + got_ref[term, at, :].astype(F32)
+                outs[d][term, b * 64 : (b + 1) * 64, :] = total.astype(BF16)
+    own = pltpu.make_async_copy(own_ref, own_hbm, sem)
+    own.start()
+    own.wait()
+
+
+def plane_kernel(own_hbm, *refs):
+    others, outs, (sum_ref, own_ref, sem) = refs[:3], refs[3:7], refs[7:]
+    own = pltpu.make_async_copy(own_hbm, own_ref, sem)
+    own.start()
+    me = place(True)
+    sum_ref[...] = sum(r[...].astype(F32) for r in others)
+    own.wait()
+    sum_ref[...] += own_ref[...].astype(F32)
+    for d in range(4):
+        at = pl.ds(pl.multiple_of(((me + d) & 3) * 64, 64), 64)
+        outs[d][...] = sum_ref[:, at, :].astype(BF16)
 
 
 def line_kernel(*refs):
-    ins, out_ref = refs[:8], refs[8]
-    half = WIDTH // 2
-    for side in range(2):
-        group = ins[4 * side : 4 * side + 4]
-        total = sum(r[...].astype(F32) for r in group).astype(BF16)
-        out_ref[:, side * half : (side + 1) * half] = total
+    ins, out_ref = refs[:4], refs[4]
+    for term in range(2):
+        total = sum(r[term].astype(F32) for r in ins)
+        for z in range(8):
+            out_ref[z, term * 8 : (term + 1) * 8, :] = total[z * 8 : (z + 1) * 8, :].astype(BF16)
 
 
 def final_kernel(wire_ref, out_ref):
@@ -347,13 +355,15 @@
     )
 
 
-def ring(x, axis, d, n=4):
-    return lax.ppermute(x, axis, [(i, (i + d) % n) for i in range(n)])
-
-
-def spread_out(pieces, axis):
-    far, right, left = (ring(pieces[d], axis, d) for d in (2, 1, 3))
-    return [pieces[0], right, far, left]
+def ring(x, d, turn):
+    pairs = []
+    for a in range(4):
+        for b in range(4):
+            for c in range(2):
+                over_dp = (c == 0) != turn
+                to = ((a + d) % 4, b) if over_dp else (a, (b + d) % 4)
+                pairs.append(((a * 4 + b) * 2 + c, (to[0] * 4 + to[1]) * 2 + c))
+    return lax.ppermute(x, ("dp", "y", "core"), pairs)
 
 
 def in_hbm(*arrays):
@@ -397,44 +407,49 @@
 
     a_shape = (PEERS, PART, ROWS)
     vmem = pl.BlockSpec(memory_space=pltpu.VMEM)
-    a_wire, *ends, total = call(
+    a_wire, keep, give, total = call(
         counts_kernel, "counts",
-        [(a_shape, BF16), *[((WIDTH, half), BF16)] * 4, ((1, 128), F32)],
+        [(a_shape, BF16), ((2, WIDTH, half), BF16), ((2, WIDTH, half), BF16), ((1, 128), F32)],
         [
             (y_shape, BF16), ((ROWS, WIDTH), BF16), (square, BF16),
-            ((STEPS, WIDTH, ROWS), BF16), ((WIDTH, STEPS * ROWS), BF16), (a_shape, BF16),
-            ((STEPS * ROWS, WIDTH), BF16), ((WIDTH, STEPS * ROWS), BF16),
-            pltpu.SemaphoreType.DMA((5,)), pltpu.SemaphoreType.DMA(()),
+            ((STEPS, WIDTH, ROWS), BF16), ((1, ROWS), F32), ((WIDTH, STEPS * ROWS), BF16),
+            (a_shape, BF16), ((STEPS * ROWS, WIDTH), BF16), ((WIDTH, STEPS * ROWS), BF16),
+            pltpu.SemaphoreType.DMA((6,)), pltpu.SemaphoreType.DMA(()),
         ],
         limit=40 * 2**20,
-        specs=dict(in_specs=[vmem] * 2 + [hbm] * 5, out_specs=[hbm] + [vmem] * 5),
-    )(got, local, *in_hbm(y, alpha, turned, factor, weight))
-    keep, give = ends[:2], ends[2:]
-
+        specs=dict(in_specs=[vmem] + [hbm] * 6, out_specs=[hbm] + [vmem] * 3),
+    )(got, *in_hbm(y, alpha, turned, factor, local, weight))
     core = lax.axis_index("core")
     swap_cores = [(0, 1), (1, 0)]
-    parts = []
-    for n, axis in enumerate(("dp", "y")):
-        got_half = lax.ppermute(give[n], "core", swap_cores)
-        pieces = call(functools.partial(pair_kernel, axis), "pair_" + axis, [((256, half), BF16)] * 4)(
-            keep[n], got_half
-        )
-        parts += spread_out(pieces, axis)
-    a_wire, parts[1] = lax.optimization_barrier((a_wire, parts[1]))
+    shape, small = (2, 256, half), (2, 64, half)
+    own, *pieces = call(
+        pair_kernel, "pair", [(shape, BF16)] * 4, [(shape, BF16), pltpu.SemaphoreType.DMA(())],
+        specs=dict(out_specs=[hbm] + [vmem] * 3),
+    )(keep, lax.ppermute(give, "core", swap_cores))
+    far, right, left = (ring(pieces[d - 1], d, False) for d in (2, 1, 3))
+    mark, *_ = lax.optimization_barrier((total, *pieces))
+    a_wire, _ = lax.optimization_barrier((a_wire, lax.ppermute(mark, "core", swap_cores)))
     a_got = lax.all_to_all(a_wire, state, 0, 0, tiled=True)
-    pieces = call(plane_kernel, "plane", [((64, half), BF16)] * 8, [((256, half), F32)])(*parts)
-    parts = spread_out(pieces[:4], "y") + spread_out(pieces[4:], "dp")
-    (part,) = call(line_kernel, "line", [((64, WIDTH), BF16)])(*parts)
+    own, *pieces = call(
+        plane_kernel, "plane", [(small, BF16)] * 4,
+        [(shape, F32), (shape, BF16), pltpu.SemaphoreType.DMA(())],
+        specs=dict(in_specs=[hbm] + [vmem] * 3),
+    )(*in_hbm(own), far, right, left)
+    far, right, left = (ring(pieces[d - 1], d, True) for d in (2, 1, 3))
+    (part,) = call(line_kernel, "line", [((8, 16, half), BF16)])(own, far, right, left)
     (alpha_final,) = call(final_kernel, "final", [((ROWS, WIDTH), BF16)])(a_got)
-    part = lax.all_to_all(part.reshape(8, 8, WIDTH), "z", 0, 0, tiled=True)
+    part = lax.all_to_all(part, "z", 0, 0, tiled=True)
     loglik = jnp.log(total[0, 2 : 3 * SEQ_DEV : 3] / (WIDTH * WIDTH))
     part, alpha_final, loglik = lax.optimization_barrier((part, alpha_final, loglik))
     part = jnp.sum(part.astype(F32), axis=0)
-    mine = jnp.where(core == 0, part[:4], part[4:])
-    other = lax.ppermute(jnp.where(core == 0, part[4:], part[:4]), "core", swap_cores)
+    part = part.reshape(2, 2, 4, half)
+    mine = jnp.where(core == 0, part[:, 0], part[:, 1])
+    other = lax.ppermute(jnp.where(core == 0, part[:, 1], part[:, 0]), "core", swap_cores)
+    left, right = jnp.where(core == 0, mine, other), jnp.where(core == 0, other, mine)
+    sums = jnp.concatenate([left, right], axis=2)
     scale = 1.0 / (SEQ_DEV * 4 * STEPS)
-    counts_rows = jnp.where(core == 0, mine, other) * take_rows[:4] * scale
-    counts_cols = jnp.where(core == 0, other, mine) * take_cols[:4] * scale
+    counts_rows = sums[0] * take_rows[:4] * scale
+    counts_cols = sums[1] * take_cols[:4] * scale
 
     return (
         alpha_final.reshape(SEQ_DEV, PART, WIDTH),

time: 131 us -> 124 us (0.947)
  starting transfers between devices: 45.3 us -> 38.4 us
  local copies, waits for them, and re-layouts: 2.4 us -> 0.92 us
    ppermute x15 -> x8, starting transfers between devices: 21.3 us -> 15 us  [the longest x6 12.9 us: ring(): return lax.ppermute(x, ('dp', 'y', 'core'), pairs)]
    unnamed x10 -> x6, local copies, waits for them, and re-layouts: 2.31 us -> 0.81 us
    pallas_call x5 -> x4, Pallas kernels: 11.3 us -> 12.2 us  [the longest x1 9.67 us: on_device(): call(counts_kernel, 'counts', [(a_shape, BF16), ((2, WIDTH, half), BF16),...]
    ppermute x15 -> x8, waiting for transfers between devices: 10.8 us -> 10.8 us  [the longest x6 5.91 us: ring(): return lax.ppermute(x, ('dp', 'y', 'core'), pairs)]
  transfers between devices with their start and end apart: 18 -> 11, of which waited for: 9 -> 7; matrix products, arithmetic and copies ran while one was open for 0% -> 0% of each run, Pallas kernels for 8% -> 9%
where the time goes in v4:
time: 124 us; the launch traced here: 123 us
  waiting for transfers between devices  52.4 us (42%)
  starting transfers between devices  38.4 us (31%)
  Pallas kernels  29.7 us (24%)
    all_to_all x1, waiting for transfers between devices, on_device(): got = lax.all_to_all(wire, state, 0, 0, tiled=True)  35.4 us
    all_to_all x1, starting transfers between devices, on_device(): got = lax.all_to_all(wire, state, 0, 0, tiled=True)  13.2 us
    ppermute x6, starting transfers between devices, ring(): return lax.ppermute(x, ('dp', 'y', 'core'), pairs)  12.9 us
    pallas_call x1, Pallas kernels, on_device(): call(counts_kernel, 'counts', [(a_shape, BF16), ((2, WIDTH, half), BF16),...  9.67 us
    pallas_call x1, Pallas kernels, on_device(): call(send_kernel, 'send', [(wire_shape, BF16), (y_shape, BF16)], [((ROWS,...  8.93 us
    pallas_call x1, Pallas kernels, on_device(): call(local_kernel, 'local', [((WIDTH, STEPS * ROWS), BF16), (square, BF16...  7.23 us
    all_to_all x1, starting transfers between devices, on_device(): a_got = lax.all_to_all(a_wire, state, 0, 0, tiled=True)  6.84 us
    all_to_all x1, waiting for transfers between devices, on_device(): part = lax.all_to_all(part, 'z', 0, 0, tiled=True)  6.26 us
  transfers between devices with their start and end apart: 11, of which 7 were waited for; matrix products, arithmetic and copies ran while one was open for 0% of the time, Pallas kernels for 9%

profile of v4, /device:TPU:1, one launch (start us, length us, event | category | flops | bytes accessed | tf_op | source)
XLA Modules:
  0.0 123.3 jit_solution(3560323451276579820)
XLA Ops:
  0.6 8.9 %send.1 = (bf16[64,104,128]{2,1,0:T(8,128)(2,1)}, bf16[2,128,1024]{2,1,0:T(8,128)(2,1)}) custom-call(s32[3,8]{1,0:T(4,128)} %bitcast.57, bf16[128,1024]{1,0:T(8,128)(2,1)} %bitcast.55, bf16[1024,1024]{1,0:T(8,128)(2,1)} %rows_ref.1, bf16[1024,1024]{1,0:T(8,128)(2,1)} %cols_ref.1, bf16[512,1024]{1,0:T(8,128)(2,1)} %emit_rows_ref.1, ...), custom_call_target="tpu_custom_call" | custom-call | flops 1000000000 | bytes 8000000 | tf_op jit(solution)/shard_map/send/pallas_call | solution.py:383
  9.6 13.2 %all-to-all-start = ((bf16[64,104,128]{2,1,0:T(8,128)(2,1)}), bf16[64,104,128]{2,1,0:T(8,128)(2,1)S(1)}, u32[]{:S(2)}, u32[]{:S(2)}) async-start(bf16[64,104,128]{2,1,0:T(8,128)(2,1)} %get-tuple-element.27), calls=%async_computation | async-start | bytes 3407872 | tf_op jit(solution)/shard_map/all_to_all | solution.py:397
  22.8 7.2 %local.1 = (bf16[1024,384]{1,0:T(8,128)(2,1)}, bf16[1024,1024]{1,0:T(8,128)(2,1)}, bf16[3,1024,128]{2,1,0:T(8,128)(2,1)}, f32[1,128]{1,0:T(1,128)}, f32[8,1024]{1,0:T(8,128)}, /*index=5*/f32[8,1024]{1,0:T(8,128)}) custom-call(s32[3,8]{1,0:T(4,128)} %bitcast.58, bf16[1024,1024]{1,0:T(8,128)(2,1)} %rows_ref.1, bf16[1024,1024]{1,0:T(8,128)(2,1)} %cols_ref.1, ...), custom_call_target="tpu_custom_call" | custom-call | flops 1000000000 | bytes 8000000 | tf_op jit(solution)/shard_map/local/pallas_call | solution.py:399
  30.0 35.4 %all-to-all-done.wire_ref = bf16[64,104,128]{2,1,0:T(8,128)(2,1)S(1)} async-done(((bf16[64,104,128]{2,1,0:T(8,128)(2,1)}), bf16[64,104,128]{2,1,0:T(8,128)(2,1)S(1)}, u32[]{:S(2)}, u32[]{:S(2)}) %all-to-all-start) | async-done | bytes 1703968 | tf_op jit(solution)/shard_map/all_to_all | solution.py:397
  65.4 9.7 %counts.1 = (bf16[64,16,128]{2,1,0:T(8,128)(2,1)}, bf16[2,1024,512]{2,1,0:T(8,128)(2,1)S(1)}, bf16[2,1024,512]{2,1,0:T(8,128)(2,1)S(1)}, f32[1,128]{1,0:T(1,128)S(1)}) custom-call(bf16[64,104,128]{2,1,0:T(8,128)(2,1)S(1)} %all-to-all-done.wire_ref, bf16[2,128,1024]{2,1,0:T(8,128)(2,1)} %get-tuple-element.28.y_hbm, bf16[128,1024]{1,0:T(8,128)(2,1)} %bitcast.56, ...), custom_call_target="tpu_custom_call" | custom-call | flops 1000000000 | bytes 8000000 | tf_op jit(solution)/shard_map/counts/pallas_call | solution.py:410
  75.2 4.1 %collective-permute-done.got_ref = bf16[2,1024,512]{2,1,0:T(8,128)(2,1)S(1)} collective-permute-done((bf16[2,1024,512]{2,1,0:T(8,128)(2,1)S(1)}, bf16[2,1024,512]{2,1,0:T(8,128)(2,1)S(1)}, u32[]{:S(2)}, u32[]{:S(2)}) %collective-permute-start) | collective-permute-done | bytes 2097184 | tf_op jit(solution)/shard_map/ppermute | solution.py:428
  79.3 0.5 pair.1
  79.8 0.8 copy-done
  80.6 2.8 %collective-permute-start.1 = (bf16[2,256,512]{2,1,0:T(8,128)(2,1)S(1)}, bf16[2,256,512]{2,1,0:T(8,128)(2,1)S(1)}, u32[]{:S(2)}, u32[]{:S(2)}) collective-permute-start(bf16[2,256,512]{2,1,0:T(8,128)(2,1)S(1)} %get-tuple-element.36), channel_id=1, source_target_pairs={{0,128},{1,33},{16,144},{17,49},{32,160},{33,1},{48,176},{49,17},{... | collective-permute-start | bytes 1572872 | tf_op jit(solution)/shard_map/ppermute | solution.py:366
  83.8 2.3 %collective-permute-start.3 = (bf16[2,256,512]{2,1,0:T(8,128)(2,1)S(1)}, bf16[2,256,512]{2,1,0:T(8,128)(2,1)S(1)}, u32[]{:S(2)}, u32[]{:S(2)}) collective-permute-start(bf16[2,256,512]{2,1,0:T(8,128)(2,1)S(1)} %get-tuple-element.38), channel_id=1, source_target_pairs={{0,192},{1,49},{16,208},{17,1},{32,224},{33,17},{48,240},{49,33},{... | collective-permute-start | bytes 1572872 | tf_op jit(solution)/shard_map/ppermute | solution.py:366
  86.1 6.8 %all-to-all-start.2 = ((bf16[64,16,128]{2,1,0:T(8,128)(2,1)}), bf16[64,16,128]{2,1,0:T(8,128)(2,1)S(1)}, u32[]{:S(2)}, u32[]{:S(2)}) async-start(bf16[64,16,128]{2,1,0:T(8,128)(2,1)} %get-tuple-element.43), calls=%async_computation.2 | async-start | bytes 524288 | tf_op jit(solution)/shard_map/all_to_all | solution.py:432
  93.0 3.1 %collective-permute-done.2.refs_1_ = bf16[2,256,512]{2,1,0:T(8,128)(2,1)S(1)} collective-permute-done((bf16[2,256,512]{2,1,0:T(8,128)(2,1)S(1)}, bf16[2,256,512]{2,1,0:T(8,128)(2,1)S(1)}, u32[]{:S(2)}, u32[]{:S(2)}) %collective-permute-start.2) | collective-permute-done | bytes 524320 | tf_op jit(solution)/shard_map/ppermute | solution.py:366
  96.1 0.6 collective-permute-done.3.refs_2_
  96.6 1.3 %plane.1 = (bf16[2,64,512]{2,1,0:T(8,128)(2,1)S(1)}, bf16[2,64,512]{2,1,0:T(8,128)(2,1)S(1)}, bf16[2,64,512]{2,1,0:T(8,128)(2,1)S(1)}, bf16[2,64,512]{2,1,0:T(8,128)(2,1)S(1)}) custom-call(bf16[2,256,512]{2,1,0:T(8,128)(2,1)} %copy-done, bf16[2,256,512]{2,1,0:T(8,128)(2,1)S(1)} %collective-permute-done.1.refs_0_, ...), custom_call_target="tpu_custom_call" | custom-call | flops 1000000000 | bytes 8000000 | tf_op jit(solution)/shard_map/plane/pallas_call | solution.py:433
  97.9 4.7 %collective-permute-start.4 = (bf16[2,64,512]{2,1,0:T(8,128)(2,1)S(1)}, bf16[2,64,512]{2,1,0:T(8,128)(2,1)S(1)}, u32[]{:S(2)}, u32[]{:S(2)}) collective-permute-start(bf16[2,64,512]{2,1,0:T(8,128)(2,1)S(1)} %get-tuple-element.40), channel_id=1, source_target_pairs={{0,32},{1,129},{16,48},{17,145},{32,0},{33,161},{48,16},{49,177},{... | collective-permute-start | bytes 393224 | tf_op jit(solution)/shard_map/ppermute | solution.py:366
  102.6 2.7 %collective-permute-start.6 = (bf16[2,64,512]{2,1,0:T(8,128)(2,1)S(1)}, bf16[2,64,512]{2,1,0:T(8,128)(2,1)S(1)}, u32[]{:S(2)}, u32[]{:S(2)}) collective-permute-start(bf16[2,64,512]{2,1,0:T(8,128)(2,1)S(1)} %get-tuple-element.42), channel_id=1, source_target_pairs={{0,48},{1,193},{16,0},{17,209},{32,16},{33,225},{48,32},{49,241},{... | collective-permute-start | bytes 393224 | tf_op jit(solution)/shard_map/ppermute | solution.py:366
  105.4 2.3 %collective-permute-done.5.refs_2_ = bf16[2,64,512]{2,1,0:T(8,128)(2,1)S(1)} collective-permute-done((bf16[2,64,512]{2,1,0:T(8,128)(2,1)S(1)}, bf16[2,64,512]{2,1,0:T(8,128)(2,1)S(1)}, u32[]{:S(2)}, u32[]{:S(2)}) %collective-permute-start.5) | collective-permute-done | bytes 131104 | tf_op jit(solution)/shard_map/ppermute | solution.py:366
  107.6 0.7 line.1
  108.4 3.4 %all-to-all-start.1 = ((bf16[8,16,512]{2,1,0:T(8,128)(2,1)}), bf16[8,16,512]{2,1,0:T(8,128)(2,1)S(1)}, u32[]{:S(2)}, u32[]{:S(2)}) async-start(bf16[8,16,512]{2,1,0:T(8,128)(2,1)} %line.1), calls=%async_computation.1 | async-start | bytes 262144 | tf_op jit(solution)/shard_map/all_to_all | solution.py:441
  112.3 1.3 %final.1 = bf16[128,1024]{1,0:T(8,128)(2,1)} custom-call(bf16[64,16,128]{2,1,0:T(8,128)(2,1)S(1)} %all-to-all-done.2.wire_ref), custom_call_target="tpu_custom_call" | custom-call | flops 1000000000 | bytes 8000000 | tf_op jit(solution)/shard_map/final/pallas_call | solution.py:440
  113.6 6.3 %all-to-all-done.1 = bf16[8,16,512]{2,1,0:T(8,128)(2,1)S(1)} async-done(((bf16[8,16,512]{2,1,0:T(8,128)(2,1)}), bf16[8,16,512]{2,1,0:T(8,128)(2,1)S(1)}, u32[]{:S(2)}, u32[]{:S(2)}) %all-to-all-start.1) | async-done | bytes 131104 | tf_op jit(solution)/shard_map/all_to_all | solution.py:441
  119.9 1.9 %collective-permute-start.7 = (f32[2,4,512]{2,1,0:T(4,128)S(1)}, f32[2,4,512]{2,1,0:T(4,128)S(1)}, u32[]{:S(2)}, u32[]{:S(2)}) collective-permute-start(f32[2,4,512]{2,1,0:T(4,128)S(1)} %select_bitcast_fusion), channel_id=1, source_target_pairs={{0,1},{1,0},{2,3},{3,2},{4,5},{5,4},{6,7},{7,6},{8,9},{9,8},{10,11... | collective-permute-start | bytes 49160 | tf_op jit(solution)/shard_map/ppermute | solution.py:447
  121.8 0.8 collective-permute-done.7
  122.7 0.6 fusion.8
  (18 shorter events, 1.3 us)
Async XLA Ops:
  9.6 55.8 %all-to-all-start = ((bf16[64,104,128]{2,1,0:T(8,128)(2,1)}), bf16[64,104,128]{2,1,0:T(8,128)(2,1)S(1)}, u32[]{:S(2)}, u32[]{:S(2)}) async-start(bf16[64,104,128]{2,1,0:T(8,128)(2,1)} %get-tuple-element.27), calls=%async_computation | async-start | bytes 3407872 | tf_op jit(solution)/shard_map/all_to_all | solution.py:397
  75.0 4.2 %collective-permute-start = (bf16[2,1024,512]{2,1,0:T(8,128)(2,1)S(1)}, bf16[2,1024,512]{2,1,0:T(8,128)(2,1)S(1)}, u32[]{:S(2)}, u32[]{:S(2)}) collective-permute-start(bf16[2,1024,512]{2,1,0:T(8,128)(2,1)S(1)} %get-tuple-element.34), channel_id=1, source_target_pairs={{0,1},{1,0},{2,3},{3,2},{4,5},{5,4},{6,7},{7,6},{8,9},{9,8},{10,11... | collective-permute-start | bytes 6291464 | tf_op jit(solution)/shard_map/ppermute | solution.py:428
  79.8 0.8 copy-start
  80.6 12.4 %collective-permute-start.1 = (bf16[2,256,512]{2,1,0:T(8,128)(2,1)S(1)}, bf16[2,256,512]{2,1,0:T(8,128)(2,1)S(1)}, u32[]{:S(2)}, u32[]{:S(2)}) collective-permute-start(bf16[2,256,512]{2,1,0:T(8,128)(2,1)S(1)} %get-tuple-element.36), channel_id=1, source_target_pairs={{0,128},{1,33},{16,144},{17,49},{32,160},{33,1},{48,176},{49,17},{... | collective-permute-start | bytes 1572872 | tf_op jit(solution)/shard_map/ppermute | solution.py:366
  83.5 12.6 %collective-permute-start.2 = (bf16[2,256,512]{2,1,0:T(8,128)(2,1)S(1)}, bf16[2,256,512]{2,1,0:T(8,128)(2,1)S(1)}, u32[]{:S(2)}, u32[]{:S(2)}) collective-permute-start(bf16[2,256,512]{2,1,0:T(8,128)(2,1)S(1)} %get-tuple-element.37), channel_id=1, source_target_pairs={{0,64},{1,17},{16,80},{17,33},{32,96},{33,49},{48,112},{49,1},{64,... | collective-permute-start | bytes 1572872 | tf_op jit(solution)/shard_map/ppermute | solution.py:366
  83.8 12.8 %collective-permute-start.3 = (bf16[2,256,512]{2,1,0:T(8,128)(2,1)S(1)}, bf16[2,256,512]{2,1,0:T(8,128)(2,1)S(1)}, u32[]{:S(2)}, u32[]{:S(2)}) collective-permute-start(bf16[2,256,512]{2,1,0:T(8,128)(2,1)S(1)} %get-tuple-element.38), channel_id=1, source_target_pairs={{0,192},{1,49},{16,208},{17,1},{32,224},{33,17},{48,240},{49,33},{... | collective-permute-start | bytes 1572872 | tf_op jit(solution)/shard_map/ppermute | solution.py:366
  86.1 22.2 %all-to-all-start.2 = ((bf16[64,16,128]{2,1,0:T(8,128)(2,1)}), bf16[64,16,128]{2,1,0:T(8,128)(2,1)S(1)}, u32[]{:S(2)}, u32[]{:S(2)}) async-start(bf16[64,16,128]{2,1,0:T(8,128)(2,1)} %get-tuple-element.43), calls=%async_computation.2 | async-start | bytes 524288 | tf_op jit(solution)/shard_map/all_to_all | solution.py:432
  97.9 7.5 %collective-permute-start.4 = (bf16[2,64,512]{2,1,0:T(8,128)(2,1)S(1)}, bf16[2,64,512]{2,1,0:T(8,128)(2,1)S(1)}, u32[]{:S(2)}, u32[]{:S(2)}) collective-permute-start(bf16[2,64,512]{2,1,0:T(8,128)(2,1)S(1)} %get-tuple-element.40), channel_id=1, source_target_pairs={{0,32},{1,129},{16,48},{17,145},{32,0},{33,161},{48,16},{49,177},{... | collective-permute-start | bytes 393224 | tf_op jit(solution)/shard_map/ppermute | solution.py:366
  102.6 5.0 %collective-permute-start.5 = (bf16[2,64,512]{2,1,0:T(8,128)(2,1)S(1)}, bf16[2,64,512]{2,1,0:T(8,128)(2,1)S(1)}, u32[]{:S(2)}, u32[]{:S(2)}) collective-permute-start(bf16[2,64,512]{2,1,0:T(8,128)(2,1)S(1)} %get-tuple-element.41), channel_id=1, source_target_pairs={{0,16},{1,65},{16,32},{17,81},{32,48},{33,97},{48,0},{49,113},{64,... | collective-permute-start | bytes 393224 | tf_op jit(solution)/shard_map/ppermute | solution.py:366
  102.6 5.0 %collective-permute-start.6 = (bf16[2,64,512]{2,1,0:T(8,128)(2,1)S(1)}, bf16[2,64,512]{2,1,0:T(8,128)(2,1)S(1)}, u32[]{:S(2)}, u32[]{:S(2)}) collective-permute-start(bf16[2,64,512]{2,1,0:T(8,128)(2,1)S(1)} %get-tuple-element.42), channel_id=1, source_target_pairs={{0,48},{1,193},{16,0},{17,209},{32,16},{33,225},{48,32},{49,241},{... | collective-permute-start | bytes 393224 | tf_op jit(solution)/shard_map/ppermute | solution.py:366
  108.4 11.5 %all-to-all-start.1 = ((bf16[8,16,512]{2,1,0:T(8,128)(2,1)}), bf16[8,16,512]{2,1,0:T(8,128)(2,1)S(1)}, u32[]{:S(2)}, u32[]{:S(2)}) async-start(bf16[8,16,512]{2,1,0:T(8,128)(2,1)} %line.1), calls=%async_computation.1 | async-start | bytes 262144 | tf_op jit(solution)/shard_map/all_to_all | solution.py:441
  111.7 10.9 %copy-start.1 = (f32[8,1024]{1,0:T(8,128)S(1)}, f32[8,1024]{1,0:T(8,128)}, u32[]{:S(2)}) copy-start(f32[8,1024]{1,0:T(8,128)} %get-tuple-element.47) | copy-start | bytes 98308
  111.8 10.9 %copy-start.2 = (f32[8,1024]{1,0:T(8,128)S(1)}, f32[8,1024]{1,0:T(8,128)}, u32[]{:S(2)}) copy-start(f32[8,1024]{1,0:T(8,128)} %get-tuple-element.48) | copy-start | bytes 98308
  119.9 2.7 %collective-permute-start.7 = (f32[2,4,512]{2,1,0:T(4,128)S(1)}, f32[2,4,512]{2,1,0:T(4,128)S(1)}, u32[]{:S(2)}, u32[]{:S(2)}) collective-permute-start(f32[2,4,512]{2,1,0:T(4,128)S(1)} %select_bitcast_fusion), channel_id=1, source_target_pairs={{0,1},{1,0},{2,3},{3,2},{4,5},{5,4},{6,7},{7,6},{8,9},{9,8},{10,11... | collective-permute-start | bytes 49160 | tf_op jit(solution)/shard_map/ppermute | solution.py:447

commit v5 on v4

--- a/solution.py
+++ b/solution.py
@@ -222,14 +222,13 @@
 
 
 def counts_kernel(
-    wire_ref, y_hbm, alpha_hbm, turned_hbm, factor_hbm, local_hbm, weight_hbm,
-    out_hbm, keep_ref, give_ref, total_ref,
-    y_ref, alpha_ref, turned_ref, factor_ref, local_ref, weight_ref, out_ref, ys_ref, m_ref,
-    in_sem, out_sem,
+    wire_ref, y_hbm, alpha_hbm, turned_hbm, factor_hbm, weight_hbm,
+    after_ref, keep_ref, give_ref, total_ref,
+    y_ref, alpha_ref, turned_ref, factor_ref, weight_ref, ys_ref, m_ref, in_sem,
 ):
     pairs = [
         (y_hbm, y_ref), (alpha_hbm, alpha_ref), (turned_hbm, turned_ref),
-        (factor_hbm, factor_ref), (local_hbm, local_ref), (weight_hbm, weight_ref),
+        (factor_hbm, factor_ref), (weight_hbm, weight_ref),
     ]
     loads = [pltpu.make_async_copy(a, b, in_sem.at[n]) for n, (a, b) in enumerate(pairs)]
     for load in loads:
@@ -237,14 +236,10 @@
     core = lax.axis_index("core")
     half = WIDTH // 2
 
-    def put(term, side, rows, lanes, value):
-        @pl.when(core == side)
-        def _():
-            keep_ref[term, rows, lanes] = value.astype(BF16)
-
-        @pl.when(core != side)
-        def _():
-            give_ref[term, rows, lanes] = value.astype(BF16)
+    targets = [
+        (ref, pl.multiple_of(side * half, half))
+        for ref, side in ((keep_ref, core), (give_ref, 1 - core))
+    ]
 
     totals = total_of(wire_ref)
     total_ref[...] = totals
@@ -269,28 +264,30 @@
             ],
             axis=1,
         )
-        value = dot(v, ys_ref[...])
-        for side in range(2):
-            part = value[:, side * half : (side + 1) * half]
-            put(1, side, slice(b * 256, (b + 1) * 256), slice(0, half), part)
+        for ref, start in targets:
+            ref[1, b * 256 : (b + 1) * 256, :] = dot(v, ys_ref[:, pl.ds(start, half)]).astype(BF16)
 
     loads[2].wait()
     loads[3].wait()
-    loads[4].wait()
-    f0, f1, f2 = (factor_ref[t].astype(F32) for t in range(STEPS))
+    f0, f1 = (factor_ref[t].astype(F32) for t in range(2))
     h = dot(turned_ref[...], jnp.concatenate([x_of(1), x_of(2)], axis=1))
     m_ref[:, ROWS : 2 * ROWS] = (h[:, :ROWS] * f0 * inv[1]).astype(BF16)
     h = dot(turned_ref[...], (h[:, ROWS:] * f0).astype(BF16)) * f1
     m_ref[:, 2 * ROWS :] = (h * inv[2]).astype(BF16)
-    a = dot(turned_ref[...], h.astype(BF16)) * f2 * (local_ref[...] * inv[2])
+    after_ref[...] = h.astype(BF16)
+    loads[4].wait()
+    for b in range(2):
+        for ref, start in targets:
+            at = pl.ds(pl.multiple_of(start + b * 256, 256), 256)
+            value = dot_nt(weight_ref[...], m_ref[at, :])
+            ref[0, :, b * 256 : (b + 1) * 256] = value.astype(BF16)
+
+
+def alpha_kernel(after_ref, turned_ref, factor_ref, local_ref, total_ref, out_ref):
+    inv = to_row(inverse_norm(total_ref[...], STEPS - 1))
+    factor = factor_ref[STEPS - 1].astype(F32) * (local_ref[...] * inv)
+    a = dot(turned_ref[...], after_ref[...]) * factor
     out_ref[...] = a.astype(BF16).reshape(PEERS, PART, ROWS)
-    send = pltpu.make_async_copy(out_ref, out_hbm, out_sem)
-    send.start()
-    loads[5].wait()
-    for b in range(4):
-        value = dot_nt(weight_ref[...], m_ref[b * 256 : (b + 1) * 256, :])
-        put(0, b // 2, slice(0, WIDTH), slice((b & 1) * 256, (b & 1) * 256 + 256), value)
-    send.wait()
 
 
 def place(turn):
@@ -407,18 +404,27 @@
 
     a_shape = (PEERS, PART, ROWS)
     vmem = pl.BlockSpec(memory_space=pltpu.VMEM)
-    a_wire, keep, give, total = call(
+    after, keep, give, total = call(
         counts_kernel, "counts",
-        [(a_shape, BF16), ((2, WIDTH, half), BF16), ((2, WIDTH, half), BF16), ((1, 128), F32)],
+        [
+            ((WIDTH, ROWS), BF16), ((2, WIDTH, half), BF16), ((2, WIDTH, half), BF16),
+            ((1, 128), F32),
+        ],
         [
             (y_shape, BF16), ((ROWS, WIDTH), BF16), (square, BF16),
-            ((STEPS, WIDTH, ROWS), BF16), ((1, ROWS), F32), ((WIDTH, STEPS * ROWS), BF16),
-            (a_shape, BF16), ((STEPS * ROWS, WIDTH), BF16), ((WIDTH, STEPS * ROWS), BF16),
-            pltpu.SemaphoreType.DMA((6,)), pltpu.SemaphoreType.DMA(()),
+            ((STEPS, WIDTH, ROWS), BF16), ((WIDTH, STEPS * ROWS), BF16),
+            ((STEPS * ROWS, WIDTH), BF16), ((WIDTH, STEPS * ROWS), BF16),
+            pltpu.SemaphoreType.DMA((5,)),
         ],
         limit=40 * 2**20,
-        specs=dict(in_specs=[vmem] + [hbm] * 6, out_specs=[hbm] + [vmem] * 3),
-    )(got, *in_hbm(y, alpha, turned, factor, local, weight))
+        specs=dict(in_specs=[vmem] + [hbm] * 5, out_specs=[vmem] * 4),
+    )(got, *in_hbm(y, alpha, turned, factor, weight))
+    (a_wire,) = call(alpha_kernel, "alpha", [(a_shape, BF16)])(
+        after, *in_hbm(turned, factor, local), total
+    )
+
+    keep, a_wire = lax.optimization_barrier((keep, a_wire))
+
     core = lax.axis_index("core")
     swap_cores = [(0, 1), (1, 0)]
     shape, small = (2, 256, half), (2, 64, half)

time: 124 us -> 120 us (0.968)
  waiting for transfers between devices: 52.4 us -> 49.4 us
    ppermute x1, waiting for transfers between devices: 4.06 us -> 0.83 us  [on_device(): lax.ppermute(give, 'core', swap_cores)]
    pallas_call x1 -> x2, Pallas kernels: 9.67 us -> 9.42 us  [the longest x1 6.17 us: on_device(): call(counts_kernel, 'counts', [((WIDTH, ROWS), BF16), ((2, WIDTH, half),...]
  transfers between devices with their start and end apart: 11 -> 11, of which waited for: 7 -> 7; matrix products, arithmetic and copies ran while one was open for 0% -> 1% of each run, Pallas kernels for 9% -> 11%
where the time goes in v5:
time: 120 us
  waiting for transfers between devices  49.4 us (41%)
  starting transfers between devices  38.4 us (32%)
  Pallas kernels  29.4 us (24%)
    all_to_all x1, waiting for transfers between devices, on_device(): got = lax.all_to_all(wire, state, 0, 0, tiled=True)  35.4 us
    all_to_all x1, starting transfers between devices, on_device(): got = lax.all_to_all(wire, state, 0, 0, tiled=True)  13.2 us
    ppermute x6, starting transfers between devices, ring(): return lax.ppermute(x, ('dp', 'y', 'core'), pairs)  12.9 us
    pallas_call x1, Pallas kernels, on_device(): call(send_kernel, 'send', [(wire_shape, BF16), (y_shape, BF16)], [((ROWS,...  8.93 us
    pallas_call x1, Pallas kernels, on_device(): call(local_kernel, 'local', [((WIDTH, STEPS * ROWS), BF16), (square, BF16...  7.23 us
    all_to_all x1, starting transfers between devices, on_device(): a_got = lax.all_to_all(a_wire, state, 0, 0, tiled=True)  6.82 us
    all_to_all x1, waiting for transfers between devices, on_device(): part = lax.all_to_all(part, 'z', 0, 0, tiled=True)  6.42 us
    pallas_call x1, Pallas kernels, on_device(): call(counts_kernel, 'counts', [((WIDTH, ROWS), BF16), ((2, WIDTH, half),...  6.17 us
  transfers between devices with their start and end apart: 11, of which 7 were waited for; matrix products, arithmetic and copies ran while one was open for 1% of the time, Pallas kernels for 11%

profile of v5, /device:TPU:1, one launch (start us, length us, event | category | flops | bytes accessed | tf_op | source)
XLA Modules:
  0.0 120.0 jit_solution(13770270419441275128)
XLA Ops:
  0.6 8.9 %send.1 = (bf16[64,104,128]{2,1,0:T(8,128)(2,1)}, bf16[2,128,1024]{2,1,0:T(8,128)(2,1)}) custom-call(s32[3,8]{1,0:T(4,128)} %bitcast.57, bf16[128,1024]{1,0:T(8,128)(2,1)} %bitcast.55, bf16[1024,1024]{1,0:T(8,128)(2,1)} %rows_ref.1, bf16[1024,1024]{1,0:T(8,128)(2,1)} %cols_ref.1, bf16[512,1024]{1,0:T(8,128)(2,1)} %emit_rows_ref.1, ...), custom_call_target="tpu_custom_call" | custom-call | flops 1000000000 | bytes 8000000 | tf_op jit(solution)/shard_map/send/pallas_call | solution.py:380
  9.6 13.2 %all-to-all-start = ((bf16[64,104,128]{2,1,0:T(8,128)(2,1)}), bf16[64,104,128]{2,1,0:T(8,128)(2,1)S(1)}, u32[]{:S(2)}, u32[]{:S(2)}) async-start(bf16[64,104,128]{2,1,0:T(8,128)(2,1)} %get-tuple-element.29), calls=%async_computation | async-start | bytes 3407872 | tf_op jit(solution)/shard_map/all_to_all | solution.py:394
  22.8 7.2 %local.1 = (bf16[1024,384]{1,0:T(8,128)(2,1)}, bf16[1024,1024]{1,0:T(8,128)(2,1)}, bf16[3,1024,128]{2,1,0:T(8,128)(2,1)}, f32[1,128]{1,0:T(1,128)}, f32[8,1024]{1,0:T(8,128)}, /*index=5*/f32[8,1024]{1,0:T(8,128)}) custom-call(s32[3,8]{1,0:T(4,128)} %bitcast.58, bf16[1024,1024]{1,0:T(8,128)(2,1)} %rows_ref.1, bf16[1024,1024]{1,0:T(8,128)(2,1)} %cols_ref.1, ...), custom_call_target="tpu_custom_call" | custom-call | flops 1000000000 | bytes 8000000 | tf_op jit(solution)/shard_map/local/pallas_call | solution.py:396
  30.0 35.4 %all-to-all-done.wire_ref = bf16[64,104,128]{2,1,0:T(8,128)(2,1)S(1)} async-done(((bf16[64,104,128]{2,1,0:T(8,128)(2,1)}), bf16[64,104,128]{2,1,0:T(8,128)(2,1)S(1)}, u32[]{:S(2)}, u32[]{:S(2)}) %all-to-all-start) | async-done | bytes 1703968 | tf_op jit(solution)/shard_map/all_to_all | solution.py:394
  65.4 6.2 %counts.1 = (bf16[1024,128]{1,0:T(8,128)(2,1)S(1)}, bf16[2,1024,512]{2,1,0:T(8,128)(2,1)S(1)}, bf16[2,1024,512]{2,1,0:T(8,128)(2,1)S(1)}, f32[1,128]{1,0:T(1,128)S(1)}) custom-call(bf16[64,104,128]{2,1,0:T(8,128)(2,1)S(1)} %all-to-all-done.wire_ref, bf16[2,128,1024]{2,1,0:T(8,128)(2,1)} %get-tuple-element.30.y_hbm, bf16[128,1024]{1,0:T(8,128)(2,1)} %bitcast.56, ...), custom_call_target="tpu_custom_call" | custom-call | flops 1000000000 | bytes 8000000 | tf_op jit(solution)/shard_map/counts/pallas_call | solution.py:407
  71.9 3.3 %alpha.1 = bf16[64,16,128]{2,1,0:T(8,128)(2,1)} custom-call(bf16[1024,128]{1,0:T(8,128)(2,1)S(1)} %get-tuple-element.35.after_ref, bf16[1024,1024]{1,0:T(8,128)(2,1)} %get-tuple-element.31.turned_hbm.turned_ref, bf16[3,1024,128]{2,1,0:T(8,128)(2,1)} %get-tuple-element.32.factor_hbm.factor_ref, f32[1,128]{1,0:T(1,128)} %get-tuple-element.36.local_ref, ...), custom_call_target="tpu_custom_call" | custom-call | flops 1000000000 | bytes 8000000 | tf_op jit(solution)/shard_map/alpha/pallas_call | solution.py:422
  75.1 0.8 collective-permute-done.got_ref
  76.5 0.8 copy-done
  77.3 2.8 %collective-permute-start.1 = (bf16[2,256,512]{2,1,0:T(8,128)(2,1)S(1)}, bf16[2,256,512]{2,1,0:T(8,128)(2,1)S(1)}, u32[]{:S(2)}, u32[]{:S(2)}) collective-permute-start(bf16[2,256,512]{2,1,0:T(8,128)(2,1)S(1)} %get-tuple-element.41), channel_id=1, source_target_pairs={{0,128},{1,33},{16,144},{17,49},{32,160},{33,1},{48,176},{49,17},{... | collective-permute-start | bytes 1572872 | tf_op jit(solution)/shard_map/ppermute | solution.py:363
  80.5 2.3 %collective-permute-start.3 = (bf16[2,256,512]{2,1,0:T(8,128)(2,1)S(1)}, bf16[2,256,512]{2,1,0:T(8,128)(2,1)S(1)}, u32[]{:S(2)}, u32[]{:S(2)}) collective-permute-start(bf16[2,256,512]{2,1,0:T(8,128)(2,1)S(1)} %get-tuple-element.43), channel_id=1, source_target_pairs={{0,192},{1,49},{16,208},{17,1},{32,224},{33,17},{48,240},{49,33},{... | collective-permute-start | bytes 1572872 | tf_op jit(solution)/shard_map/ppermute | solution.py:363
  82.8 6.8 %all-to-all-start.2 = ((bf16[64,16,128]{2,1,0:T(8,128)(2,1)}), bf16[64,16,128]{2,1,0:T(8,128)(2,1)S(1)}, u32[]{:S(2)}, u32[]{:S(2)}) async-start(bf16[64,16,128]{2,1,0:T(8,128)(2,1)} %alpha.1), calls=%async_computation.2 | async-start | bytes 524288 | tf_op jit(solution)/shard_map/all_to_all | solution.py:438
  89.7 3.1 %collective-permute-done.2.refs_1_ = bf16[2,256,512]{2,1,0:T(8,128)(2,1)S(1)} collective-permute-done((bf16[2,256,512]{2,1,0:T(8,128)(2,1)S(1)}, bf16[2,256,512]{2,1,0:T(8,128)(2,1)S(1)}, u32[]{:S(2)}, u32[]{:S(2)}) %collective-permute-start.2) | collective-permute-done | bytes 524320 | tf_op jit(solution)/shard_map/ppermute | solution.py:363
  92.8 0.6 collective-permute-done.3.refs_2_
  93.3 1.3 %plane.1 = (bf16[2,64,512]{2,1,0:T(8,128)(2,1)S(1)}, bf16[2,64,512]{2,1,0:T(8,128)(2,1)S(1)}, bf16[2,64,512]{2,1,0:T(8,128)(2,1)S(1)}, bf16[2,64,512]{2,1,0:T(8,128)(2,1)S(1)}) custom-call(bf16[2,256,512]{2,1,0:T(8,128)(2,1)} %copy-done, bf16[2,256,512]{2,1,0:T(8,128)(2,1)S(1)} %collective-permute-done.1.refs_0_, ...), custom_call_target="tpu_custom_call" | custom-call | flops 1000000000 | bytes 8000000 | tf_op jit(solution)/shard_map/plane/pallas_call | solution.py:439
  94.6 4.7 %collective-permute-start.4 = (bf16[2,64,512]{2,1,0:T(8,128)(2,1)S(1)}, bf16[2,64,512]{2,1,0:T(8,128)(2,1)S(1)}, u32[]{:S(2)}, u32[]{:S(2)}) collective-permute-start(bf16[2,64,512]{2,1,0:T(8,128)(2,1)S(1)} %get-tuple-element.45), channel_id=1, source_target_pairs={{0,32},{1,129},{16,48},{17,145},{32,0},{33,161},{48,16},{49,177},{... | collective-permute-start | bytes 393224 | tf_op jit(solution)/shard_map/ppermute | solution.py:363
  99.3 2.7 %collective-permute-start.6 = (bf16[2,64,512]{2,1,0:T(8,128)(2,1)S(1)}, bf16[2,64,512]{2,1,0:T(8,128)(2,1)S(1)}, u32[]{:S(2)}, u32[]{:S(2)}) collective-permute-start(bf16[2,64,512]{2,1,0:T(8,128)(2,1)S(1)} %get-tuple-element.47), channel_id=1, source_target_pairs={{0,48},{1,193},{16,0},{17,209},{32,16},{33,225},{48,32},{49,241},{... | collective-permute-start | bytes 393224 | tf_op jit(solution)/shard_map/ppermute | solution.py:363
  102.1 2.3 %collective-permute-done.5.refs_2_ = bf16[2,64,512]{2,1,0:T(8,128)(2,1)S(1)} collective-permute-done((bf16[2,64,512]{2,1,0:T(8,128)(2,1)S(1)}, bf16[2,64,512]{2,1,0:T(8,128)(2,1)S(1)}, u32[]{:S(2)}, u32[]{:S(2)}) %collective-permute-start.5) | collective-permute-done | bytes 131104 | tf_op jit(solution)/shard_map/ppermute | solution.py:363
  104.4 0.7 line.1
  105.1 3.4 %all-to-all-start.1 = ((bf16[8,16,512]{2,1,0:T(8,128)(2,1)}), bf16[8,16,512]{2,1,0:T(8,128)(2,1)S(1)}, u32[]{:S(2)}, u32[]{:S(2)}) async-start(bf16[8,16,512]{2,1,0:T(8,128)(2,1)} %line.1), calls=%async_computation.1 | async-start | bytes 262144 | tf_op jit(solution)/shard_map/all_to_all | solution.py:447
  109.0 1.3 %final.1 = bf16[128,1024]{1,0:T(8,128)(2,1)} custom-call(bf16[64,16,128]{2,1,0:T(8,128)(2,1)S(1)} %all-to-all-done.2.wire_ref), custom_call_target="tpu_custom_call" | custom-call | flops 1000000000 | bytes 8000000 | tf_op jit(solution)/shard_map/final/pallas_call | solution.py:446
  110.3 6.4 %all-to-all-done.1 = bf16[8,16,512]{2,1,0:T(8,128)(2,1)S(1)} async-done(((bf16[8,16,512]{2,1,0:T(8,128)(2,1)}), bf16[8,16,512]{2,1,0:T(8,128)(2,1)S(1)}, u32[]{:S(2)}, u32[]{:S(2)}) %all-to-all-start.1) | async-done | bytes 131104 | tf_op jit(solution)/shard_map/all_to_all | solution.py:447
  116.8 1.7 %collective-permute-start.7 = (f32[2,4,512]{2,1,0:T(4,128)S(1)}, f32[2,4,512]{2,1,0:T(4,128)S(1)}, u32[]{:S(2)}, u32[]{:S(2)}) collective-permute-start(f32[2,4,512]{2,1,0:T(4,128)S(1)} %select_bitcast_fusion), channel_id=1, source_target_pairs={{0,1},{1,0},{2,3},{3,2},{4,5},{5,4},{6,7},{7,6},{8,9},{9,8},{10,11... | collective-permute-start | bytes 49160 | tf_op jit(solution)/shard_map/ppermute | solution.py:453
  118.5 0.8 collective-permute-done.7
  119.4 0.6 fusion.8
  (19 shorter events, 1.9 us)
Async XLA Ops:
  9.6 55.8 %all-to-all-start = ((bf16[64,104,128]{2,1,0:T(8,128)(2,1)}), bf16[64,104,128]{2,1,0:T(8,128)(2,1)S(1)}, u32[]{:S(2)}, u32[]{:S(2)}) async-start(bf16[64,104,128]{2,1,0:T(8,128)(2,1)} %get-tuple-element.29), calls=%async_computation | async-start | bytes 3407872 | tf_op jit(solution)/shard_map/all_to_all | solution.py:394
  71.5 4.4 %collective-permute-start = (bf16[2,1024,512]{2,1,0:T(8,128)(2,1)S(1)}, bf16[2,1024,512]{2,1,0:T(8,128)(2,1)S(1)}, u32[]{:S(2)}, u32[]{:S(2)}) collective-permute-start(bf16[2,1024,512]{2,1,0:T(8,128)(2,1)S(1)} %get-tuple-element.39), channel_id=1, source_target_pairs={{0,1},{1,0},{2,3},{3,2},{4,5},{5,4},{6,7},{7,6},{8,9},{9,8},{10,11... | collective-permute-start | bytes 6291464 | tf_op jit(solution)/shard_map/ppermute | solution.py:434
  76.5 0.8 copy-start
  77.3 12.3 %collective-permute-start.1 = (bf16[2,256,512]{2,1,0:T(8,128)(2,1)S(1)}, bf16[2,256,512]{2,1,0:T(8,128)(2,1)S(1)}, u32[]{:S(2)}, u32[]{:S(2)}) collective-permute-start(bf16[2,256,512]{2,1,0:T(8,128)(2,1)S(1)} %get-tuple-element.41), channel_id=1, source_target_pairs={{0,128},{1,33},{16,144},{17,49},{32,160},{33,1},{48,176},{49,17},{... | collective-permute-start | bytes 1572872 | tf_op jit(solution)/shard_map/ppermute | solution.py:363
  80.1 12.6 %collective-permute-start.2 = (bf16[2,256,512]{2,1,0:T(8,128)(2,1)S(1)}, bf16[2,256,512]{2,1,0:T(8,128)(2,1)S(1)}, u32[]{:S(2)}, u32[]{:S(2)}) collective-permute-start(bf16[2,256,512]{2,1,0:T(8,128)(2,1)S(1)} %get-tuple-element.42), channel_id=1, source_target_pairs={{0,64},{1,17},{16,80},{17,33},{32,96},{33,49},{48,112},{49,1},{64,... | collective-permute-start | bytes 1572872 | tf_op jit(solution)/shard_map/ppermute | solution.py:363
  80.5 12.8 %collective-permute-start.3 = (bf16[2,256,512]{2,1,0:T(8,128)(2,1)S(1)}, bf16[2,256,512]{2,1,0:T(8,128)(2,1)S(1)}, u32[]{:S(2)}, u32[]{:S(2)}) collective-permute-start(bf16[2,256,512]{2,1,0:T(8,128)(2,1)S(1)} %get-tuple-element.43), channel_id=1, source_target_pairs={{0,192},{1,49},{16,208},{17,1},{32,224},{33,17},{48,240},{49,33},{... | collective-permute-start | bytes 1572872 | tf_op jit(solution)/shard_map/ppermute | solution.py:363
  82.8 22.3 %all-to-all-start.2 = ((bf16[64,16,128]{2,1,0:T(8,128)(2,1)}), bf16[64,16,128]{2,1,0:T(8,128)(2,1)S(1)}, u32[]{:S(2)}, u32[]{:S(2)}) async-start(bf16[64,16,128]{2,1,0:T(8,128)(2,1)} %alpha.1), calls=%async_computation.2 | async-start | bytes 524288 | tf_op jit(solution)/shard_map/all_to_all | solution.py:438
  94.6 7.5 %collective-permute-start.4 = (bf16[2,64,512]{2,1,0:T(8,128)(2,1)S(1)}, bf16[2,64,512]{2,1,0:T(8,128)(2,1)S(1)}, u32[]{:S(2)}, u32[]{:S(2)}) collective-permute-start(bf16[2,64,512]{2,1,0:T(8,128)(2,1)S(1)} %get-tuple-element.45), channel_id=1, source_target_pairs={{0,32},{1,129},{16,48},{17,145},{32,0},{33,161},{48,16},{49,177},{... | collective-permute-start | bytes 393224 | tf_op jit(solution)/shard_map/ppermute | solution.py:363
  99.3 5.0 %collective-permute-start.5 = (bf16[2,64,512]{2,1,0:T(8,128)(2,1)S(1)}, bf16[2,64,512]{2,1,0:T(8,128)(2,1)S(1)}, u32[]{:S(2)}, u32[]{:S(2)}) collective-permute-start(bf16[2,64,512]{2,1,0:T(8,128)(2,1)S(1)} %get-tuple-element.46), channel_id=1, source_target_pairs={{0,16},{1,65},{16,32},{17,81},{32,48},{33,97},{48,0},{49,113},{64,... | collective-permute-start | bytes 393224 | tf_op jit(solution)/shard_map/ppermute | solution.py:363
  99.3 5.0 %collective-permute-start.6 = (bf16[2,64,512]{2,1,0:T(8,128)(2,1)S(1)}, bf16[2,64,512]{2,1,0:T(8,128)(2,1)S(1)}, u32[]{:S(2)}, u32[]{:S(2)}) collective-permute-start(bf16[2,64,512]{2,1,0:T(8,128)(2,1)S(1)} %get-tuple-element.47), channel_id=1, source_target_pairs={{0,48},{1,193},{16,0},{17,209},{32,16},{33,225},{48,32},{49,241},{... | collective-permute-start | bytes 393224 | tf_op jit(solution)/shard_map/ppermute | solution.py:363
  105.1 11.7 %all-to-all-start.1 = ((bf16[8,16,512]{2,1,0:T(8,128)(2,1)}), bf16[8,16,512]{2,1,0:T(8,128)(2,1)S(1)}, u32[]{:S(2)}, u32[]{:S(2)}) async-start(bf16[8,16,512]{2,1,0:T(8,128)(2,1)} %line.1), calls=%async_computation.1 | async-start | bytes 262144 | tf_op jit(solution)/shard_map/all_to_all | solution.py:447
  108.5 10.9 %copy-start.1 = (f32[8,1024]{1,0:T(8,128)S(1)}, f32[8,1024]{1,0:T(8,128)}, u32[]{:S(2)}) copy-start(f32[8,1024]{1,0:T(8,128)} %get-tuple-element.51) | copy-start | bytes 98308
  108.5 10.9 %copy-start.2 = (f32[8,1024]{1,0:T(8,128)S(1)}, f32[8,1024]{1,0:T(8,128)}, u32[]{:S(2)}) copy-start(f32[8,1024]{1,0:T(8,128)} %get-tuple-element.52) | copy-start | bytes 98308
  116.8 2.6 %collective-permute-start.7 = (f32[2,4,512]{2,1,0:T(4,128)S(1)}, f32[2,4,512]{2,1,0:T(4,128)S(1)}, u32[]{:S(2)}, u32[]{:S(2)}) collective-permute-start(f32[2,4,512]{2,1,0:T(4,128)S(1)} %select_bitcast_fusion), channel_id=1, source_target_pairs={{0,1},{1,0},{2,3},{3,2},{4,5},{5,4},{6,7},{7,6},{8,9},{9,8},{10,11... | collective-permute-start | bytes 49160 | tf_op jit(solution)/shard_map/ppermute | solution.py:453

commit v6 on v5

--- a/solution.py
+++ b/solution.py
@@ -329,8 +329,8 @@
     ins, out_ref = refs[:4], refs[4]
     for term in range(2):
         total = sum(r[term].astype(F32) for r in ins)
-        for z in range(8):
-            out_ref[z, term * 8 : (term + 1) * 8, :] = total[z * 8 : (z + 1) * 8, :].astype(BF16)
+        for n in range(16):
+            out_ref[n, term * 4 : (term + 1) * 4, :] = total[n * 4 : (n + 1) * 4, :].astype(BF16)
 
 
 def final_kernel(wire_ref, out_ref):
@@ -442,17 +442,13 @@
         specs=dict(in_specs=[hbm] + [vmem] * 3),
     )(*in_hbm(own), far, right, left)
     far, right, left = (ring(pieces[d - 1], d, True) for d in (2, 1, 3))
-    (part,) = call(line_kernel, "line", [((8, 16, half), BF16)])(own, far, right, left)
+    (part,) = call(line_kernel, "line", [((16, 8, half), BF16)])(own, far, right, left)
     (alpha_final,) = call(final_kernel, "final", [((ROWS, WIDTH), BF16)])(a_got)
-    part = lax.all_to_all(part, "z", 0, 0, tiled=True)
+    part = lax.all_to_all(part, ("z", "core"), 0, 0, tiled=True)
     loglik = jnp.log(total[0, 2 : 3 * SEQ_DEV : 3] / (WIDTH * WIDTH))
     part, alpha_final, loglik = lax.optimization_barrier((part, alpha_final, loglik))
-    part = jnp.sum(part.astype(F32), axis=0)
-    part = part.reshape(2, 2, 4, half)
-    mine = jnp.where(core == 0, part[:, 0], part[:, 1])
-    other = lax.ppermute(jnp.where(core == 0, part[:, 1], part[:, 0]), "core", swap_cores)
-    left, right = jnp.where(core == 0, mine, other), jnp.where(core == 0, other, mine)
-    sums = jnp.concatenate([left, right], axis=2)
+    sums = jnp.sum(part.reshape(8, 2, 2, 4, half).astype(F32), axis=0)
+    sums = jnp.concatenate([sums[0], sums[1]], axis=2)
     scale = 1.0 / (SEQ_DEV * 4 * STEPS)
     counts_rows = sums[0] * take_rows[:4] * scale
     counts_cols = sums[1] * take_cols[:4] * scale

time: 120 us -> 119 us (level)
  starting transfers between devices: 38.4 us -> 37 us
    ppermute x1 -> x0, starting transfers between devices: 1.74 us -> none  [on_device(): lax.ppermute(jnp.where(core == 0, part[:, 1], part[:, 0]), 'core', swap_c...]
  transfers between devices with their start and end apart: 11 -> 10, of which waited for: 7 -> 6; matrix products, arithmetic and copies ran while one was open for 1% -> 1% of each run, Pallas kernels for 11% -> 12%
where the time goes in v6:
time: 119 us
  waiting for transfers between devices  49.4 us (42%)
  starting transfers between devices  37 us (31%)
  Pallas kernels  29.5 us (25%)
  other arithmetic  1.19 us (1%)
    all_to_all x1, waiting for transfers between devices, on_device(): got = lax.all_to_all(wire, state, 0, 0, tiled=True)  35.4 us
    all_to_all x1, starting transfers between devices, on_device(): got = lax.all_to_all(wire, state, 0, 0, tiled=True)  13.2 us
    ppermute x6, starting transfers between devices, ring(): return lax.ppermute(x, ('dp', 'y', 'core'), pairs)  12.9 us
    pallas_call x1, Pallas kernels, on_device(): call(send_kernel, 'send', [(wire_shape, BF16), (y_shape, BF16)], [((ROWS,...  8.97 us
    all_to_all x1, waiting for transfers between devices, on_device(): part = lax.all_to_all(part, ('z', 'core'), 0, 0, tiled=True)  7.32 us
    pallas_call x1, Pallas kernels, on_device(): call(local_kernel, 'local', [((WIDTH, STEPS * ROWS), BF16), (square, BF16...  7.25 us
    all_to_all x1, starting transfers between devices, on_device(): a_got = lax.all_to_all(a_wire, state, 0, 0, tiled=True)  6.82 us
    pallas_call x1, Pallas kernels, on_device(): call(counts_kernel, 'counts', [((WIDTH, ROWS), BF16), ((2, WIDTH, half),...  6.17 us
  transfers between devices with their start and end apart: 10, of which 6 were waited for; matrix products, arithmetic and copies ran while one was open for 1% of the time, Pallas kernels for 12%

profile of v6, /device:TPU:1, one launch (start us, length us, event | category | flops | bytes accessed | tf_op | source)
XLA Modules:
  0.0 118.8 jit_solution(11415098870987853980)
XLA Ops:
  0.6 9.0 %send.1 = (bf16[64,104,128]{2,1,0:T(8,128)(2,1)}, bf16[2,128,1024]{2,1,0:T(8,128)(2,1)}) custom-call(s32[3,8]{1,0:T(4,128)} %bitcast.36, bf16[128,1024]{1,0:T(8,128)(2,1)} %bitcast.34, bf16[1024,1024]{1,0:T(8,128)(2,1)} %rows_ref.1, bf16[1024,1024]{1,0:T(8,128)(2,1)} %cols_ref.1, bf16[512,1024]{1,0:T(8,128)(2,1)} %emit_rows_ref.1, ...), custom_call_target="tpu_custom_call" | custom-call | flops 1000000000 | bytes 8000000 | tf_op jit(solution)/shard_map/send/pallas_call | solution.py:380
  9.6 13.2 %all-to-all-start = ((bf16[64,104,128]{2,1,0:T(8,128)(2,1)}), bf16[64,104,128]{2,1,0:T(8,128)(2,1)S(1)}, u32[]{:S(2)}, u32[]{:S(2)}) async-start(bf16[64,104,128]{2,1,0:T(8,128)(2,1)} %get-tuple-element.29), calls=%async_computation | async-start | bytes 3407872 | tf_op jit(solution)/shard_map/all_to_all | solution.py:394
  22.8 7.2 %local.1 = (bf16[1024,384]{1,0:T(8,128)(2,1)}, bf16[1024,1024]{1,0:T(8,128)(2,1)}, bf16[3,1024,128]{2,1,0:T(8,128)(2,1)}, f32[1,128]{1,0:T(1,128)}, f32[8,1024]{1,0:T(8,128)}, /*index=5*/f32[8,1024]{1,0:T(8,128)}) custom-call(s32[3,8]{1,0:T(4,128)} %bitcast.37, bf16[1024,1024]{1,0:T(8,128)(2,1)} %rows_ref.1, bf16[1024,1024]{1,0:T(8,128)(2,1)} %cols_ref.1, ...), custom_call_target="tpu_custom_call" | custom-call | flops 1000000000 | bytes 8000000 | tf_op jit(solution)/shard_map/local/pallas_call | solution.py:396
  30.0 35.4 %all-to-all-done.wire_ref = bf16[64,104,128]{2,1,0:T(8,128)(2,1)S(1)} async-done(((bf16[64,104,128]{2,1,0:T(8,128)(2,1)}), bf16[64,104,128]{2,1,0:T(8,128)(2,1)S(1)}, u32[]{:S(2)}, u32[]{:S(2)}) %all-to-all-start) | async-done | bytes 1703968 | tf_op jit(solution)/shard_map/all_to_all | solution.py:394
  65.4 6.2 %counts.1 = (bf16[1024,128]{1,0:T(8,128)(2,1)S(1)}, bf16[2,1024,512]{2,1,0:T(8,128)(2,1)S(1)}, bf16[2,1024,512]{2,1,0:T(8,128)(2,1)S(1)}, f32[1,128]{1,0:T(1,128)S(1)}) custom-call(bf16[64,104,128]{2,1,0:T(8,128)(2,1)S(1)} %all-to-all-done.wire_ref, bf16[2,128,1024]{2,1,0:T(8,128)(2,1)} %get-tuple-element.30.y_hbm, bf16[128,1024]{1,0:T(8,128)(2,1)} %bitcast.35, ...), custom_call_target="tpu_custom_call" | custom-call | flops 1000000000 | bytes 8000000 | tf_op jit(solution)/shard_map/counts/pallas_call | solution.py:407
  71.9 3.3 %alpha.1 = bf16[64,16,128]{2,1,0:T(8,128)(2,1)} custom-call(bf16[1024,128]{1,0:T(8,128)(2,1)S(1)} %get-tuple-element.35.after_ref, bf16[1024,1024]{1,0:T(8,128)(2,1)} %get-tuple-element.31.turned_hbm.turned_ref, bf16[3,1024,128]{2,1,0:T(8,128)(2,1)} %get-tuple-element.32.factor_hbm.factor_ref, f32[1,128]{1,0:T(1,128)} %get-tuple-element.36.local_ref, ...), custom_call_target="tpu_custom_call" | custom-call | flops 1000000000 | bytes 8000000 | tf_op jit(solution)/shard_map/alpha/pallas_call | solution.py:422
  75.2 0.8 collective-permute-done.got_ref
  76.0 0.5 pair.1
  76.5 0.8 copy-done
  77.3 2.8 %collective-permute-start.1 = (bf16[2,256,512]{2,1,0:T(8,128)(2,1)S(1)}, bf16[2,256,512]{2,1,0:T(8,128)(2,1)S(1)}, u32[]{:S(2)}, u32[]{:S(2)}) collective-permute-start(bf16[2,256,512]{2,1,0:T(8,128)(2,1)S(1)} %get-tuple-element.41), channel_id=1, source_target_pairs={{0,128},{1,33},{16,144},{17,49},{32,160},{33,1},{48,176},{49,17},{... | collective-permute-start | bytes 1572872 | tf_op jit(solution)/shard_map/ppermute | solution.py:363
  80.6 2.3 %collective-permute-start.3 = (bf16[2,256,512]{2,1,0:T(8,128)(2,1)S(1)}, bf16[2,256,512]{2,1,0:T(8,128)(2,1)S(1)}, u32[]{:S(2)}, u32[]{:S(2)}) collective-permute-start(bf16[2,256,512]{2,1,0:T(8,128)(2,1)S(1)} %get-tuple-element.43), channel_id=1, source_target_pairs={{0,192},{1,49},{16,208},{17,1},{32,224},{33,17},{48,240},{49,33},{... | collective-permute-start | bytes 1572872 | tf_op jit(solution)/shard_map/ppermute | solution.py:363
  82.8 6.8 %all-to-all-start.2 = ((bf16[64,16,128]{2,1,0:T(8,128)(2,1)}), bf16[64,16,128]{2,1,0:T(8,128)(2,1)S(1)}, u32[]{:S(2)}, u32[]{:S(2)}) async-start(bf16[64,16,128]{2,1,0:T(8,128)(2,1)} %alpha.1), calls=%async_computation.2 | async-start | bytes 524288 | tf_op jit(solution)/shard_map/all_to_all | solution.py:438
  89.7 3.1 %collective-permute-done.2.refs_1_ = bf16[2,256,512]{2,1,0:T(8,128)(2,1)S(1)} collective-permute-done((bf16[2,256,512]{2,1,0:T(8,128)(2,1)S(1)}, bf16[2,256,512]{2,1,0:T(8,128)(2,1)S(1)}, u32[]{:S(2)}, u32[]{:S(2)}) %collective-permute-start.2) | collective-permute-done | bytes 524320 | tf_op jit(solution)/shard_map/ppermute | solution.py:363
  92.8 0.6 collective-permute-done.3.refs_2_
  93.3 1.3 %plane.1 = (bf16[2,64,512]{2,1,0:T(8,128)(2,1)S(1)}, bf16[2,64,512]{2,1,0:T(8,128)(2,1)S(1)}, bf16[2,64,512]{2,1,0:T(8,128)(2,1)S(1)}, bf16[2,64,512]{2,1,0:T(8,128)(2,1)S(1)}) custom-call(bf16[2,256,512]{2,1,0:T(8,128)(2,1)} %copy-done, bf16[2,256,512]{2,1,0:T(8,128)(2,1)S(1)} %collective-permute-done.1.refs_0_, ...), custom_call_target="tpu_custom_call" | custom-call | flops 1000000000 | bytes 8000000 | tf_op jit(solution)/shard_map/plane/pallas_call | solution.py:439
  94.6 4.7 %collective-permute-start.4 = (bf16[2,64,512]{2,1,0:T(8,128)(2,1)S(1)}, bf16[2,64,512]{2,1,0:T(8,128)(2,1)S(1)}, u32[]{:S(2)}, u32[]{:S(2)}) collective-permute-start(bf16[2,64,512]{2,1,0:T(8,128)(2,1)S(1)} %get-tuple-element.45), channel_id=1, source_target_pairs={{0,32},{1,129},{16,48},{17,145},{32,0},{33,161},{48,16},{49,177},{... | collective-permute-start | bytes 393224 | tf_op jit(solution)/shard_map/ppermute | solution.py:363
  99.4 2.7 %collective-permute-start.6 = (bf16[2,64,512]{2,1,0:T(8,128)(2,1)S(1)}, bf16[2,64,512]{2,1,0:T(8,128)(2,1)S(1)}, u32[]{:S(2)}, u32[]{:S(2)}) collective-permute-start(bf16[2,64,512]{2,1,0:T(8,128)(2,1)S(1)} %get-tuple-element.47), channel_id=1, source_target_pairs={{0,48},{1,193},{16,0},{17,209},{32,16},{33,225},{48,32},{49,241},{... | collective-permute-start | bytes 393224 | tf_op jit(solution)/shard_map/ppermute | solution.py:363
  102.1 2.3 %collective-permute-done.5.refs_2_ = bf16[2,64,512]{2,1,0:T(8,128)(2,1)S(1)} collective-permute-done((bf16[2,64,512]{2,1,0:T(8,128)(2,1)S(1)}, bf16[2,64,512]{2,1,0:T(8,128)(2,1)S(1)}, u32[]{:S(2)}, u32[]{:S(2)}) %collective-permute-start.5) | collective-permute-done | bytes 131104 | tf_op jit(solution)/shard_map/ppermute | solution.py:363
  104.4 0.7 line.1
  105.1 3.7 %all-to-all-start.1 = ((bf16[16,8,512]{2,1,0:T(8,128)(2,1)}), bf16[16,8,512]{2,1,0:T(8,128)(2,1)S(1)}, u32[]{:S(2)}, u32[]{:S(2)}) async-start(bf16[16,8,512]{2,1,0:T(8,128)(2,1)} %line.1), calls=%async_computation.1 | async-start | bytes 262144 | tf_op jit(solution)/shard_map/all_to_all | solution.py:447
  108.8 0.5 log_bitcast_fusion
  109.3 1.3 %final.1 = bf16[128,1024]{1,0:T(8,128)(2,1)} custom-call(bf16[64,16,128]{2,1,0:T(8,128)(2,1)S(1)} %all-to-all-done.2.wire_ref), custom_call_target="tpu_custom_call" | custom-call | flops 1000000000 | bytes 8000000 | tf_op jit(solution)/shard_map/final/pallas_call | solution.py:446
  110.7 7.3 %all-to-all-done.1 = bf16[16,8,512]{2,1,0:T(8,128)(2,1)S(1)} async-done(((bf16[16,8,512]{2,1,0:T(8,128)(2,1)}), bf16[16,8,512]{2,1,0:T(8,128)(2,1)S(1)}, u32[]{:S(2)}, u32[]{:S(2)}) %all-to-all-start.1) | async-done | bytes 131104 | tf_op jit(solution)/shard_map/all_to_all | solution.py:447
  118.2 0.6 fusion.8
  (16 shorter events, 1.0 us)
Async XLA Ops:
  9.6 55.8 %all-to-all-start = ((bf16[64,104,128]{2,1,0:T(8,128)(2,1)}), bf16[64,104,128]{2,1,0:T(8,128)(2,1)S(1)}, u32[]{:S(2)}, u32[]{:S(2)}) async-start(bf16[64,104,128]{2,1,0:T(8,128)(2,1)} %get-tuple-element.29), calls=%async_computation | async-start | bytes 3407872 | tf_op jit(solution)/shard_map/all_to_all | solution.py:394
  71.6 4.4 %collective-permute-start = (bf16[2,1024,512]{2,1,0:T(8,128)(2,1)S(1)}, bf16[2,1024,512]{2,1,0:T(8,128)(2,1)S(1)}, u32[]{:S(2)}, u32[]{:S(2)}) collective-permute-start(bf16[2,1024,512]{2,1,0:T(8,128)(2,1)S(1)} %get-tuple-element.39), channel_id=1, source_target_pairs={{0,1},{1,0},{2,3},{3,2},{4,5},{5,4},{6,7},{7,6},{8,9},{9,8},{10,11... | collective-permute-start | bytes 6291464 | tf_op jit(solution)/shard_map/ppermute | solution.py:434
  76.5 0.8 copy-start
  77.3 12.3 %collective-permute-start.1 = (bf16[2,256,512]{2,1,0:T(8,128)(2,1)S(1)}, bf16[2,256,512]{2,1,0:T(8,128)(2,1)S(1)}, u32[]{:S(2)}, u32[]{:S(2)}) collective-permute-start(bf16[2,256,512]{2,1,0:T(8,128)(2,1)S(1)} %get-tuple-element.41), channel_id=1, source_target_pairs={{0,128},{1,33},{16,144},{17,49},{32,160},{33,1},{48,176},{49,17},{... | collective-permute-start | bytes 1572872 | tf_op jit(solution)/shard_map/ppermute | solution.py:363
  80.2 12.6 %collective-permute-start.2 = (bf16[2,256,512]{2,1,0:T(8,128)(2,1)S(1)}, bf16[2,256,512]{2,1,0:T(8,128)(2,1)S(1)}, u32[]{:S(2)}, u32[]{:S(2)}) collective-permute-start(bf16[2,256,512]{2,1,0:T(8,128)(2,1)S(1)} %get-tuple-element.42), channel_id=1, source_target_pairs={{0,64},{1,17},{16,80},{17,33},{32,96},{33,49},{48,112},{49,1},{64,... | collective-permute-start | bytes 1572872 | tf_op jit(solution)/shard_map/ppermute | solution.py:363
  80.6 12.8 %collective-permute-start.3 = (bf16[2,256,512]{2,1,0:T(8,128)(2,1)S(1)}, bf16[2,256,512]{2,1,0:T(8,128)(2,1)S(1)}, u32[]{:S(2)}, u32[]{:S(2)}) collective-permute-start(bf16[2,256,512]{2,1,0:T(8,128)(2,1)S(1)} %get-tuple-element.43), channel_id=1, source_target_pairs={{0,192},{1,49},{16,208},{17,1},{32,224},{33,17},{48,240},{49,33},{... | collective-permute-start | bytes 1572872 | tf_op jit(solution)/shard_map/ppermute | solution.py:363
  82.8 22.3 %all-to-all-start.2 = ((bf16[64,16,128]{2,1,0:T(8,128)(2,1)}), bf16[64,16,128]{2,1,0:T(8,128)(2,1)S(1)}, u32[]{:S(2)}, u32[]{:S(2)}) async-start(bf16[64,16,128]{2,1,0:T(8,128)(2,1)} %alpha.1), calls=%async_computation.2 | async-start | bytes 524288 | tf_op jit(solution)/shard_map/all_to_all | solution.py:438
  94.6 7.5 %collective-permute-start.4 = (bf16[2,64,512]{2,1,0:T(8,128)(2,1)S(1)}, bf16[2,64,512]{2,1,0:T(8,128)(2,1)S(1)}, u32[]{:S(2)}, u32[]{:S(2)}) collective-permute-start(bf16[2,64,512]{2,1,0:T(8,128)(2,1)S(1)} %get-tuple-element.45), channel_id=1, source_target_pairs={{0,32},{1,129},{16,48},{17,145},{32,0},{33,161},{48,16},{49,177},{... | collective-permute-start | bytes 393224 | tf_op jit(solution)/shard_map/ppermute | solution.py:363
  99.4 5.0 %collective-permute-start.5 = (bf16[2,64,512]{2,1,0:T(8,128)(2,1)S(1)}, bf16[2,64,512]{2,1,0:T(8,128)(2,1)S(1)}, u32[]{:S(2)}, u32[]{:S(2)}) collective-permute-start(bf16[2,64,512]{2,1,0:T(8,128)(2,1)S(1)} %get-tuple-element.46), channel_id=1, source_target_pairs={{0,16},{1,65},{16,32},{17,81},{32,48},{33,97},{48,0},{49,113},{64,... | collective-permute-start | bytes 393224 | tf_op jit(solution)/shard_map/ppermute | solution.py:363
  99.4 5.0 %collective-permute-start.6 = (bf16[2,64,512]{2,1,0:T(8,128)(2,1)S(1)}, bf16[2,64,512]{2,1,0:T(8,128)(2,1)S(1)}, u32[]{:S(2)}, u32[]{:S(2)}) collective-permute-start(bf16[2,64,512]{2,1,0:T(8,128)(2,1)S(1)} %get-tuple-element.47), channel_id=1, source_target_pairs={{0,48},{1,193},{16,0},{17,209},{32,16},{33,225},{48,32},{49,241},{... | collective-permute-start | bytes 393224 | tf_op jit(solution)/shard_map/ppermute | solution.py:363
  105.1 12.9 %all-to-all-start.1 = ((bf16[16,8,512]{2,1,0:T(8,128)(2,1)}), bf16[16,8,512]{2,1,0:T(8,128)(2,1)S(1)}, u32[]{:S(2)}, u32[]{:S(2)}) async-start(bf16[16,8,512]{2,1,0:T(8,128)(2,1)} %line.1), calls=%async_computation.1 | async-start | bytes 262144 | tf_op jit(solution)/shard_map/all_to_all | solution.py:447
  109.3 8.8 %copy-start.1 = (f32[8,1024]{1,0:T(8,128)S(1)}, f32[8,1024]{1,0:T(8,128)}, u32[]{:S(2)}) copy-start(f32[8,1024]{1,0:T(8,128)} %get-tuple-element.51) | copy-start | bytes 98308
  109.3 8.8 %copy-start.2 = (f32[8,1024]{1,0:T(8,128)S(1)}, f32[8,1024]{1,0:T(8,128)}, u32[]{:S(2)}) copy-start(f32[8,1024]{1,0:T(8,128)} %get-tuple-element.52) | copy-start | bytes 98308
